TPU v7x, 32 devices: a whole 2x2x4 slice. The times are simulated.
32 devices in a mesh: dp: 4 (over x, core), tensor: 8 (over z, y).
Axes of the slice: x: 2, y: 2, z: 4, core: 2. Of those that a mesh axis runs over, the one named last changes fastest.
Arguments:
- tokens: bfloat16 [8192, 1024], P('dp'), may hold values from -6 to 6
- segment_ids: int32 [4, 2048], P('dp'), may hold values from 0 to 7, never falling along the last dimension, each value on 1 to 512 neighbouring positions
- first_gain: bfloat16 [1024], replicated, may hold values from 0.5 to 1.5
- first_shift: bfloat16 [1024], replicated, may hold values from -3 to 3
- qkv_weight: bfloat16 [1024, 16, 192], P(None, 'tensor'), may hold values from -0.1875 to 0.1875
- qv_bias: bfloat16 [16, 128], P('tensor'), may hold values from -3 to 3
- out_weight: bfloat16 [1024, 1024], P('tensor'), may hold values from -0.5 to 0.5
- out_bias: bfloat16 [1024], replicated, may hold values from -2 to 2
- second_gain: bfloat16 [1024], replicated, may hold values from 0.5 to 1.5
- second_shift: bfloat16 [1024], replicated, may hold values from -3 to 3
- up_weight: bfloat16 [1024, 4096], P(None, 'tensor'), may hold values from -0.1875 to 0.1875
- up_bias: bfloat16 [4096], P('tensor'), may hold values from -3 to 3
- down_weight: bfloat16 [4096, 1024], P('tensor'), may hold values from -0.125 to 0.125
- down_bias: bfloat16 [1024], replicated, may hold values from -2 to 2
- cotangent: bfloat16 [8192, 1024], P('dp'), may hold values from -6 to 6
Outputs:
- output: bfloat16 [8192, 1024], P('dp')
- grad_tokens: bfloat16 [8192, 1024], P('dp')
- grad_first_gain: float32 [1024], replicated
- grad_first_shift: float32 [1024], replicated
- grad_qkv_weight: float32 [1024, 16, 192], P(None, 'tensor')
- grad_qv_bias: float32 [16, 128], P('tensor')
- grad_out_weight: float32 [1024, 1024], P('tensor')
- grad_out_bias: float32 [1024], replicated
- grad_second_gain: float32 [1024], replicated
- grad_second_shift: float32 [1024], replicated
- grad_up_weight: float32 [1024, 4096], P(None, 'tensor')
- grad_up_bias: float32 [4096], P('tensor')
- grad_down_weight: float32 [4096, 1024], P('tensor')
- grad_down_bias: float32 [1024], replicated
Inputs may be any that keep to these rules, and one draw needn't show every extreme that they name: `segment_ids`: each row of 2048 positions is cut into documents of consecutive positions, at most 512 long, one exactly that long; ids never fall along a row.
All inputs are finite; a program needn't handle non-finite values.
Results may differ from a plain program's by a relative error of at most 0.023.
Values may be sent and summed in bfloat16 or wider, within the bound.
A program may use at most 128 MiB of HBM per device.

v0:
```python
import math

import jax
import jax.numpy as jnp
from jax import lax
from jax.sharding import PartitionSpec as P

norm_eps = 1e-05


def layer_norm(values, gain_vec, shift_vec):
    center = jnp.mean(values, axis=-1, keepdims=True)
    offset = values - center
    spread = jnp.mean(offset * offset, axis=-1, keepdims=True)
    return offset * lax.rsqrt(spread + norm_eps) * gain_vec + shift_vec


def gelu_tanh(values):
    return (
        0.5
        * values
        * (1.0 + jnp.tanh(0.7978845608028654 * (values + 0.044715 * values * values * values)))
    )


def head_slopes(local_heads):
    total = local_heads * lax.axis_size("tensor")
    first = lax.axis_index("tensor") * local_heads
    heads_idx = first + jnp.arange(local_heads, dtype=jnp.int32)
    return jnp.exp2(-8.0 * (heads_idx + 1).astype(jnp.float32) / total)


def block_scores(query_blk, keys, start, seg_row, slopes):
    rows = query_blk.shape[0]
    length = keys.shape[0]
    scale = 1.0 / math.sqrt(keys.shape[2])
    raw = jnp.einsum("qhe,khe->hqk", query_blk, keys, preferred_element_type=jnp.float32) * scale
    query_pos = start + jnp.arange(rows, dtype=jnp.int32)
    key_pos = jnp.arange(length, dtype=jnp.int32)
    distance = (query_pos[:, None] - key_pos[None, :]).astype(jnp.float32)
    raw = raw - slopes[:, None, None] * distance[None]
    query_seg = lax.dynamic_slice_in_dim(seg_row, start, rows, 0)
    allowed = (query_seg[:, None] == seg_row[None, :]) & (key_pos[None, :] <= query_pos[:, None])
    return jnp.where(allowed[None], raw, -1e30)


def attend_forward(query, keys, values, seg_row, slopes):
    length = query.shape[0]
    block = min(512, length)

    def one_block(index):
        start = index * block
        query_blk = lax.dynamic_slice_in_dim(query, start, block, 0)
        scores = block_scores(query_blk, keys, start, seg_row, slopes)
        peak = jnp.max(scores, axis=-1, keepdims=True)
        expo = jnp.exp(scores - peak)
        total = jnp.sum(expo, axis=-1, keepdims=True)
        weights_low = (expo / total).astype(jnp.bfloat16)
        ctx_blk = jnp.einsum(
            "hqk,khe->qhe", weights_low, values, preferred_element_type=jnp.float32
        )
        return (ctx_blk, (peak + jnp.log(total))[:, :, 0])

    ctx_blocks, lse_blocks = lax.map(one_block, jnp.arange(length // block, dtype=jnp.int32))
    return (ctx_blocks.reshape(query.shape), lse_blocks)


def attend_backward(query, keys, values, seg_row, slopes, lse_blocks, grad_context):
    length = query.shape[0]
    block = min(512, length)
    scale = 1.0 / math.sqrt(keys.shape[2])

    def one_block(carry, index):
        grad_keys, grad_values = carry
        start = index * block
        query_blk = lax.dynamic_slice_in_dim(query, start, block, 0)
        grad_blk = lax.dynamic_slice_in_dim(grad_context, start, block, 0)
        scores = block_scores(query_blk, keys, start, seg_row, slopes)
        probs = jnp.exp(scores - lse_blocks[index][:, :, None])
        probs_low = probs.astype(jnp.bfloat16)
        grad_probs = jnp.einsum(
            "qhe,khe->hqk", grad_blk, values, preferred_element_type=jnp.float32
        )
        inner = jnp.sum(probs * grad_probs, axis=-1, keepdims=True)
        grad_scores = (probs * (grad_probs - inner)).astype(jnp.bfloat16)
        grad_query = (
            jnp.einsum("hqk,khe->qhe", grad_scores, keys, preferred_element_type=jnp.float32)
            * scale
        )
        grad_keys = (
            grad_keys
            + jnp.einsum("hqk,qhe->khe", grad_scores, query_blk, preferred_element_type=jnp.float32)
            * scale
        )
        grad_values = grad_values + jnp.einsum(
            "hqk,qhe->khe", probs_low, grad_blk, preferred_element_type=jnp.float32
        )
        return ((grad_keys, grad_values), grad_query)

    empty = jnp.zeros(keys.shape, jnp.float32)
    (grad_keys, grad_values), grad_query = lax.scan(
        one_block, (empty, empty), jnp.arange(length // block, dtype=jnp.int32)
    )
    return (grad_query.reshape(query.shape), grad_keys, grad_values)


def attn_front(
    tokens_f, seg_row, first_gain, first_shift, qkv_weight, qv_bias, out_weight, out_bias, again
):
    length = tokens_f.shape[0]
    normed_low = layer_norm(
        tokens_f, first_gain.astype(jnp.float32), first_shift.astype(jnp.float32)
    ).astype(jnp.bfloat16)
    merged = jnp.einsum("td,dhe->the", normed_low, qkv_weight, preferred_element_type=jnp.float32)
    width = merged.shape[2] // 3
    bias_f = qv_bias.astype(jnp.float32)
    query = (merged[:, :, :width] + bias_f[:, :width]).astype(jnp.bfloat16)
    keys = merged[:, :, width : 2 * width].astype(jnp.bfloat16)
    values = (merged[:, :, 2 * width :] + bias_f[:, width:]).astype(jnp.bfloat16)
    slopes = head_slopes(query.shape[1])
    context, lse_blocks = attend_forward(query, keys, values, seg_row, slopes)
    context_low = context.reshape(length, -1).astype(jnp.bfloat16)
    partial_out = jnp.dot(context_low, out_weight, preferred_element_type=jnp.float32).astype(
        jnp.bfloat16
    )
    if again:
        mixed = lax.psum(partial_out, "tensor").astype(jnp.float32)
    else:
        mixed = lax.psum(partial_out, "tensor").astype(jnp.float32)
    middle = tokens_f + mixed + out_bias.astype(jnp.float32)
    return (normed_low, query, keys, values, context_low, lse_blocks, middle, slopes)


def mlp_front(middle, second_gain, second_shift, up_weight, up_bias):
    second_low = layer_norm(
        middle, second_gain.astype(jnp.float32), second_shift.astype(jnp.float32)
    ).astype(jnp.bfloat16)
    upper = jnp.dot(second_low, up_weight, preferred_element_type=jnp.float32) + up_bias.astype(
        jnp.float32
    )
    hidden_low = gelu_tanh(upper).astype(jnp.bfloat16)
    return (second_low, upper, hidden_low)


def norm_pull(values, gain_vec, shift_vec, grad_norm):
    norm_value, pull_fn = jax.vjp(
        layer_norm, values, gain_vec.astype(jnp.float32), shift_vec.astype(jnp.float32)
    )
    return pull_fn(grad_norm)


def per_device(
    tokens,
    segment_ids,
    first_gain,
    first_shift,
    qkv_weight,
    qv_bias,
    out_weight,
    out_bias,
    second_gain,
    second_shift,
    up_weight,
    up_bias,
    down_weight,
    down_bias,
    cotangent,
):
    tokens_f = tokens.astype(jnp.float32)
    seg_row = segment_ids[0]
    saved = attn_front(
        tokens_f, seg_row, first_gain, first_shift, qkv_weight, qv_bias, out_weight, out_bias, False
    )
    middle = saved[6]
    second_low, upper, hidden_low = mlp_front(middle, second_gain, second_shift, up_weight, up_bias)
    part_down = jnp.dot(hidden_low, down_weight, preferred_element_type=jnp.float32).astype(
        jnp.bfloat16
    )
    feed = lax.psum(part_down, "tensor").astype(jnp.float32)
    output = (middle + feed + down_bias.astype(jnp.float32)).astype(jnp.bfloat16)
    saved = attn_front(
        tokens_f, seg_row, first_gain, first_shift, qkv_weight, qv_bias, out_weight, out_bias, True
    )
    middle = saved[6]
    second_low, upper, hidden_low = mlp_front(middle, second_gain, second_shift, up_weight, up_bias)
    normed_low, query, keys, values, context_low, lse_blocks, middle, slopes = saved
    grad_out = cotangent.astype(jnp.float32)
    grad_down_weight = jnp.einsum(
        "tf,td->fd", hidden_low, cotangent, preferred_element_type=jnp.float32
    )
    grad_down_bias = jnp.sum(grad_out, axis=0)
    grad_hidden = jnp.einsum(
        "td,fd->tf", cotangent, down_weight, preferred_element_type=jnp.float32
    )
    gelu_value, gelu_pull = jax.vjp(gelu_tanh, upper)
    grad_upper_low = gelu_pull(grad_hidden)[0].astype(jnp.bfloat16)
    grad_up_bias = jnp.sum(grad_upper_low.astype(jnp.float32), axis=0)
    grad_up_weight = jnp.einsum(
        "td,tf->df", second_low, grad_upper_low, preferred_element_type=jnp.float32
    )
    part_second = jnp.einsum(
        "tf,df->td", grad_upper_low, up_weight, preferred_element_type=jnp.float32
    )
    grad_second = lax.psum(part_second.astype(jnp.bfloat16), "tensor").astype(jnp.float32)
    grad_middle_norm, grad_second_gain, grad_second_shift = norm_pull(
        middle, second_gain, second_shift, grad_second
    )
    grad_middle = grad_out + grad_middle_norm
    mlp_grads = (
        lax.psum(grad_down_weight.astype(jnp.bfloat16), "dp").astype(jnp.float32),
        lax.psum(grad_up_weight.astype(jnp.bfloat16), "dp").astype(jnp.float32),
        lax.psum(grad_up_bias.astype(jnp.bfloat16), "dp").astype(jnp.float32),
        lax.psum(grad_down_bias.astype(jnp.bfloat16), "dp").astype(jnp.float32),
        lax.psum(grad_second_gain.astype(jnp.bfloat16), "dp").astype(jnp.float32),
        lax.psum(grad_second_shift.astype(jnp.bfloat16), "dp").astype(jnp.float32),
    )
    grad_middle_low = grad_middle.astype(jnp.bfloat16)
    grad_out_bias = jnp.sum(grad_middle, axis=0)
    grad_out_weight = jnp.einsum(
        "tc,td->cd", context_low, grad_middle_low, preferred_element_type=jnp.float32
    )
    grad_context = jnp.einsum(
        "td,cd->tc", grad_middle_low, out_weight, preferred_element_type=jnp.float32
    )
    grad_context = grad_context.astype(jnp.bfloat16).reshape(query.shape)
    grad_query, grad_keys, grad_values = attend_backward(
        query, keys, values, seg_row, slopes, lse_blocks, grad_context
    )
    grad_query_low = grad_query.astype(jnp.bfloat16)
    grad_values_low = grad_values.astype(jnp.bfloat16)
    grad_merged = jnp.concatenate(
        [grad_query_low, grad_keys.astype(jnp.bfloat16), grad_values_low], axis=2
    )
    grad_qv_bias = jnp.concatenate(
        [
            jnp.sum(grad_query_low.astype(jnp.float32), axis=0),
            jnp.sum(grad_values_low.astype(jnp.float32), axis=0),
        ],
        axis=1,
    )
    grad_qkv_weight = jnp.einsum(
        "td,the->dhe", normed_low, grad_merged, preferred_element_type=jnp.float32
    )
    part_first = jnp.einsum(
        "the,dhe->td", grad_merged, qkv_weight, preferred_element_type=jnp.float32
    )
    grad_first = lax.psum(part_first.astype(jnp.bfloat16), "tensor").astype(jnp.float32)
    grad_tokens_norm, grad_first_gain, grad_first_shift = norm_pull(
        tokens_f, first_gain, first_shift, grad_first
    )
    grad_tokens_f = grad_middle + grad_tokens_norm
    grad_tokens = grad_tokens_f.astype(jnp.bfloat16)
    attn_grads = (
        lax.psum(grad_qkv_weight.astype(jnp.bfloat16), "dp").astype(jnp.float32),
        lax.psum(grad_qv_bias.astype(jnp.bfloat16), "dp").astype(jnp.float32),
        lax.psum(grad_out_weight.astype(jnp.bfloat16), "dp").astype(jnp.float32),
        lax.psum(grad_out_bias.astype(jnp.bfloat16), "dp").astype(jnp.float32),
        lax.psum(grad_first_gain.astype(jnp.bfloat16), "dp").astype(jnp.float32),
        lax.psum(grad_first_shift.astype(jnp.bfloat16), "dp").astype(jnp.float32),
    )
    return (
        output,
        grad_tokens,
        attn_grads[4],
        attn_grads[5],
        attn_grads[0],
        attn_grads[1],
        attn_grads[2],
        attn_grads[3],
        mlp_grads[4],
        mlp_grads[5],
        mlp_grads[1],
        mlp_grads[2],
        mlp_grads[0],
        mlp_grads[3],
    )


def solution(mesh):
    return jax.shard_map(
        per_device,
        mesh=mesh,
        in_specs=(
            P("dp", None),
            P("dp", None),
            P(),
            P(),
            P(None, "tensor", None),
            P("tensor", None),
            P("tensor", None),
            P(),
            P(),
            P(),
            P(None, "tensor"),
            P("tensor"),
            P("tensor", None),
            P(),
            P("dp", None),
        ),
        out_specs=(
            P("dp", None),
            P("dp", None),
            P(),
            P(),
            P(None, "tensor", None),
            P("tensor", None),
            P("tensor", None),
            P(),
            P(),
            P(),
            P(None, "tensor"),
            P("tensor"),
            P("tensor", None),
            P(),
        ),
        check_vma=False,
    )
```

profile of v0, /device:TPU:0, one launch (start us, length us, event | category | flops | bytes accessed | tf_op | source)
XLA Modules:
  0.0 1107.8 jit_solution(12583510933273416951)
XLA Ops:
  9.8 2.9 convert_reduce_fusion
  12.7 3.0 fusion.87
  23.7 54.3 %while.40 = (s32[]{:T(128)}, bf16[4,512,2,64]{1,3,2,0:T(8,128)(2,1)S(1)}, f32[4,2,512]{2,1,0:T(2,128)}, s32[4]{0:T(128)S(1)}, s32[2048]{0:T(1024)S(1)}, /*index=...) while((s32[]{:T(128)}, ...), condition=%wide.region_13.14_spmd.clone, body=%wide.region_10.13_spmd.clone.sunk | while | flops 579862016 | bytes 47633140 | solution.py:64
  26.6 3.6 fusion.215
  30.2 3.2 fusion.216
  33.5 3.2 fusion.217
  40.2 3.6 fusion.215
  43.8 3.2 fusion.216
  47.0 3.2 fusion.217
  53.7 3.6 fusion.215
  57.4 3.2 fusion.216
  60.6 3.2 fusion.217
  67.3 3.6 fusion.215
  71.0 3.2 fusion.216
  74.2 3.2 fusion.217
  78.6 3.3 convolution_convert_fusion.2
  82.8 71.0 %while.39 = (s32[]{:T(128)}, bf16[4,512,2,64]{1,3,2,0:T(8,128)(2,1)}, s32[4]{0:T(128)S(1)}, s32[2048]{0:T(1024)S(1)}, s32[1,2048]{1,0:T(1,128)S(1)}, /*index=5*/...) while((s32[]{:T(128)}, ...), condition=%wide.region_5.6_spmd.clone, body=%wide.region_2.5_spmd.clone.sunk | while | flops 837817856 | bytes 17854704 | solution.py:64
  88.0 6.0 fusion.210
  94.0 6.9 fusion.211
  105.7 5.9 fusion.210
  111.6 6.9 fusion.211
  123.4 5.9 fusion.210
  129.3 6.9 fusion.211
  141.1 5.8 fusion.210
  146.9 6.9 fusion.211
  155.5 3.3 convolution_convert_fusion.3
  158.8 82.3 %all-reduce.9.cloned.1.call-done = bf16[2048,1024]{1,0:T(8,128)(2,1)} async-done(((bf16[2048,1024]{1,0:T(8,128)(2,1)}), bf16[2048,1024]{1,0:T(8,128)(2,1)}) %all-reduce.9.cloned.1.call-update) | async-done | bytes 4194320 | tf_op jit(solution)/shard_map/psum | solution.py:127
  241.1 5.0 fusion.92
  247.1 12.2 %multiply_reduce_fusion.1 = f32[2048]{0:T(1024)S(1)} fusion(f32[2048]{0:T(1024)S(1)} %broadcast_multiply_fusion, f32[1024]{0:T(1024)S(1)} %convert_element_type.254, bf16[2048,1024]{1,0:T(8,128)(2,1)S(1)} %copy-done.8, bf16[2048,1024]{1,0:T(8,128)(2,1)S(1)} %copy-done.4), kind=kLoop, calls=%fused_computation.112 | loop fusion | flops 14678016 | bytes 8409088 | tf_op jit(solution)/shard_map/reduce_sum | solution.py:14
  259.3 3.5 fusion.133
  262.9 6.4 fusion.136
  270.6 4.4 convolution_convert_fusion
  275.2 7.0 fusion.116
  283.0 4.5 convolution_convert_fusion.5
  287.5 256.7 %all-reduce.13.cloned.1.call-done = (bf16[2048,1024]{1,0:T(8,128)(2,1)}, bf16[2048,1024]{1,0:T(8,128)(2,1)}) async-done(((bf16[2048,1024]{1,0:T(8,128)(2,1)}, bf16[2048,1024]{1,0:T(8,128)(2,1)}), (bf16[2048,1024]{1,0:T(8,128)(2,1)}, bf16[2048,1024]{1,0:T(8,128)(2,1)})) %all-reduce.13.cloned.1.call-update) | async-done | bytes 8388624 | tf_op jit(solution)/shard_map/psum | solution.py:129
  544.2 9.5 fusion.84
  554.9 10.1 fusion.85
  565.1 5.8 fusion.138
  575.9 127.6 %while.41 = (s32[]{:T(128)}, f32[2048,2,64]{0,2,1:T(8,128)S(1)}, f32[2048,2,64]{0,2,1:T(8,128)}, bf16[4,512,2,64]{1,3,2,0:T(8,128)(2,1)}, s32[4]{0:T(128)S(1)}, ...) while((s32[]{:T(128)}, f32[2048,2,64]{0,2,1:T(8,128)S(1)}, ...), condition=%wide.region_22.23_spmd.clone, body=%wide.region_20.22_spmd.clone.sunk | while | flops 1371864576 | bytes 142909952 | solution.py:101
  584.0 7.2 multiply_reduce_fusion.4
  591.3 8.7 multiply_convert_fusion.6
  599.9 4.6 fusion.230
  615.8 7.2 multiply_reduce_fusion.4
  623.1 8.7 multiply_convert_fusion.6
  631.7 4.6 fusion.230
  647.6 7.2 multiply_reduce_fusion.4
  654.9 8.7 multiply_convert_fusion.6
  663.5 4.6 fusion.230
  679.4 7.2 multiply_reduce_fusion.4
  686.6 8.7 multiply_convert_fusion.6
  695.3 4.6 fusion.230
  706.2 5.7 bitcast_convert_fusion
  714.9 9.4 convolution_convert_fusion.1
  724.3 3.0 reduce_sum.248
  727.4 2.9 reduce_sum.243
  730.5 52.1 %all-reduce.15.cloned.1.call-done = (bf16[1024,2,192]{0,2,1:T(8,128)(2,1)}, bf16[128,1024]{1,0:T(8,128)(2,1)}, bf16[1024,512]{1,0:T(8,128)(2,1)}, bf16[512,1024]{1,0:T(8,128)(2,1)}) async-done(((bf16[1024,2,192]{0,2,1:T(8,128)(2,1)}, bf16[128,1024]{1,0:T(8,128)(2,1)}, bf16[1024,512]{1,0:T(8,128)(2,1)}, bf16[512,1024]{1,0:T(8,128)(2,1)}), (bf16[1024,2,192]{0,2,1:T(8,128)(2,1)}, bf16[128,1024]{1,0:T(8,128)(2,1)}, ...) | async-done | bytes 3145744 | tf_op jit(solution)/shard_map/psum | solution.py:254
  786.8 2.8 convert_element_type.298
  789.6 2.8 convert_element_type.302
  792.4 264.8 %all-reduce.11.cloned.1.call-done = (bf16[2048,1024]{1,0:T(8,128)(2,1)}, bf16[2048,1024]{1,0:T(8,128)(2,1)}) async-done(((bf16[2048,1024]{1,0:T(8,128)(2,1)}, bf16[2048,1024]{1,0:T(8,128)(2,1)}), (bf16[2048,1024]{1,0:T(8,128)(2,1)}, bf16[2048,1024]{1,0:T(8,128)(2,1)})) %all-reduce.11.cloned.1.call-update) | async-done | bytes 8388624 | tf_op jit(solution)/shard_map/psum | solution.py:179
  1057.2 4.5 fusion.88
  1061.7 2.9 reduce_sum.235
  1064.6 6.8 fusion.86
  1071.4 10.8 all-reduce.2
  1086.9 14.1 %add_convert_fusion = (bf16[2048,1024]{1,0:T(8,128)(2,1)}, bf16[2048,1024]{1,0:T(8,128)(2,1)}) fusion(f32[2048,1024]{1,0:T(8,128)} %copy-done.7, bf16[2048,1024]{1,0:T(8,128)(2,1)} %param.21, bf16[2048,1024]{1,0:T(8,128)(2,1)} %get-tuple-element.350, f32[2048]{0:T(1024)S(1)} %negate_multiply_fusion, f32[2048]{0:T(1024)S(1)} %multiply_multiply_fusion.2, ...), kind=kLoop, calls=%fused_computation.109 | loop fusion | flops 37748736 | bytes 33599488 | tf_op jit(solution)/shard_map/convert_element_type | solution.py:252
  (296 shorter events, 100.3 us)
Async XLA Ops:
  7.2 252.1 %copy-start = (bf16[1024,512]{1,0:T(8,128)(2,1)S(1)}, bf16[1024,512]{1,0:T(8,128)(2,1)}, u32[]{:S(2)}) copy-start(bf16[1024,512]{1,0:T(8,128)(2,1)} %param.31) | copy-start | bytes 3145732
  7.2 233.9 %all-reduce.9.cloned.1.call-start = ((), (), s32[]{:S(2)}) async-start(), calls=%async_computation | async-start | bytes 8388608 | tf_op jit(solution)/shard_map/psum | solution.py:127
  7.3 8.5 copy-start.3
  9.1 8.3 copy-start.31
  9.8 7.7 copy-start.49
  12.7 6.6 copy-start.27
  15.7 3.6 copy-start.33
  15.7 3.6 copy-start.29
  17.5 6.2 copy-start.24
  23.7 54.9 %copy-start.25 = (bf16[128,1024]{1,0:T(8,128)(2,1)S(1)}, bf16[128,1024]{1,0:T(8,128)(2,1)}, u32[]{:S(2)}) copy-start(bf16[128,1024]{1,0:T(8,128)(2,1)} %param.27) | copy-start | bytes 786436
  78.5 4.3 copy-start.17
  81.9 462.3 %all-reduce.13.cloned.1.call-start = ((), (), s32[]{:S(2)}) async-start(), calls=%async_computation.2 | async-start | bytes 16777216 | tf_op jit(solution)/shard_map/psum | solution.py:129
  82.8 71.1 %copy-start.45 = (bf16[512]{0:T(512)(128)(2,1)S(1)}, bf16[512]{0:T(512)(128)(2,1)}, u32[]{:S(2)}) copy-start(bf16[512]{0:T(512)(128)(2,1)} %param.32) | copy-start | bytes 3076
  82.8 71.1 %copy-start.39 = (bf16[1024]{0:T(1024)(128)(2,1)S(1)}, bf16[1024]{0:T(1024)(128)(2,1)}, u32[]{:S(2)}) copy-start(bf16[1024]{0:T(1024)(128)(2,1)} %param.28) | copy-start | bytes 6148
  82.8 71.1 %copy-start.40 = (bf16[1024]{0:T(1024)(128)(2,1)S(1)}, bf16[1024]{0:T(1024)(128)(2,1)}, u32[]{:S(2)}) copy-start(bf16[1024]{0:T(1024)(128)(2,1)} %param.29) | copy-start | bytes 6148
  82.8 71.1 %copy-start.41 = (bf16[1024]{0:T(1024)(128)(2,1)S(1)}, bf16[1024]{0:T(1024)(128)(2,1)}, u32[]{:S(2)}) copy-start(bf16[1024]{0:T(1024)(128)(2,1)} %param.30) | copy-start | bytes 6148
  153.8 121.3 %copy-start.43 = (f32[512]{0:T(512)}, f32[512]{0:T(512)S(1)}, u32[]{:S(2)}) copy-start(f32[512]{0:T(512)S(1)} %convert_element_type.258) | copy-start | bytes 6148
  153.9 128.3 %copy-start.37 = (f32[1024]{0:T(1024)}, f32[1024]{0:T(1024)S(1)}, u32[]{:S(2)}) copy-start(f32[1024]{0:T(1024)S(1)} %convert_element_type.256) | copy-start | bytes 12292
  241.1 5.0 copy-start.4
  241.1 5.9 copy-start.8
  259.3 3.5 copy-start.15
  259.3 3.5 copy-start.47
  262.9 6.4 copy-start.52
  275.1 507.5 %all-reduce.15.cloned.1.call-start = ((), (), s32[]{:S(2)}) async-start(), calls=%async_computation.3 | async-start | bytes 6291456 | tf_op jit(solution)/shard_map/psum | solution.py:254
  275.2 7.1 copy-start.5
  275.2 7.1 copy-start.9
  275.2 7.9 copy-start.51
  544.2 9.5 copy-start.6
  544.2 9.5 copy-start.10
  544.2 9.6 copy-start.11
  544.2 10.7 copy-start.12
  554.9 10.1 copy-start.16
  565.0 5.8 copy-start.18
  570.8 4.3 copy-start.7
  584.0 7.2 copy-start.1
  591.3 8.7 copy-start.13
  599.9 4.6 copy-start.2
  599.9 4.8 copy-start.19
  604.7 3.4 copy-start.14
  615.8 7.2 copy-start.1
  623.1 8.7 copy-start.13
  631.7 4.6 copy-start.2
  631.7 4.8 copy-start.19
  636.5 3.4 copy-start.14
  647.6 7.2 copy-start.1
  654.8 8.7 copy-start.13
  663.5 4.6 copy-start.2
  663.5 4.8 copy-start.19
  668.3 3.4 copy-start.14
  679.4 7.2 copy-start.1
  686.6 8.7 copy-start.13
  695.3 4.6 copy-start.2
  695.3 4.8 copy-start.19
  700.1 3.4 copy-start.14
  706.2 5.7 copy-start.23
  714.8 342.4 %all-reduce.11.cloned.1.call-start = ((), (), s32[]{:S(2)}) async-start(), calls=%async_computation.1 | async-start | bytes 16777216 | tf_op jit(solution)/shard_map/psum | solution.py:179
  724.3 6.0 copy-start.21
  724.3 332.9 %copy-start.28 = (f32[2048]{0:T(1024)S(1)}, f32[2048]{0:T(1024)}, u32[]{:S(2)}) copy-start(f32[2048]{0:T(1024)} %copy-done.27) | copy-start | bytes 24580
  724.3 332.9 %copy-start.32 = (f32[1024]{0:T(1024)S(1)}, f32[1024]{0:T(1024)}, u32[]{:S(2)}) copy-start(f32[1024]{0:T(1024)} %copy-done.31) | copy-start | bytes 12292
  789.6 275.0 %copy-start.34 = (f32[2048]{0:T(1024)S(1)}, f32[2048]{0:T(1024)}, u32[]{:S(2)}) copy-start(f32[2048]{0:T(1024)} %copy-done.33) | copy-start | bytes 24580
  789.6 275.0 %copy-start.30 = (f32[2048]{0:T(1024)S(1)}, f32[2048]{0:T(1024)}, u32[]{:S(2)}) copy-start(f32[2048]{0:T(1024)} %copy-done.29) | copy-start | bytes 24580
  1061.7 9.8 copy-start.35
  1061.7 9.8 copy-start.36
  1061.7 9.8 copy-start.46
  (11 other events, 24.8 us)
Sparse Core Ops, SparseCore 0:
  82.0 159.0 all-reduce.8
  275.2 268.9 all-reduce.12
  714.9 67.5 all-reduce.14
  787.0 270.1 all-reduce.10
where the time goes:
time: 1110 us
  waiting for transfers between devices  656 us (59%)
  matrix products  204 us (18%)
  other arithmetic  183 us (16%)
  local copies, waits for them, and re-layouts  23.2 us (2%)
  loops' own time  17 us (2%)
  between operations  14.7 us (1%)
    psum x2, waiting for transfers between devices, attn_front(): mixed = lax.psum(partial_out, 'tensor').astype(jnp.float32)  339 us
    psum x1, waiting for transfers between devices, per_device(): feed = lax.psum(part_down, 'tensor').astype(jnp.float32)  265 us
    psum x1, waiting for transfers between devices, per_device(): lax.psum(grad_qkv_weight.astype(jnp.bfloat16), 'dp').astype(jnp.float32)  52.1 us
    dot_general x8, matrix products, block_scores(): jnp.einsum('qhe,khe->hqk', query_blk, keys, preferred_element_type=jnp.fl...  43.4 us
    dot_general x8, matrix products, one_block(): jnp.einsum('hqk,khe->qhe', weights_low, values, preferred_element_type=jn...  40.4 us
    reduce_sum x6, other arithmetic, layer_norm(): return offset * lax.rsqrt(spread + norm_eps) * gain_vec + shift_vec  36.7 us
    convert_element_type x4, other arithmetic, one_block(): grad_scores = (probs * (grad_probs - inner)).astype(jnp.bfloat16)  34.7 us
    sub x4, matrix products, one_block(): expo = jnp.exp(scores - peak)  23.6 us
  transfers between devices with their start and end apart: 4, of which 4 were waited for; matrix products, arithmetic and copies ran while one was open for 10% of the time, Pallas kernels for 0%

commit v1 on v0

--- a/solution.py
+++ b/solution.py
@@ -105,7 +105,7 @@
 
 
 def attn_front(
-    tokens_f, seg_row, first_gain, first_shift, qkv_weight, qv_bias, out_weight, out_bias, again
+    tokens_f, seg_row, first_gain, first_shift, qkv_weight, qv_bias, out_weight, out_bias
 ):
     length = tokens_f.shape[0]
     normed_low = layer_norm(
@@ -123,10 +123,7 @@
     partial_out = jnp.dot(context_low, out_weight, preferred_element_type=jnp.float32).astype(
         jnp.bfloat16
     )
-    if again:
-        mixed = lax.psum(partial_out, "tensor").astype(jnp.float32)
-    else:
-        mixed = lax.psum(partial_out, "tensor").astype(jnp.float32)
+    mixed = lax.psum(partial_out, "tensor").astype(jnp.float32)
     middle = tokens_f + mixed + out_bias.astype(jnp.float32)
     return (normed_low, query, keys, values, context_low, lse_blocks, middle, slopes)
 
@@ -169,7 +166,7 @@
     tokens_f = tokens.astype(jnp.float32)
     seg_row = segment_ids[0]
     saved = attn_front(
-        tokens_f, seg_row, first_gain, first_shift, qkv_weight, qv_bias, out_weight, out_bias, False
+        tokens_f, seg_row, first_gain, first_shift, qkv_weight, qv_bias, out_weight, out_bias
     )
     middle = saved[6]
     second_low, upper, hidden_low = mlp_front(middle, second_gain, second_shift, up_weight, up_bias)
@@ -178,11 +175,6 @@
     )
     feed = lax.psum(part_down, "tensor").astype(jnp.float32)
     output = (middle + feed + down_bias.astype(jnp.float32)).astype(jnp.bfloat16)
-    saved = attn_front(
-        tokens_f, seg_row, first_gain, first_shift, qkv_weight, qv_bias, out_weight, out_bias, True
-    )
-    middle = saved[6]
-    second_low, upper, hidden_low = mlp_front(middle, second_gain, second_shift, up_weight, up_bias)
     normed_low, query, keys, values, context_low, lse_blocks, middle, slopes = saved
     grad_out = cotangent.astype(jnp.float32)
     grad_down_weight = jnp.einsum(

time: 1110 us -> 964 us (0.87)
  matrix products: 204 us -> 134 us
  waiting for transfers between devices: 656 us -> 617 us
  other arithmetic: 183 us -> 146 us
    psum x2 -> x1, waiting for transfers between devices: 339 us -> 159 us  [attn_front(): mixed = lax.psum(partial_out, 'tensor').astype(jnp.float32)]
    psum x0 -> x1, waiting for transfers between devices: none -> 143 us  [per_device(): lax.psum(part_second.astype(jnp.bfloat16), 'tensor').astype(jnp.float32)]
    dot_general x8 -> x4, matrix products: 40.4 us -> 12.8 us  [one_block(): jnp.einsum('hqk,khe->qhe', weights_low, values, preferred_element_type=jn...]
    sub x4 -> x0, matrix products: 23.6 us -> none  [one_block(): expo = jnp.exp(scores - peak)]
    reduce_sum x2, other arithmetic: 15.2 us -> 3.51 us  [layer_norm(): spread = jnp.mean(offset * offset, axis=-1, keepdims=True)]
  transfers between devices with their start and end apart: 4 -> 4, of which waited for: 4 -> 4; matrix products, arithmetic and copies ran while one was open for 10% -> 4% of each run, Pallas kernels for 0% -> 0%
where the time goes in v1:
time: 964 us; the launch traced here: 956 us
  waiting for transfers between devices  617 us (64%)
  other arithmetic  146 us (15%)
  matrix products  134 us (14%)
  local copies, waits for them, and re-layouts  18.3 us (2%)
  between operations  14.6 us (2%)
  loops' own time  14.3 us (1%)
  blocking collectives  10.8 us (1%)
    psum x1, waiting for transfers between devices, per_device(): feed = lax.psum(part_down, 'tensor').astype(jnp.float32)  266 us
    psum x1, waiting for transfers between devices, attn_front(): mixed = lax.psum(partial_out, 'tensor').astype(jnp.float32)  159 us
    psum x1, waiting for transfers between devices, per_device(): lax.psum(part_second.astype(jnp.bfloat16), 'tensor').astype(jnp.float32)  143 us
    psum x1, waiting for transfers between devices, per_device(): lax.psum(grad_qkv_weight.astype(jnp.bfloat16), 'dp').astype(jnp.float32)  49.7 us
    dot_general x8, matrix products, block_scores(): jnp.einsum('qhe,khe->hqk', query_blk, keys, preferred_element_type=jnp.fl...  36 us
    convert_element_type x4, other arithmetic, one_block(): grad_scores = (probs * (grad_probs - inner)).astype(jnp.bfloat16)  34.7 us
    reduce_sum x6, other arithmetic, layer_norm(): return offset * lax.rsqrt(spread + norm_eps) * gain_vec + shift_vec  30.7 us
  transfers between devices with their start and end apart: 4, of which 4 were waited for; matrix products, arithmetic and copies ran while one was open for 4% of the time, Pallas kernels for 0%

profile of v1, /device:TPU:0, one launch (start us, length us, event | category | flops | bytes accessed | tf_op | source)
XLA Modules:
  0.0 955.8 jit_solution(13853205372670522851)
XLA Ops:
  9.8 2.8 convert_reduce_fusion
  14.1 1.7 fusion.46
  15.8 1.8 fusion.81
  19.6 1.7 fusion.68
  21.4 48.7 %while.28 = (s32[]{:T(128)}, bf16[4,512,2,64]{1,3,2,0:T(8,128)(2,1)S(1)}, f32[4,2,512]{2,1,0:T(2,128)S(1)}, s32[4]{0:T(128)S(1)}, s32[2048]{0:T(1024)S(1)}, /*in...) while((s32[]{:T(128)}, ...), condition=%wide.region_5.6_spmd.clone, body=%wide.region_2.5_spmd.clone.sunk | while | flops 579862016 | bytes 47633644 | solution.py:64
  24.4 2.8 fusion.130
  27.1 3.2 fusion.131
  30.3 3.2 fusion.132
  36.5 2.8 fusion.130
  39.3 3.2 fusion.131
  42.5 3.2 fusion.132
  48.6 2.8 fusion.130
  51.4 3.2 fusion.131
  54.6 3.2 fusion.132
  60.8 2.8 fusion.130
  63.5 3.2 fusion.131
  66.7 3.2 fusion.132
  70.7 3.3 convolution_convert_fusion.2
  74.8 158.6 %all-reduce.8.cloned.1.call-done = bf16[2048,1024]{1,0:T(8,128)(2,1)} async-done(((bf16[2048,1024]{1,0:T(8,128)(2,1)}), bf16[2048,1024]{1,0:T(8,128)(2,1)}) %all-reduce.8.cloned.1.call-update) | async-done | bytes 4194320 | tf_op jit(solution)/shard_map/psum | solution.py:126
  233.3 5.0 fusion.54
  239.2 2.1 multiply_reduce_fusion.1
  241.4 3.5 fusion.73
  244.9 6.4 fusion.76
  252.7 4.4 convolution_convert_fusion
  257.5 7.1 convolution_convert_fusion.4
  265.3 4.5 convolution_convert_fusion.5
  269.8 142.9 %all-reduce.10.cloned.1.call-done = bf16[2048,1024]{1,0:T(8,128)(2,1)} async-done(((bf16[2048,1024]{1,0:T(8,128)(2,1)}), bf16[2048,1024]{1,0:T(8,128)(2,1)}) %all-reduce.10.cloned.1.call-update) | async-done | bytes 4194320 | tf_op jit(solution)/shard_map/psum | solution.py:196
  412.7 6.8 fusion.47
  421.0 6.9 fusion.48
  427.9 5.7 fusion.78
  433.6 1.9 fusion.65
  436.9 2.3 convolution_convert_fusion.3
  440.1 117.1 %while.29 = (s32[]{:T(128)}, f32[2048,2,64]{0,2,1:T(8,128)S(1)}, f32[2048,2,64]{0,2,1:T(8,128)}, bf16[4,512,2,64]{1,3,2,0:T(8,128)(2,1)}, s32[4]{0:T(128)S(1)}, ...) while((s32[]{:T(128)}, f32[2048,2,64]{0,2,1:T(8,128)S(1)}, ...), condition=%wide.region_15.16_spmd.clone, body=%wide.region_13.15_spmd.clone.sunk | while | flops 1371864576 | bytes 145007648 | solution.py:101
  445.3 2.2 fusion.142
  447.6 6.2 multiply_reduce_fusion.3
  453.8 8.7 multiply_convert_fusion.5
  462.5 4.6 fusion.145
  474.5 2.2 fusion.142
  476.8 6.2 multiply_reduce_fusion.3
  483.0 8.7 multiply_convert_fusion.5
  491.7 4.6 fusion.145
  503.7 2.3 fusion.142
  505.9 6.2 multiply_reduce_fusion.3
  512.2 8.7 multiply_convert_fusion.5
  520.8 4.6 fusion.145
  532.8 2.2 fusion.142
  535.1 6.2 multiply_reduce_fusion.3
  541.3 8.7 multiply_convert_fusion.5
  550.0 4.6 fusion.145
  560.1 1.8 fusion.82
  563.2 7.1 convolution_convert_fusion.1
  570.3 4.4 bitcast_convert_fusion
  574.7 3.0 reduce_sum.218
  577.7 2.9 reduce_sum.213
  580.9 49.7 %all-reduce.14.cloned.1.call-done = (bf16[1024,2,192]{0,2,1:T(8,128)(2,1)}, bf16[128,1024]{1,0:T(8,128)(2,1)}, bf16[1024,512]{1,0:T(8,128)(2,1)}, bf16[512,1024]{1,0:T(8,128)(2,1)}) async-done(((bf16[1024,2,192]{0,2,1:T(8,128)(2,1)}, bf16[128,1024]{1,0:T(8,128)(2,1)}, bf16[1024,512]{1,0:T(8,128)(2,1)}, bf16[512,1024]{1,0:T(8,128)(2,1)}), (bf16[1024,2,192]{0,2,1:T(8,128)(2,1)}, bf16[128,1024]{1,0:T(8,128)(2,1)}, ...) | async-done | bytes 3145744 | tf_op jit(solution)/shard_map/psum | solution.py:246
  630.6 1.9 convert_element_type.246
  632.4 2.5 convert_element_type.241
  634.9 2.8 convert_element_type.253
  639.3 265.9 %all-reduce.12.cloned.1.call-done = (bf16[2048,1024]{1,0:T(8,128)(2,1)}, bf16[2048,1024]{1,0:T(8,128)(2,1)}) async-done(((bf16[2048,1024]{1,0:T(8,128)(2,1)}, bf16[2048,1024]{1,0:T(8,128)(2,1)}), (bf16[2048,1024]{1,0:T(8,128)(2,1)}, bf16[2048,1024]{1,0:T(8,128)(2,1)})) %all-reduce.12.cloned.1.call-update) | async-done | bytes 8388624 | tf_op jit(solution)/shard_map/psum | solution.py:176
  905.2 4.5 fusion.51
  909.7 2.9 reduce_sum.205
  912.7 6.8 fusion.49
  919.5 10.8 %all-reduce.1 = (bf16[1024]{0:T(1024)(128)(2,1)S(1)}, bf16[1024]{0:T(1024)(128)(2,1)S(1)}, bf16[2,128]{1,0:T(2,128)(2,1)S(1)}, bf16[1024]{0:T(1024)(128)(2,1)S(1...) all-reduce(bf16[1024]{0:T(1024)(128)(2,1)S(1)} %get-tuple-element.2, ...), channel_id=1, replica_groups=mesh['dp'=4,'tensor'=8] {'dp'}, use_global_device_ids=true, to_apply=%region_20.21 | all-reduce | flops 6912 | bytes 27648 | tf_op jit(solution)/shard_map/psum | solution.py:250
  935.0 14.1 %add_convert_fusion = (bf16[2048,1024]{1,0:T(8,128)(2,1)}, bf16[2048,1024]{1,0:T(8,128)(2,1)}) fusion(f32[2048,1024]{1,0:T(8,128)} %copy-done.10, bf16[2048,1024]{1,0:T(8,128)(2,1)} %param.19, bf16[2048,1024]{1,0:T(8,128)(2,1)} %get-tuple-element.260, f32[2048]{0:T(1024)S(1)} %negate_multiply_fusion, f32[2048]{0:T(1024)S(1)} %multiply_multiply_fusion.2, ...), kind=kLoop, calls=%fused_computation.75 | loop fusion | flops 37748736 | bytes 33599488 | tf_op jit(solution)/shard_map/convert_element_type | solution.py:244
  (267 shorter events, 52.9 us)
Async XLA Ops:
  7.2 237.7 %copy-start = (bf16[512,1024]{1,0:T(8,128)(2,1)S(1)}, bf16[512,1024]{1,0:T(8,128)(2,1)}, u32[]{:S(2)}) copy-start(bf16[512,1024]{1,0:T(8,128)(2,1)} %param.31) | copy-start | bytes 3145732
  7.2 226.1 %all-reduce.8.cloned.1.call-start = ((), (), s32[]{:S(2)}) async-start(), calls=%async_computation | async-start | bytes 8388608 | tf_op jit(solution)/shard_map/psum | solution.py:126
  7.3 5.4 copy-start.3
  9.1 5.0 copy-start.35
  12.6 3.2 copy-start.29
  17.9 3.5 copy-start.26
  21.4 49.3 %copy-start.28 = (bf16[128,1024]{1,0:T(8,128)(2,1)S(1)}, bf16[128,1024]{1,0:T(8,128)(2,1)}, u32[]{:S(2)}) copy-start(bf16[128,1024]{1,0:T(8,128)(2,1)} %param.25) | copy-start | bytes 786436
  70.2 3.9 copy-start.16
  70.7 3.3 copy-start.18
  74.1 338.6 %all-reduce.10.cloned.1.call-start = ((), (), s32[]{:S(2)}) async-start(), calls=%async_computation.1 | async-start | bytes 8388608 | tf_op jit(solution)/shard_map/psum | solution.py:196
  74.7 182.7 %copy-start.45 = (f32[512]{0:T(512)}, f32[512]{0:T(512)S(1)}, u32[]{:S(2)}) copy-start(f32[512]{0:T(512)S(1)} %convert_element_type.218) | copy-start | bytes 6148
  74.7 353.1 %copy-start.31 = (f32[1024]{0:T(1024)}, f32[1024]{0:T(1024)S(1)}, u32[]{:S(2)}) copy-start(f32[1024]{0:T(1024)S(1)} %convert_element_type.214) | copy-start | bytes 12292
  233.3 5.0 copy-start.4
  233.3 5.9 copy-start.7
  241.4 3.5 copy-start.14
  244.9 6.4 copy-start.54
  257.1 373.4 %all-reduce.14.cloned.1.call-start = ((), (), s32[]{:S(2)}) async-start(), calls=%async_computation.3 | async-start | bytes 6291456 | tf_op jit(solution)/shard_map/psum | solution.py:246
  257.4 7.1 copy-start.5
  257.4 7.1 copy-start.8
  257.4 7.9 copy-start.53
  412.7 6.8 copy-start.6
  412.7 7.1 copy-start.9
  412.7 8.3 copy-start.11
  421.0 6.9 copy-start.15
  427.9 5.7 copy-start.19
  433.6 3.3 copy-start.10
  445.3 2.3 copy-start.17
  447.6 6.2 copy-start.1
  453.8 8.7 copy-start.12
  462.5 4.6 copy-start.2
  462.5 4.8 copy-start.20
  467.2 2.4 copy-start.13
  474.5 2.3 copy-start.17
  476.8 6.2 copy-start.1
  483.0 8.7 copy-start.12
  491.7 4.6 copy-start.2
  491.7 4.8 copy-start.20
  496.4 2.4 copy-start.13
  503.6 2.3 copy-start.17
  505.9 6.2 copy-start.1
  512.2 8.7 copy-start.12
  520.8 4.6 copy-start.2
  520.8 4.8 copy-start.20
  525.6 2.4 copy-start.13
  532.8 2.3 copy-start.17
  535.1 6.2 copy-start.1
  541.3 8.7 copy-start.12
  550.0 4.6 copy-start.2
  550.0 4.8 copy-start.20
  554.8 2.4 copy-start.13
  557.2 2.9 copy-start.24
  562.9 7.4 copy-start.51
  562.9 342.3 %all-reduce.12.cloned.1.call-start = ((), (), s32[]{:S(2)}) async-start(), calls=%async_computation.2 | async-start | bytes 16777216 | tf_op jit(solution)/shard_map/psum | solution.py:176
  574.7 3.0 copy-start.44
  574.7 5.9 copy-start.22
  630.6 7.2 copy-start.27
  632.4 272.8 %copy-start.30 = (f32[2048]{0:T(1024)S(1)}, f32[2048]{0:T(1024)}, u32[]{:S(2)}) copy-start(f32[2048]{0:T(1024)} %copy-done.29) | copy-start | bytes 24580
  632.4 272.8 %copy-start.36 = (f32[1024]{0:T(1024)S(1)}, f32[1024]{0:T(1024)}, u32[]{:S(2)}) copy-start(f32[1024]{0:T(1024)} %copy-done.35) | copy-start | bytes 12292
  909.7 2.9 copy-start.38
  909.7 2.9 copy-start.34
  912.6 6.9 copy-start.39
  912.6 6.9 copy-start.40
  912.6 6.8 copy-start.48
  912.7 22.3 %copy-start.32 = (f32[1024]{0:T(1024)S(1)}, f32[1024]{0:T(1024)}, u32[]{:S(2)}) copy-start(f32[1024]{0:T(1024)} %copy-done.31) | copy-start | bytes 12292
  (16 other events, 20.4 us)
Sparse Core Ops, SparseCore 0:
  74.2 159.0 all-reduce.7
  257.3 155.3 all-reduce.9
  563.0 67.4 all-reduce.13
  635.1 270.1 all-reduce.11

commit v2 on v1

v2 whole, which is shorter than its diff:
```python
import functools
import math

import jax
import jax.numpy as jnp
from jax import lax
from jax.experimental import pallas as pl
from jax.experimental.pallas import tpu as pltpu
from jax.sharding import PartitionSpec as P

MESH = pl.DeviceIdType.MESH
ANY = pl.BlockSpec(memory_space=pl.ANY)
VM = pl.BlockSpec(memory_space=pltpu.VMEM)


def grid_of(n_tensor):
    lines = min(4, n_tensor)
    return lines, n_tensor // lines


def where_am_i(n_tensor):
    lines, wide = grid_of(n_tensor)
    dp, t = lax.axis_index("dp"), lax.axis_index("tensor")
    return dp, t, t // wide, t % wide


def greet(peers):
    barrier = pltpu.get_barrier_semaphore()
    for ok, peer in peers:
        @pl.when(ok)
        def _():
            pl.semaphore_signal(barrier, inc=1, device_id=peer, device_id_type=MESH)
    pl.semaphore_wait(barrier, sum(jnp.int32(ok) for ok, peer in peers))


def neighbours(n_tensor, use_y=True, use_x=True, use_core=True):
    lines, wide = grid_of(n_tensor)
    dp, t, z, y = where_am_i(n_tensor)
    out = [(z > 0, (dp, t - wide)), (z < lines - 1, (dp, t + wide))]
    if use_y:
        out += [(y > 0, (dp, t - 1)), (y < wide - 1, (dp, t + 1))]
    if use_x:
        out.append((dp >= 0, (dp ^ 2, t)))
    if use_core:
        out.append((dp >= 0, (dp ^ 1, t)))
    return out


def gather_kernel(n_tensor, n_attn, n_mlp, *refs):
    lines, wide = grid_of(n_tensor)
    dp, t, z, y = where_am_i(n_tensor)
    n = n_attn + n_mlp
    own, full = refs[:n], refs[n : 2 * n]
    z_send, z_recv, y_send, y_recv, x_send, x_recv, c_send, c_recv, l_sem = refs[2 * n :]
    quad = dp % 4

    def slot(a, zz, yy):
        return zz * wide + yy if a < n_attn else zz

    def piece(ref, a, q):
        rows = own[a].shape[0] // 4
        return ref.at[pl.ds(pl.multiple_of(q * rows, rows), rows)]

    def block(a, zz, yy, q):
        return piece(full[a].at[slot(a, zz, yy)], a, q)

    def copy(src, dst, send, recv, peer):
        return pltpu.make_async_remote_copy(
            src_ref=src, dst_ref=dst, send_sem=send, recv_sem=recv, device_id=peer, device_id_type=MESH
        )

    greet(neighbours(n_tensor))
    local = [pltpu.make_async_copy(own[a], full[a].at[slot(a, z, y)], l_sem.at[a]) for a in range(n)]
    for c in local:
        c.start()
    up, down = (dp, t + wide), (dp, t - wide)

    def z_copy(a, zz, side, mine=False):
        src = piece(own[a], a, quad) if mine else block(a, zz, y, quad)
        return copy(src, block(a, zz, y, quad), z_send.at[side, a, zz], z_recv.at[side, a, zz], (up, down)[side])

    def y_copy(a, zz, yy, side, mine=False):
        src = piece(own[a], a, quad) if mine else block(a, zz, yy, quad)
        peer = ((dp, t + 1), (dp, t - 1))[side]
        return copy(src, block(a, zz, yy, quad), y_send.at[side, a, zz, yy], y_recv.at[side, a, zz, yy], peer)

    def x_copy(a, zz, yy, q):
        return copy(block(a, zz, yy, q), block(a, zz, yy, q), x_send.at[a, zz, yy], x_recv.at[a, zz, yy], (dp ^ 2, t))

    def c_copy(a, zz, yy, q, hop):
        return copy(
            block(a, zz, yy, q), block(a, zz, yy, q), c_send.at[hop, a, zz, yy], c_recv.at[hop, a, zz, yy], (dp ^ 1, t)
        )

    def spread(a, zz, yy):
        x_copy(a, zz, yy, quad).start()
        c_copy(a, zz, yy, quad, 0).start()

    def arrays(group):
        return range(n_attn) if group == 0 else range(n_attn, n)

    def y_start(zz, yy, side, mine=False):
        @pl.when((y < wide - 1) if side == 0 else (y > 0))
        def _():
            for a in range(n_attn):
                y_copy(a, zz, yy, side, mine).start()

    for group in range(2):
        for side in range(2):
            @pl.when((z < lines - 1) if side == 0 else (z > 0))
            def _():
                for a in arrays(group):
                    z_copy(a, z, side, True).start()
        if group == 0:
            for side in range(2):
                y_start(z, y, side, True)
    for group in range(2):
        for k in range(1, lines):
            for side in range(2):
                zz = z - k if side == 0 else z + k

                @pl.when((zz >= 0) if side == 0 else (zz < lines))
                def _():
                    for a in arrays(group):
                        z_copy(a, zz, side).wait_recv()

                    @pl.when((z < lines - 1) if side == 0 else (z > 0))
                    def _():
                        for a in arrays(group):
                            z_copy(a, zz, side).start()

                    if group == 0:
                        for s in range(2):
                            y_start(zz, y, s)
                    for a in arrays(group):
                        spread(a, zz, y)
        if group == 0:
            for m in range(1, wide):
                for side in range(2):
                    yy = y - m if side == 0 else y + m

                    @pl.when((yy >= 0) if side == 0 else (yy < wide))
                    def _():
                        for zz in range(lines):
                            for a in range(n_attn):
                                y_copy(a, zz, yy, side).wait_recv()
                            if m < wide - 1:
                                y_start(zz, yy, side)
                            for a in range(n_attn):
                                spread(a, zz, yy)
    def others(group, body):
        for zz in range(lines):
            for yy in range(wide) if group == 0 else [y]:
                @pl.when((zz != z) | (yy != y))
                def _():
                    body(zz, yy)

    for group in range(2):
        def pass_on(zz, yy):
            for a in arrays(group):
                x_copy(a, zz, yy, quad ^ 2).wait_recv()
                c_copy(a, zz, yy, quad ^ 2, 1).start()

        others(group, pass_on)
    for group in range(2):
        def settle(zz, yy):
            for a in arrays(group):
                for hop in range(2):
                    c_copy(a, zz, yy, quad ^ (1 + 2 * hop), hop).wait_recv()
                    c_copy(a, zz, yy, quad ^ (2 * hop), hop).wait_send()
                x_copy(a, zz, yy, quad).wait_send()

        others(group, settle)
        for side in range(2):
            @pl.when((z < lines - 1) if side == 0 else (z > 0))
            def _():
                for k in range(lines):
                    zz = z - k if side == 0 else z + k

                    @pl.when((zz >= 0) if side == 0 else (zz < lines))
                    def _():
                        for a in arrays(group):
                            z_copy(a, zz, side).wait_send()
    for side in range(2):
        @pl.when((y < wide - 1) if side == 0 else (y > 0))
        def _():
            for zz in range(lines):
                for m in range(wide):
                    yy = y - m if side == 0 else y + m

                    @pl.when((yy >= 0) if side == 0 else (yy < wide))
                    def _():
                        for a in range(n_attn):
                            y_copy(a, zz, yy, side).wait_send()
    for c in local:
        c.wait()


def gather_weights(n_tensor, attn, mlp):
    lines, wide = grid_of(n_tensor)
    n = len(attn) + len(mlp)
    arrays = list(attn) + list(mlp)
    outs = [
        jax.ShapeDtypeStruct(((n_tensor if i < len(attn) else lines),) + a.shape, a.dtype) for i, a in enumerate(arrays)
    ]
    dma = pltpu.SemaphoreType.DMA
    return pl.pallas_call(
        functools.partial(gather_kernel, n_tensor, len(attn), len(mlp)),
        out_shape=outs,
        in_specs=[ANY] * n,
        out_specs=[ANY] * n,
        scratch_shapes=[dma((2, n, lines))] * 2
        + [dma((2, len(attn), lines, wide))] * 2
        + [dma((n, lines, wide))] * 2
        + [dma((2, n, lines, wide))] * 2
        + [dma((n,))],
        compiler_params=pltpu.CompilerParams(collective_id=0, has_side_effects=True),
        name="gather_weights",
    )(*arrays)


def add_rows(dst, terms):
    rows = dst.shape[0]
    step = 32 if rows % 32 == 0 else rows

    @pl.loop(0, rows // step)
    def _(i):
        part = pl.ds(pl.multiple_of(i * step, step), step)
        total = terms[0][part].astype(jnp.float32)
        for term in terms[1:]:
            total = total + term[part].astype(jnp.float32)
        dst[part] = total.astype(dst.dtype)


def reduce_kernel(n_tensor, n_attn, n_mlp, *refs):
    lines, wide = grid_of(n_tensor)
    dp, t, z, y = where_am_i(n_tensor)
    n = n_attn + n_mlp
    terms, final = refs[:n], refs[n : 2 * n]
    from_c, from_x, to_x, acc, from_y, from_z = (refs[(2 + i) * n : (3 + i) * n] for i in range(6))
    c_send, c_recv, x_send, x_recv, y_send, y_recv, z_send, z_recv, q_send, q_recv = refs[8 * n :]
    quad = dp % 4
    side_x = quad // 2
    core = quad % 2
    core_peer, x_peer = (dp ^ 1, t), (dp ^ 2, t)

    def copy(src, dst, send, recv, peer):
        return pltpu.make_async_remote_copy(
            src_ref=src, dst_ref=dst, send_sem=send, recv_sem=recv, device_id=peer, device_id_type=MESH
        )

    def slots(a):
        return [(zz, yy) for zz in range(lines) for yy in (range(wide) if a < n_attn else [0])]

    def index(a, zz, yy):
        return zz * wide + yy if a < n_attn else zz

    def quarter(ref, a, q):
        rows = final[a].shape[0] // 4
        return ref.at[pl.ds(pl.multiple_of(q * rows, rows), rows)]

    greet(neighbours(n_tensor))

    def c_copy(a, s, h):
        return copy(
            quarter(terms[a].at[s], a, h * 2 + 1 - core), from_c[a].at[s, h], c_send.at[a, s, h], c_recv.at[a, s, h],
            core_peer,
        )

    def x_copy(a, s):
        return copy(to_x[a].at[s], from_x[a].at[s], x_send.at[a, s], x_recv.at[a, s], x_peer)

    def y_copy(a, zz, yy, side):
        peer = ((dp, t + 1), (dp, t - 1))[side]
        return copy(
            acc[a].at[index(a, zz, yy)], from_y[a].at[side, zz * wide + yy], y_send.at[side, a, zz * wide + yy],
            y_recv.at[side, a, zz * wide + yy], peer,
        )

    def z_copy(a, zz, side):
        peer = ((dp, t + wide), (dp, t - wide))[side]
        return copy(
            acc[a].at[index(a, zz, y)], from_z[a].at[side, zz], z_send.at[side, a, zz], z_recv.at[side, a, zz], peer
        )

    order = list(range(n_attn, n)) + list(range(n_attn))
    for a in order:
        for zz, yy in slots(a):
            for h in range(2):
                c_copy(a, index(a, zz, yy), h).start()
    for a in order:
        for zz, yy in slots(a):
            s = index(a, zz, yy)
            for h in range(2):
                c_copy(a, s, h).wait_recv()
            add_rows(to_x[a].at[s], [quarter(terms[a].at[s], a, (1 - side_x) * 2 + core), from_c[a].at[s, 1 - side_x]])
            x_copy(a, s).start()
            add_rows(acc[a].at[s], [quarter(terms[a].at[s], a, quad), from_c[a].at[s, side_x]])
    for a in order:
        for zz, yy in slots(a):
            s = index(a, zz, yy)
            x_copy(a, s).wait_recv()
            add_rows(acc[a].at[s], [acc[a].at[s], from_x[a].at[s]])

            if a < n_attn:
                @pl.when((y == 0) & (yy > y))
                def _():
                    y_copy(a, zz, yy, 0).start()

                @pl.when((y == wide - 1) & (yy < y))
                def _():
                    y_copy(a, zz, yy, 1).start()
        if a >= n_attn:
            z_stage(a, lines, wide, z, y, z_copy, acc, from_z, index)
    for a in range(n_attn):
        for side in range(2):
            for m in range(1, wide):
                @pl.when((y >= 1) if side == 0 else (y < wide - 1))
                def _():
                    for zz in range(lines):
                        for yy in range(wide):
                            if m > 1:
                                continue

                            @pl.when((yy >= y) if side == 0 else (yy <= y))
                            def _():
                                s = index(a, zz, yy)
                                y_copy(a, zz, yy, side).wait_recv()
                                add_rows(acc[a].at[s], [acc[a].at[s], from_y[a].at[side, zz * wide + yy]])

                                @pl.when(yy != y)
                                def _():
                                    y_copy(a, zz, yy, side).start()

        z_stage(a, lines, wide, z, y, z_copy, acc, from_z, index)

    def q_copy(a, q, hop, peer):
        return copy(quarter(final[a], a, q), quarter(final[a], a, q), q_send.at[hop, a], q_recv.at[hop, a], peer)

    for a in order:
        add_rows(quarter(final[a], a, quad), [acc[a].at[index(a, z, y)]])
        q_copy(a, quad, 0, x_peer).start()
        q_copy(a, quad, 1, core_peer).start()
    for a in order:
        q_copy(a, quad ^ 2, 0, x_peer).wait_recv()
        q_copy(a, quad ^ 2, 2, core_peer).start()
    for a in order:
        q_copy(a, quad ^ 1, 1, core_peer).wait_recv()
        q_copy(a, quad ^ 3, 2, core_peer).wait_recv()
        q_copy(a, quad, 0, x_peer).wait_send()
        q_copy(a, quad, 1, core_peer).wait_send()
        q_copy(a, quad ^ 2, 2, core_peer).wait_send()
        for zz, yy in slots(a):
            s = index(a, zz, yy)
            for h in range(2):
                c_copy(a, s, h).wait_send()
            x_copy(a, s).wait_send()
            if a < n_attn:
                @pl.when((yy > y))
                def _():
                    y_copy(a, zz, yy, 0).wait_send()

                @pl.when((yy < y))
                def _():
                    y_copy(a, zz, yy, 1).wait_send()
        for zz in range(lines):
            @pl.when(zz > z)
            def _():
                z_copy(a, zz, 0).wait_send()

            @pl.when(zz < z)
            def _():
                z_copy(a, zz, 1).wait_send()


def z_stage(a, lines, wide, z, y, z_copy, acc, from_z, index):
    for k in range(lines - 1):
        far = lines - 1 - k
        for side, zz in ((0, far), (1, k)):
            @pl.when((z < zz) if side == 0 else (z > zz))
            def _():
                s = index(a, zz, y)

                @pl.when((z > 0) if side == 0 else (z < lines - 1))
                def _():
                    z_copy(a, zz, side).wait_recv()
                    add_rows(acc[a].at[s], [acc[a].at[s], from_z[a].at[side, zz]])

                z_copy(a, zz, side).start()
    s = index(a, z, y)
    for side in range(2):
        @pl.when((z > 0) if side == 0 else (z < lines - 1))
        def _():
            z_copy(a, z, side).wait_recv()
            add_rows(acc[a].at[s], [acc[a].at[s], from_z[a].at[side, z]])


def reduce_weights(n_tensor, attn, mlp):
    lines, wide = grid_of(n_tensor)
    arrays = list(attn) + list(mlp)
    n = len(arrays)
    vm, dma = pltpu.VMEM, pltpu.SemaphoreType.DMA
    quarters = [(a.shape[1] // 4, a.shape[2]) for a in arrays]
    outs = [jax.ShapeDtypeStruct(a.shape[1:], a.dtype) for a in arrays]
    low = jnp.bfloat16
    scratch = (
        [vm((a.shape[0], 2) + q, low) for a, q in zip(arrays, quarters)]
        + [vm((a.shape[0],) + q, low) for a, q in zip(arrays, quarters)]
        + [vm((a.shape[0],) + q, low) for a, q in zip(arrays, quarters)]
        + [vm((a.shape[0],) + q, low) for a, q in zip(arrays, quarters)]
        + [vm(((2, n_tensor) if i < len(attn) else (1, 1)) + q, low) for i, q in enumerate(quarters)]
        + [vm((2, lines) + q, low) for q in quarters]
    )
    sems = (
        [dma((n, n_tensor, 2))] * 2
        + [dma((n, n_tensor))] * 2
        + [dma((2, len(attn), n_tensor))] * 2
        + [dma((2, n, lines))] * 2
        + [dma((3, n))] * 2
    )
    sums = pl.pallas_call(
        functools.partial(reduce_kernel, n_tensor, len(attn), len(mlp)),
        out_shape=outs,
        in_specs=[VM] * n,
        out_specs=[VM] * n,
        scratch_shapes=scratch + sems,
        compiler_params=pltpu.CompilerParams(collective_id=1, has_side_effects=True, vmem_limit_bytes=60 * 2**20),
        name="reduce_weights",
    )(*arrays)
    if lax.axis_size("dp") > 4:
        sums = [lax.psum(s, "dp").astype(jnp.float32) * 0.25 for s in sums]
    return sums


def group_kernel(n_tensor, scatter, own, full, send, recv, l_sem):
    lines, wide = grid_of(n_tensor)
    dp, t, z, y = where_am_i(n_tensor)
    peers = [(y != yy, (dp, z * wide + yy)) for yy in range(wide)]
    greet(peers)
    local = pltpu.make_async_copy(own.at[y] if scatter else own, full.at[y], l_sem)
    local.start()

    def step(yy, slot):
        return pltpu.make_async_remote_copy(
            src_ref=own.at[yy] if scatter else own, dst_ref=full.at[slot], send_sem=send.at[yy], recv_sem=recv.at[slot],
            device_id=peers[yy][1], device_id_type=MESH,
        )

    for yy in range(wide):
        @pl.when(peers[yy][0])
        def _():
            step(yy, y).start()
    for yy in range(wide):
        @pl.when(peers[yy][0])
        def _():
            step(yy, yy).wait_recv()
            step(yy, y).wait_send()
    local.wait()


def group_exchange(n_tensor, own, scatter, cid, name):
    lines, wide = grid_of(n_tensor)
    dma = pltpu.SemaphoreType.DMA
    shape = own.shape if scatter else (wide,) + own.shape
    return pl.pallas_call(
        functools.partial(group_kernel, n_tensor, scatter),
        out_shape=jax.ShapeDtypeStruct(shape, own.dtype),
        in_specs=[ANY],
        out_specs=ANY,
        scratch_shapes=[dma((wide,)), dma((wide,)), dma],
        compiler_params=pltpu.CompilerParams(collective_id=cid, has_side_effects=True),
        name=name,
    )(own)


def halo_kernel(n_tensor, halo, own, got, send, recv):
    dp, t, z, y = where_am_i(n_tensor)
    ahead = [(t + 1 + m < n_tensor, (dp, t + 1 + m)) for m in range(halo)]
    greet(ahead + [(t - 1 - m >= 0, (dp, t - 1 - m)) for m in range(halo)])

    def step(m):
        return pltpu.make_async_remote_copy(
            src_ref=own.at[halo - 1 - m], dst_ref=got.at[m], send_sem=send.at[m], recv_sem=recv.at[m],
            device_id=(dp, t - 1 - m), device_id_type=MESH,
        )

    for m in range(halo):
        @pl.when(t - 1 - m >= 0)
        def _():
            step(m).start()
    for m in range(halo):
        @pl.when(t + 1 + m < n_tensor)
        def _():
            step(m).wait_recv()

        @pl.when(t - 1 - m >= 0)
        def _():
            step(m).wait_send()


def halo_exchange(n_tensor, own):
    halo = own.shape[0]
    dma = pltpu.SemaphoreType.DMA
    return pl.pallas_call(
        functools.partial(halo_kernel, n_tensor, halo),
        out_shape=jax.ShapeDtypeStruct(own.shape, own.dtype),
        in_specs=[ANY],
        out_specs=ANY,
        scratch_shapes=[dma((halo,)), dma((halo,))],
        compiler_params=pltpu.CompilerParams(collective_id=2, has_side_effects=True),
        name="halo_exchange",
    )(own)


def rows_kernel(n_tensor, n, *refs):
    lines, wide = grid_of(n_tensor)
    dp, t, z, y = where_am_i(n_tensor)
    own, full = refs[:n], refs[n : 2 * n]
    z_send, z_recv, y_send, y_recv, l_sem = refs[2 * n :]
    greet(neighbours(n_tensor, True, False, False))

    def copy(src, dst, send, recv, peer):
        return pltpu.make_async_remote_copy(
            src_ref=src, dst_ref=dst, send_sem=send, recv_sem=recv, device_id=peer, device_id_type=MESH
        )

    def z_copy(a, zz, side, mine=False):
        dst = full[a].at[zz * wide + y]
        peer = ((dp, t + wide), (dp, t - wide))[side]
        return copy(own[a] if mine else dst, dst, z_send.at[side, a, zz], z_recv.at[side, a, zz], peer)

    def y_copy(a, zz, yy, side, mine=False):
        dst = full[a].at[zz * wide + yy]
        peer = ((dp, t + 1), (dp, t - 1))[side]
        return copy(own[a] if mine else dst, dst, y_send.at[side, a, zz, yy], y_recv.at[side, a, zz, yy], peer)

    z_has = ((z < lines - 1), (z > 0))
    y_has = ((y < wide - 1), (y > 0))

    def when(condition, body):
        pl.when(condition)(body)

    local = [pltpu.make_async_copy(own[a], full[a].at[t], l_sem.at[a]) for a in range(n)]
    for side in range(2):
        for a in range(n):
            when(z_has[side], lambda: z_copy(a, z, side, True).start())
            when(y_has[side], lambda: y_copy(a, z, y, side, True).start())
    for c in local:
        c.start()
    for k in range(1, lines):
        for side in range(2):
            zz = z - k if side == 0 else z + k

            @pl.when((zz >= 0) & (zz < lines))
            def _():
                for a in range(n):
                    z_copy(a, zz, side).wait_recv()
                    when(z_has[side], lambda: z_copy(a, zz, side).start())
                    for s in range(2):
                        when(y_has[s], lambda: y_copy(a, zz, y, s).start())
    for m in range(1, wide):
        for side in range(2):
            yy = y - m if side == 0 else y + m

            @pl.when((yy >= 0) & (yy < wide))
            def _():
                for zz in range(lines):
                    for a in range(n):
                        y_copy(a, zz, yy, side).wait_recv()
                        if m < wide - 1:
                            when(y_has[side], lambda: y_copy(a, zz, yy, side).start())
    for side in range(2):
        for k in range(lines):
            zz = z - k if side == 0 else z + k

            @pl.when(z_has[side] & (zz >= 0) & (zz < lines))
            def _():
                for a in range(n):
                    z_copy(a, zz, side).wait_send()
        for m in range(wide):
            yy = y - m if side == 0 else y + m

            @pl.when(y_has[side] & (yy >= 0) & (yy < wide))
            def _():
                for zz in range(lines):
                    for a in range(n):
                        y_copy(a, zz, yy, side).wait_send()
    for c in local:
        c.wait()


def gather_rows(n_tensor, arrays, cid):
    lines, wide = grid_of(n_tensor)
    n = len(arrays)
    dma = pltpu.SemaphoreType.DMA
    return pl.pallas_call(
        functools.partial(rows_kernel, n_tensor, n),
        out_shape=[jax.ShapeDtypeStruct((n_tensor,) + a.shape, a.dtype) for a in arrays],
        in_specs=[ANY] * n,
        out_specs=[ANY] * n,
        scratch_shapes=[dma((2, n, lines))] * 2 + [dma((2, n, lines, wide))] * 2 + [dma((n,))],
        compiler_params=pltpu.CompilerParams(collective_id=cid, has_side_effects=True),
        name="gather_rows",
    )(*arrays)


def dot(a, b, contract, **kwargs):
    return lax.dot_general(a, b, (contract, ((), ())), preferred_element_type=jnp.float32, **kwargs)


NN, NT, TN = ((1,), (0,)), ((1,), (1,)), ((0,), (0,))


def head_of_lane(shape, heads):
    return lax.broadcasted_iota(jnp.int32, shape, 1) // (shape[1] // heads)


def attend_kernel(heads, slopes, dist, q, k, v, ctx):
    pair = pl.program_id(0)
    lanes = q.shape[2]
    scale = 1.0 / math.sqrt(lanes // heads)
    query, keys, values = q[0], k[0], v[0]
    head = head_of_lane(query.shape, heads)
    out = jnp.zeros(query.shape, jnp.float32)
    for h in range(heads):
        masked = jnp.where(head == h, query * jnp.bfloat16(scale), jnp.bfloat16(0))
        scores = dot(masked, keys, NT) - slopes[pair * heads + h] * dist[...]
        peak = jnp.max(scores, axis=1, keepdims=True)
        expo = jnp.exp(scores - peak)
        total = jnp.sum(expo, axis=1, keepdims=True)
        part = dot(expo.astype(jnp.bfloat16), values, NN) / total
        out = jnp.where(head == h, part, out)
    ctx[0] = out.astype(jnp.bfloat16)


def attend_pull_kernel(heads, slopes, dist, q, k, v, g, dq, dk, dv):
    pair = pl.program_id(0)
    lanes = q.shape[2]
    scale = 1.0 / math.sqrt(lanes // heads)
    query, keys, values, grad = q[0], k[0], v[0], g[0]
    head = head_of_lane(query.shape, heads)
    head_rows = lax.broadcasted_iota(jnp.int32, (lanes, query.shape[0]), 0) // (lanes // heads)
    low = jnp.bfloat16
    grad_q = jnp.zeros((lanes, query.shape[0]), jnp.float32)
    grad_k = jnp.zeros(keys.shape, jnp.float32)
    grad_v = jnp.zeros(keys.shape, jnp.float32)
    for h in range(heads):
        masked = jnp.where(head == h, query * low(scale), low(0))
        masked_grad = jnp.where(head == h, grad, low(0))
        scores = dot(keys, masked, NT) - slopes[pair * heads + h] * dist[...]
        peak = jnp.max(scores, axis=0, keepdims=True)
        expo = jnp.exp(scores - peak)
        probs = expo * (1.0 / jnp.sum(expo, axis=0, keepdims=True))
        grad_probs = dot(values, masked_grad, NT)
        inner = jnp.sum(probs * grad_probs, axis=0, keepdims=True)
        grad_scores = (probs * (grad_probs - inner)).astype(low)
        grad_v = grad_v + dot(probs.astype(low), masked_grad, NN)
        grad_k = grad_k + dot(grad_scores, masked, NN)
        grad_q = jnp.where(head_rows == h, dot(keys, grad_scores, TN), grad_q)
    dq[0] = (jnp.transpose(grad_q) * scale).astype(low)
    dk[0] = grad_k.astype(low)
    dv[0] = grad_v.astype(low)


def by_shard(array):
    return pl.BlockSpec((1,) + array.shape[1:], lambda p: (p, 0, 0))


def attend(slopes, dist, q, k, v):
    heads = slopes.shape[0] // q.shape[0]
    return pl.pallas_call(
        functools.partial(attend_kernel, heads),
        grid=(q.shape[0],),
        out_shape=jax.ShapeDtypeStruct(q.shape, jnp.bfloat16),
        in_specs=[pl.BlockSpec(memory_space=pltpu.SMEM), pl.BlockSpec(dist.shape, lambda p: (0, 0))]
        + [by_shard(a) for a in (q, k, v)],
        out_specs=by_shard(q),
        compiler_params=pltpu.CompilerParams(vmem_limit_bytes=50 * 2**20),
        name="attend",
    )(slopes, dist, q, k, v)


def attend_pull(slopes, dist, q, k, v, g):
    heads = slopes.shape[0] // q.shape[0]
    return pl.pallas_call(
        functools.partial(attend_pull_kernel, heads),
        grid=(q.shape[0],),
        out_shape=[jax.ShapeDtypeStruct(a.shape, jnp.bfloat16) for a in (q, k, v)],
        in_specs=[pl.BlockSpec(memory_space=pltpu.SMEM), pl.BlockSpec(dist.shape, lambda p: (0, 0))]
        + [by_shard(a) for a in (q, k, v, g)],
        out_specs=[by_shard(a) for a in (q, k, v)],
        compiler_params=pltpu.CompilerParams(vmem_limit_bytes=50 * 2**20),
        name="attend_pull",
    )(slopes, dist, q, k, v, g)


norm_eps = 1e-05


def normalized(values):
    offset = values - jnp.mean(values, axis=-1, keepdims=True)
    rate = lax.rsqrt(jnp.mean(offset * offset, axis=-1, keepdims=True) + norm_eps)
    return offset * rate, rate


def norm_input_term(xhat, rate, gain, grad):
    e = grad * gain
    return rate * (e - jnp.mean(e, axis=-1, keepdims=True) - xhat * jnp.mean(e * xhat, axis=-1, keepdims=True))


def gelu_and_slope(u):
    c, a = 0.7978845608028654, 0.044715
    th = jnp.tanh(c * (u + a * u * u * u))
    slope = 0.5 * (1.0 + th) + 0.5 * u * (1.0 - th * th) * (c * (1.0 + 3.0 * a * u * u))
    return 0.5 * u * (1.0 + th), slope


far_off = 1e33
longest = 512


def per_device(
    tokens, segment_ids, first_gain, first_shift, qkv_weight, qv_bias, out_weight, out_bias, second_gain, second_shift,
    up_weight, up_bias, down_weight, down_bias, cotangent,
):
    low, f32 = jnp.bfloat16, jnp.float32
    nt = lax.axis_size("tensor")
    lines, wide = grid_of(nt)
    t = lax.axis_index("tensor")
    z, y = t // wide, t % wide
    length, d = tokens.shape
    chunk = length // nt
    halo = -(-(longest - 1) // chunk)
    behind = halo * chunk
    span = behind + chunk
    heads_here, width = qkv_weight.shape[1], qkv_weight.shape[2] // 3
    lanes = heads_here * width
    hidden_here = up_weight.shape[1]

    qkv_own = qkv_weight.reshape(d, heads_here, 3, width).transpose(0, 2, 1, 3).reshape(d, 3 * lanes)
    bias_own = qv_bias.reshape(heads_here, 2, width).transpose(1, 0, 2).reshape(2 * lanes)
    small = jnp.concatenate([bias_own, up_bias])
    small = jnp.concatenate([small, jnp.zeros((64 * 128 - small.shape[0],), low)]).reshape(64, 128)
    qkv_all, out_all, small_all, up_all, down_all = gather_weights(
        nt, [qkv_own, out_weight, small], [up_weight, down_weight]
    )
    small_all = small_all.reshape(nt, 64 * 128).astype(f32)
    q_bias, v_bias = small_all[:, :lanes], small_all[:, lanes : 2 * lanes]
    up_bias_all = lax.dynamic_index_in_dim(
        small_all[:, 2 * lanes : 2 * lanes + hidden_here].reshape(lines, wide, hidden_here), y, 1, keepdims=False
    )

    padded = jnp.concatenate([jnp.zeros((behind, d), low), tokens])
    near = lax.dynamic_slice_in_dim(padded, t * chunk, span, 0).astype(f32)
    seg_row = jnp.concatenate([jnp.full((behind,), -1, jnp.int32), segment_ids[0]])
    seg_near = lax.dynamic_slice_in_dim(seg_row, t * chunk, span, 0)
    seg_mine = seg_near[behind:]
    distance = (behind + jnp.arange(chunk)[:, None]) - jnp.arange(span)[None, :]
    allowed = (seg_mine[:, None] == seg_near[None, :]) & (distance >= 0)
    dist = jnp.where(allowed, distance.astype(f32), far_off)
    total_heads = heads_here * nt
    slopes = jnp.exp2(-8.0 * (jnp.arange(total_heads, dtype=jnp.int32) + 1).astype(f32) / total_heads)

    gain1, shift1 = first_gain.astype(f32), first_shift.astype(f32)
    gain2, shift2 = second_gain.astype(f32), second_shift.astype(f32)
    xhat1, rate1 = normalized(near)
    normed = (xhat1 * gain1 + shift1).astype(low)
    mine = normed[behind:]
    query = (jnp.einsum("td,gde->gte", mine, qkv_all[:, :, :lanes], preferred_element_type=f32) + q_bias[:, None]).astype(low)
    keys = jnp.einsum("td,gde->gte", normed, qkv_all[:, :, lanes : 2 * lanes], preferred_element_type=f32).astype(low)
    values = (
        jnp.einsum("td,gde->gte", normed, qkv_all[:, :, 2 * lanes :], preferred_element_type=f32) + v_bias[:, None]
    ).astype(low)
    context = attend(slopes, dist, query, keys, values)
    context = context.transpose(1, 0, 2).reshape(chunk, d)
    out_full = out_all.reshape(d, d)
    mixed = jnp.dot(context, out_full, preferred_element_type=f32)
    middle = near[behind:] + mixed + out_bias.astype(f32)
    xhat2, rate2 = normalized(middle)
    second = (xhat2 * gain2 + shift2).astype(low)

    second_pair = group_exchange(nt, second, False, 3, "share_second").reshape(wide * chunk, d)
    cot_pair = lax.dynamic_slice_in_dim(cotangent, z * (wide * chunk), wide * chunk, 0)
    upper = jnp.einsum("td,zdf->ztf", second_pair, up_all, preferred_element_type=f32) + up_bias_all[:, None]
    hidden, slope = gelu_and_slope(upper)
    hidden = hidden.astype(low)
    feed_part = jnp.einsum("ztf,zfd->td", hidden, down_all, preferred_element_type=f32)
    grad_hidden = jnp.einsum("td,zfd->ztf", cot_pair, down_all, preferred_element_type=f32)
    grad_upper = (grad_hidden * slope).astype(low)
    grad_up_bias = jnp.sum(grad_upper.astype(f32), axis=1)
    grad_down = jnp.einsum("ztf,td->zfd", hidden, cot_pair, preferred_element_type=f32).astype(low)
    grad_up = jnp.einsum("td,ztf->zdf", second_pair, grad_upper, preferred_element_type=f32).astype(low)
    second_part = jnp.einsum("ztf,zdf->td", grad_upper, up_all, preferred_element_type=f32)
    parts = jnp.stack([second_part.reshape(wide, chunk, d), feed_part.reshape(wide, chunk, d)], axis=1).astype(low)
    sums = jnp.sum(group_exchange(nt, parts, True, 4, "sum_parts").astype(f32), axis=0)
    grad_second, feed = sums[0], sums[1]
    output_mine = (middle + feed + down_bias.astype(f32)).astype(low)

    cot_mine = lax.dynamic_slice_in_dim(cotangent, t * chunk, chunk, 0).astype(f32)
    grad_middle = cot_mine + norm_input_term(xhat2, rate2, gain2, grad_second)
    grad_middle_low = grad_middle.astype(low)
    grad_out = jnp.dot(context.T, grad_middle_low, preferred_element_type=f32).astype(low).reshape(out_all.shape)
    grad_context = jnp.einsum("td,gcd->gtc", grad_middle_low, out_all, preferred_element_type=f32).astype(low)
    grad_q, grad_k, grad_v = attend_pull(slopes, dist.T, query, keys, values, grad_context)
    grad_kv = jnp.concatenate([grad_k, grad_v], axis=2)
    grad_qkv = jnp.concatenate(
        [
            jnp.einsum("td,gte->gde", mine, grad_q, preferred_element_type=f32),
            jnp.einsum("td,gte->gde", normed, grad_kv, preferred_element_type=f32),
        ],
        axis=2,
    ).astype(low)
    first_part = jnp.einsum("gte,gde->td", grad_kv, qkv_all[:, :, lanes:], preferred_element_type=f32)
    first_mine = first_part[behind:] + jnp.einsum("gte,gde->td", grad_q, qkv_all[:, :, :lanes], preferred_element_type=f32)
    got = halo_exchange(nt, first_part[:behind].astype(low).reshape(halo, chunk, d)).astype(f32)
    there = (t + 1 + jnp.arange(halo)) < nt
    grad_first = first_mine + jnp.sum(jnp.where(there[:, None, None], got, 0.0), axis=0)
    xhat_mine = xhat1[behind:]
    grad_tokens = (grad_middle + norm_input_term(xhat_mine, rate1[behind:], gain1, grad_first)).astype(low)

    g_qkv, g_out, g_up, g_down = reduce_weights(nt, [grad_qkv, grad_out], [grad_up, grad_down])
    output_all, grad_tokens_all = gather_rows(nt, [output_mine, grad_tokens], 5)

    def rows_sum(v):
        return jnp.sum(v, axis=0)

    up_slots = jnp.where(jnp.arange(wide)[None, :, None] == y, grad_up_bias[:, None, :], 0.0)
    q_sum, v_sum = jnp.sum(grad_q.astype(f32), axis=1), jnp.sum(grad_v.astype(f32), axis=1)
    vectors = jnp.concatenate(
        [
            rows_sum(grad_first * xhat_mine), rows_sum(grad_first), rows_sum(grad_middle),
            rows_sum(grad_second * xhat2), rows_sum(grad_second), rows_sum(cot_mine),
            q_sum.reshape(-1), v_sum.reshape(-1), up_slots.reshape(-1),
        ]
    )
    vectors = lax.psum(vectors, ("dp", "tensor"))
    g_first_gain, g_first_shift, g_out_bias, g_second_gain, g_second_shift, g_down_bias = (
        vectors[i * d : (i + 1) * d] for i in range(6)
    )
    rest = vectors[6 * d :]
    g_q = lax.dynamic_index_in_dim(rest[:d].reshape(nt, heads_here, width), t, 0, keepdims=False)
    g_v = lax.dynamic_index_in_dim(rest[d : 2 * d].reshape(nt, heads_here, width), t, 0, keepdims=False)
    g_up_bias = lax.dynamic_index_in_dim(rest[2 * d :].reshape(nt, hidden_here), t, 0, keepdims=False)
    g_qkv = g_qkv.astype(f32).reshape(d, 3, heads_here, width).transpose(0, 2, 1, 3).reshape(d, heads_here, 3 * width)
    return (
        output_all.reshape(length, d), grad_tokens_all.reshape(length, d), g_first_gain, g_first_shift, g_qkv,
        jnp.concatenate([g_q, g_v], axis=1), g_out.astype(f32), g_out_bias, g_second_gain, g_second_shift,
        g_up.astype(f32), g_up_bias, g_down.astype(f32), g_down_bias,
    )


def solution(mesh):
    rows, cols, both = P("dp", None), P(None, "tensor"), P("tensor", None)
    return jax.shard_map(
        per_device,
        mesh=mesh,
        in_specs=(
            rows, rows, P(), P(), P(None, "tensor", None), both, both, P(), P(), P(), cols, P("tensor"), both, P(), rows,
        ),
        out_specs=(
            rows, rows, P(), P(), P(None, "tensor", None), both, both, P(), P(), P(), cols, P("tensor"), both, P(),
        ),
        check_vma=False,
    )
```

time: 964 us -> 632 us (0.66)
  waiting for transfers between devices: 617 us -> 0 us
  Pallas kernels: 0 us -> 465 us
  other arithmetic: 146 us -> 30.1 us
  matrix products: 134 us -> 63.4 us
  blocking collectives: 10.8 us -> 39.9 us
  loops' own time: 14.3 us -> 0 us
  between operations: 14.6 us -> 1.88 us
    psum x4 -> x0, waiting for transfers between devices: 617 us -> none  [the longest x1 266 us: per_device(): feed = lax.psum(part_down, 'tensor').astype(jnp.float32)]
    pallas_call x0 -> x8, Pallas kernels: none -> 465 us  [the longest x1 162 us: reduce_weights(): pl.pallas_call(functools.partial(reduce_kernel, n_tensor, len(attn), len(...]
    dot_general x38 -> x16, matrix products: 130 us -> 63.4 us  [the longest x1 8.44 us: per_device(): jnp.einsum('td,zfd->ztf', cot_pair, down_all, preferred_element_type=f32)]
    convert_element_type x36 -> x12, other arithmetic: 71.1 us -> 9.29 us  [the longest x1 2.92 us: per_device(): g_up.astype(f32)]
    reduce_sum x18 -> x10, other arithmetic: 65.2 us -> 10.7 us  [the longest x3 3.81 us: rows_sum(): return jnp.sum(v, axis=0)]
    psum x1, blocking collectives: 10.8 us -> 39.9 us  [per_device(): vectors = lax.psum(vectors, ('dp', 'tensor'))]
    another operation x2 -> x0, loops' own time: 14.3 us -> none  [the longest x1 11.2 us: attend_backward(): lax.scan(one_block, (empty, empty), jnp.arange(length // block, dtype=jnp...]
  transfers between devices with their start and end apart: 4 -> 0, of which waited for: 4 -> 0; matrix products, arithmetic and copies ran while one was open for 4% -> 0% of each run, Pallas kernels for 0% -> 0%
where the time goes in v2:
time: 632 us; the launch traced here: 623 us
  Pallas kernels  465 us (74%)
  matrix products  63.4 us (10%)
  blocking collectives  39.9 us (6%)
  other arithmetic  30.1 us (5%)
  local copies, waits for them, and re-layouts  22.5 us (4%)
    pallas_call x1, Pallas kernels, reduce_weights(): pl.pallas_call(functools.partial(reduce_kernel, n_tensor, len(attn), len(...  162 us
    pallas_call x1, Pallas kernels, gather_weights(): pl.pallas_call(functools.partial(gather_kernel, n_tensor, len(attn), len(...  104 us
    pallas_call x1, Pallas kernels, gather_rows(): pl.pallas_call(functools.partial(rows_kernel, n_tensor, n), out_shape=[ja...  93.8 us
    pallas_call x2, Pallas kernels, group_exchange(): pl.pallas_call(functools.partial(group_kernel, n_tensor, scatter), out_sh...  52 us
    psum x1, blocking collectives, per_device(): vectors = lax.psum(vectors, ('dp', 'tensor'))  39.9 us
    pallas_call x1, Pallas kernels, halo_exchange(): pl.pallas_call(functools.partial(halo_kernel, n_tensor, halo), out_shape=...  26.1 us
    pallas_call x1, Pallas kernels, attend_pull(): pl.pallas_call(functools.partial(attend_pull_kernel, heads), grid=(q.shap...  16.9 us
    unnamed x84, local copies, waits for them, and re-layouts  15.1 us

profile of v2, /device:TPU:0, one launch (start us, length us, event | category | flops | bytes accessed | tf_op | source)
XLA Modules:
  0.0 623.0 jit_solution(3574014590221486759)
XLA Ops:
  0.7 1.6 convert_reduce_fusion.3
  2.2 0.7 copy-done.1
  3.0 0.6 multiply_reduce_fusion
  3.7 2.3 subtract_multiply_fusion
  6.1 1.3 copy.65.refs_0_
  7.6 0.6 maximum_bitcast_fusion.refs_2_
  8.2 104.4 %gather_weights.1 = (bf16[8,1024,384]{2,1,0:T(8,128)(2,1)}, bf16[8,128,1024]{2,1,0:T(8,128)(2,1)}, bf16[8,64,128]{2,1,0:T(8,128)(2,1)}, bf16[4,1024,512]{2,1,0:T(8,128)(2,1)}, bf16[4,512,1024]{2,1,0:T(8,128)(2,1)}) custom-call(bf16[1024,384]{1,0:T(8,128)(2,1)} %copy.65.refs_0_, bf16[128,1024]{1,0:T(8,128)(2,1)} %refs_1_.1, ...), custom_call_target="tpu_custom_call" | custom-call | tf_op jit(solution)/shard_map/gather_weights/pallas_call | solution.py:207
  112.7 0.9 convert_bitcast_fusion.3
  113.8 4.7 fusion.24.v
  118.5 1.9 fusion.54.q
  120.4 1.8 fusion.32.k
  122.3 0.2 convert_select_fusion.1.dist
  122.6 10.1 %attend.1 = bf16[8,256,128]{2,1,0:T(8,128)(2,1)S(1)} custom-call(f32[16]{0:T(128)S(1)} %multiply_exponential_fusion.slopes, f32[256,768]{1,0:T(8,128)S(1)} %convert_select_fusion.1.dist, bf16[8,256,128]{2,1,0:T(8,128)(2,1)S(1)} %fusion.54.q, bf16[8,768,128]{2,1,0:T(8,128)(2,1)S(1)} %fusion.32.k, bf16[8,768,128]{2,1,0:T(8,128)(2,1)} %fusion.24.v), custom_call_target="tpu_custom_call" | custom-call | tf_op jit(solution)/shard_map/attend/pallas_call | solution.py:671
  132.7 0.6 fusion.79
  133.4 0.9 copy-done.5
  134.3 0.8 fusion.83
  135.1 0.3 multiply_reduce_fusion.4
  135.4 1.0 add_convert_fusion.3.own
  136.5 18.5 %share_second.1 = bf16[2,256,1024]{2,1,0:T(8,128)(2,1)} custom-call(bf16[256,1024]{1,0:T(8,128)(2,1)} %add_convert_fusion.3.own), custom_call_target="tpu_custom_call" | custom-call | tf_op jit(solution)/shard_map/share_second/pallas_call | solution.py:465
  155.0 6.9 %fusion.84 = f32[4,512,512]{1,2,0:T(8,128)} fusion(bf16[512,1024,1]{1,0,2:T(8,128)(2,1)} %bitcast.166, bf16[4,1024,512]{2,1,0:T(8,128)(2,1)} %get-tuple-element.32), kind=kOutput, calls=%fused_computation.141 | convolution fusion | flops 2147483648 | bytes 9437184 | tf_op jit(solution)/shard_map/td,zdf->ztf/dot_general | solution.py:784
  162.0 8.4 %convert_reduce_fusion = (f32[4,512]{1,0:T(4,128)S(1)}, bf16[4,512,512]{2,1,0:T(8,128)(2,1)S(1)}) fusion(f32[4,512,512]{1,2,0:T(8,128)} %fusion.84, f32[4,512]{1,0:T(4,128)S(1)} %bitcast.177, bf16[4,512,1024]{2,1,0:T(8,128)(2,1)} %get-tuple-element.31, bf16[2048,1024]{1,0:T(8,128)(2,1)} %param.29, s32[]{:T(128)S(6)} %select_n.53), kind=kOutput, calls=%fused_computation.15 | convolution fusion | flops 2170550272 | bytes 11550724 | tf_op jit(solution)/shard_map/td,zfd->ztf/dot_general | solution.py:788
  170.5 2.4 bitcast_convert_fusion.1
  172.8 0.6 copy-done.27
  173.4 1.3 copy-done.30
  174.6 2.8 bitcast_convert_fusion
  177.4 1.5 pad_maximum_fusion.1.own
  178.9 33.4 %sum_parts.1 = bf16[2,2,256,1024]{3,2,1,0:T(8,128)(2,1)} custom-call(bf16[2,2,256,1024]{3,2,1,0:T(8,128)(2,1)} %pad_maximum_fusion.1.own), custom_call_target="tpu_custom_call" | custom-call | tf_op jit(solution)/shard_map/sum_parts/pallas_call | solution.py:465
  212.4 2.3 convert_reduce_fusion.1
  214.7 1.3 copy-done.3
  216.1 0.5 fusion.61
  216.6 3.2 fusion.80
  219.8 0.8 fusion.57.g
  220.8 16.9 %attend_pull.1 = (bf16[8,256,128]{2,1,0:T(8,128)(2,1)S(1)}, bf16[8,768,128]{2,1,0:T(8,128)(2,1)S(1)}, bf16[8,768,128]{2,1,0:T(8,128)(2,1)}) custom-call(f32[16]{0:T(128)S(1)} %multiply_exponential_fusion.slopes, f32[768,256]{1,0:T(8,128)S(1)} %convert_select_fusion.dist, bf16[8,256,128]{2,1,0:T(8,128)(2,1)S(1)} %fusion.54.q, bf16[8,768,128]{2,1,0:T(8,128)(2,1)} %copy-done, ...), custom_call_target="tpu_custom_call" | custom-call | tf_op jit(solution)/shard_map/attend_pull/pallas_call | solution.py:685
  237.7 0.3 constant_dynamic-update-slice_fusion.1
  238.0 1.1 copy-done.7
  239.1 0.4 constant_dynamic-update-slice_fusion
  239.5 6.4 %fusion.14 = f32[768,1024]{1,0:T(8,128)S(1)} fusion(bf16[8,768,256]{2,1,0:T(8,128)(2,1)S(1)} %constant_dynamic-update-slice_fusion, bf16[8,1024,384]{2,1,0:T(8,128)(2,1)} %get-tuple-element.28), kind=kOutput, calls=%fused_computation.37 | convolution fusion | flops 3221225472 | bytes 10485760 | tf_op jit(solution)/shard_map/gte,gde->td/dot_general | solution.py:813
  245.9 1.7 copy-done.13
  247.6 1.2 slice.204
  248.7 26.1 %halo_exchange.1 = bf16[2,256,1024]{2,1,0:T(8,128)(2,1)} custom-call(bf16[2,256,1024]{2,1,0:T(8,128)(2,1)} %bitcast.162), custom_call_target="tpu_custom_call" | custom-call | tf_op jit(solution)/shard_map/halo_exchange/pallas_call | solution.py:504
  274.9 1.9 select_reduce_fusion
  276.8 4.2 multiply_reduce_fusion.1
  281.2 0.2 convert_reduce_fusion.2
  281.6 39.9 %psum.7 = f32[12288]{0:T(1024)S(1)} all-reduce(f32[12288]{0:T(1024)S(1)} %constant_dynamic-update-slice_fusion.3), channel_id=1, replica_groups=mesh['dp'=4,'tensor'=8] {'dp','tensor'}, use_global_device_ids=true, to_apply=%region_19.20 | all-reduce | flops 12288 | bytes 98304 | tf_op jit(solution)/shard_map/psum | solution.py:836
  321.5 0.6 fusion.82
  322.3 0.6 pad_maximum_fusion.2
  322.9 5.8 convert_bitcast_fusion.1
  328.8 1.8 convert_bitcast_fusion.2
  330.6 3.5 pad_maximum_fusion.refs_0_
  334.1 0.2 copy.77
  334.3 2.0 convolution_convert_fusion.1
  336.3 6.2 convert_bitcast_fusion.refs_2_
  342.5 6.5 %convolution_convert_fusion.refs_3_ = bf16[4,512,1024]{2,1,0:T(8,128)(2,1)} fusion(bf16[2048,1024]{1,0:T(8,128)(2,1)} %param.29, s32[]{:T(128)S(6)} %select_n.53, f32[4,512,512]{1,2,0:T(8,128)S(1)} %copy-done.31, f32[4,512]{1,0:T(4,128)S(1)} %bitcast.179), kind=kOutput, calls=%fused_computation.25 | convolution fusion | flops 2160066560 | bytes 9445380 | tf_op jit(solution)/shard_map/ztf,td->zfd/dot_general | solution.py:791
  349.0 162.0 %reduce_weights.1 = (bf16[1024,384]{1,0:T(8,128)(2,1)}, bf16[128,1024]{1,0:T(8,128)(2,1)}, bf16[1024,512]{1,0:T(8,128)(2,1)}, bf16[512,1024]{1,0:T(8,128)(2,1)}) custom-call(bf16[8,1024,384]{2,1,0:T(8,128)(2,1)} %pad_maximum_fusion.refs_0_, bf16[8,128,1024]{2,1,0:T(8,128)(2,1)} %bitcast.158, bf16[4,1024,512]{2,1,0:T(8,128)(2,1)} %convert_bitcast_fusion.refs_2_, ...), custom_call_target="tpu_custom_call" | custom-call | tf_op jit(solution)/shard_map/reduce_weights/pallas_call | solution.py:421
  511.0 1.4 copy.81
  512.5 1.2 copy.82
  513.7 2.9 convert_element_type.159
  516.7 1.6 convert_element_type.160
  518.2 0.8 convert_element_type.158
  519.1 0.6 constant_dynamic-slice_fusion
  519.7 2.3 add_convert_fusion.2.refs_1_
  522.0 93.8 %gather_rows.1 = (bf16[8,256,1024]{2,1,0:T(8,128)(2,1)}, bf16[8,256,1024]{2,1,0:T(8,128)(2,1)}) custom-call(bf16[256,1024]{1,0:T(8,128)(2,1)} %get-tuple-element.54.refs_0_, bf16[256,1024]{1,0:T(8,128)(2,1)} %add_convert_fusion.2.refs_1_), custom_call_target="tpu_custom_call" | custom-call | tf_op jit(solution)/shard_map/gather_rows/pallas_call | solution.py:596
  615.8 4.8 copy.117
  620.6 2.0 copy.118
  (115 shorter events, 1.4 us)
Async XLA Ops:
  0.6 2.3 copy-start.1
  0.7 2.9 copy-start.20
  0.7 3.0 copy-start.21
  3.6 2.4 copy-start.17
  3.7 3.8 copy-start.29
  3.7 3.9 copy-start.26
  6.0 112.4 %copy-start.11 = (bf16[768,1024]{1,0:T(8,128)(2,1)}, bf16[768,1024]{1,0:T(8,128)(2,1)S(1)}, u32[]{:S(2)}) copy-start(bf16[768,1024]{1,0:T(8,128)(2,1)S(1)} %get-tuple-element.52) | copy-start | bytes 4718596
  113.6 4.9 slice-start
  113.8 4.7 slice-start.1
  118.5 1.9 copy-start.12
  120.4 1.8 copy-start.19
  122.2 11.2 %copy-start = (bf16[8,768,128]{2,1,0:T(8,128)(2,1)}, bf16[8,768,128]{2,1,0:T(8,128)(2,1)S(1)}, u32[]{:S(2)}) copy-start(bf16[8,768,128]{2,1,0:T(8,128)(2,1)S(1)} %fusion.32.k) | copy-start | bytes 4718596
  122.2 10.5 %copy-start.2 = (bf16[2048,1024]{1,0:T(8,128)(2,1)S(1)}, bf16[2048,1024]{1,0:T(8,128)(2,1)}, u32[]{:S(2)}) copy-start(bf16[2048,1024]{1,0:T(8,128)(2,1)} %param.15) | copy-start | bytes 12582916
  132.7 0.7 copy-start.22
  132.7 1.6 copy-start.5
  133.3 2.1 copy-start.23
  133.4 2.1 copy-start.24
  162.0 8.5 %copy-start.28 = (bf16[4,1024,512]{2,1,0:T(8,128)(2,1)S(1)}, bf16[4,1024,512]{2,1,0:T(8,128)(2,1)}, u32[]{:S(2)}) copy-start(bf16[4,1024,512]{2,1,0:T(8,128)(2,1)} %get-tuple-element.32) | copy-start | bytes 12582916
  170.4 2.4 copy-start.32
  170.4 2.9 copy-start.27
  170.4 4.2 copy-start.30
  212.4 4.2 copy-start.25
  214.7 1.3 copy-start.3
  216.6 3.2 copy-start.6
  237.7 1.4 copy-start.7
  239.5 6.4 %copy-start.16 = (bf16[8,768,256]{2,1,0:T(8,128)(2,1)}, bf16[8,768,256]{2,1,0:T(8,128)(2,1)S(1)}, u32[]{:S(2)}) copy-start(bf16[8,768,256]{2,1,0:T(8,128)(2,1)S(1)} %constant_dynamic-update-slice_fusion) | copy-start | bytes 9437188
  245.9 1.7 copy-start.13
  274.9 6.2 copy-start.4
  276.8 4.5 copy-start.8
  334.1 2.3 copy-start.15
  336.3 6.2 copy-start.31
  512.5 4.2 copy-start.14
  512.5 5.8 copy-start.18
  513.7 6.0 copy-start.10
  615.8 4.8 copy-start.9

commit v3 on v2

--- a/solution.py
+++ b/solution.py
@@ -22,6 +22,16 @@
     lines, wide = grid_of(n_tensor)
     dp, t = lax.axis_index("dp"), lax.axis_index("tensor")
     return dp, t, t // wide, t % wide
+
+
+def remote(src, dst, send, recv, peer):
+    return pltpu.make_async_remote_copy(
+        src_ref=src, dst_ref=dst, send_sem=send, recv_sem=recv, device_id=peer, device_id_type=MESH
+    )
+
+
+def when(condition, body):
+    pl.when(condition)(body)
 
 
 def greet(peers):
@@ -232,25 +242,68 @@
         dst[part] = total.astype(dst.dtype)
 
 
-def reduce_kernel(n_tensor, n_attn, n_mlp, *refs):
+def doubling_peers(n_tensor):
+    dp, t, z, y = where_am_i(n_tensor)
+    bits = lambda size: [1 << i for i in range((size - 1).bit_length())]
+    return [(dp ^ b, t) for b in bits(lax.axis_size("dp"))] + [(dp, t ^ b) for b in bits(n_tensor)]
+
+
+def doubling_program(n_tensor, own, out, total, got, send, recv):
+    peers = doubling_peers(n_tensor)
+
+    def step(i):
+        return remote(total.at[i], got.at[i], send.at[i], recv.at[i], peers[i])
+
+    def begin():
+        total[0] = own[...]
+        step(0).start()
+
+    def advance(i):
+        step(i).wait_recv()
+        if i + 1 < len(peers):
+            total[i + 1] = total[i] + got[i]
+            step(i + 1).start()
+        else:
+            out[...] = total[i] + got[i]
+
+    def settle():
+        for i in range(len(peers)):
+            step(i).wait_send()
+
+    return [begin] + [functools.partial(advance, i) for i in range(len(peers))] + [settle]
+
+
+def finish_kernel(n_tensor, n_attn, n_mlp, with_feed, with_vectors, *refs):
     lines, wide = grid_of(n_tensor)
     dp, t, z, y = where_am_i(n_tensor)
     n = n_attn + n_mlp
-    terms, final = refs[:n], refs[n : 2 * n]
-    from_c, from_x, to_x, acc, from_y, from_z = (refs[(2 + i) * n : (3 + i) * n] for i in range(6))
-    c_send, c_recv, x_send, x_recv, y_send, y_recv, z_send, z_recv, q_send, q_recv = refs[8 * n :]
+    refs = list(refs)
+
+    def take(count):
+        got, refs[:] = refs[:count], refs[count:]
+        return got
+
+    terms, rows_own = take(n), take(1)
+    feed_base = take(1)[0] if with_feed else None
+    vec_own = take(1)[0] if with_vectors else None
+    final, rows_full = take(n), take(1)
+    vec_out = take(1)[0] if with_vectors else None
+    from_c, from_x, to_x, acc, from_y, from_z = (take(n) for i in range(6))
+    c_send, c_recv, x_send, x_recv, y_send, y_recv, z_send, z_recv, q_send, q_recv = take(10)
+    rows_sems = take(5)
+    if with_feed:
+        feed_parts, (feed_got, feed_sum), (f_send, f_recv) = rows_own[0], take(2), take(2)
+        rows_own = [feed_sum]
+    rows_steps = rows_program(n_tensor, rows_own, rows_full, *rows_sems)
+    vec_steps = doubling_program(n_tensor, vec_own, vec_out, *take(4)) if with_vectors else []
     quad = dp % 4
     side_x = quad // 2
     core = quad % 2
     core_peer, x_peer = (dp ^ 1, t), (dp ^ 2, t)
 
-    def copy(src, dst, send, recv, peer):
-        return pltpu.make_async_remote_copy(
-            src_ref=src, dst_ref=dst, send_sem=send, recv_sem=recv, device_id=peer, device_id_type=MESH
-        )
-
     def slots(a):
-        return [(zz, yy) for zz in range(lines) for yy in (range(wide) if a < n_attn else [0])]
+        order = [0, lines - 1] + list(range(1, lines - 1))
+        return [(zz, yy) for zz in order for yy in (range(wide) if a < n_attn else [0])]
 
     def index(a, zz, yy):
         return zz * wide + yy if a < n_attn else zz
@@ -259,91 +312,142 @@
         rows = final[a].shape[0] // 4
         return ref.at[pl.ds(pl.multiple_of(q * rows, rows), rows)]
 
-    greet(neighbours(n_tensor))
-
     def c_copy(a, s, h):
-        return copy(
+        return remote(
             quarter(terms[a].at[s], a, h * 2 + 1 - core), from_c[a].at[s, h], c_send.at[a, s, h], c_recv.at[a, s, h],
             core_peer,
         )
 
     def x_copy(a, s):
-        return copy(to_x[a].at[s], from_x[a].at[s], x_send.at[a, s], x_recv.at[a, s], x_peer)
+        return remote(to_x[a].at[s], from_x[a].at[s], x_send.at[a, s], x_recv.at[a, s], x_peer)
 
     def y_copy(a, zz, yy, side):
         peer = ((dp, t + 1), (dp, t - 1))[side]
-        return copy(
-            acc[a].at[index(a, zz, yy)], from_y[a].at[side, zz * wide + yy], y_send.at[side, a, zz * wide + yy],
-            y_recv.at[side, a, zz * wide + yy], peer,
-        )
+        lane = zz * wide + yy
+        return remote(acc[a].at[lane], from_y[a].at[side, lane], y_send.at[side, a, lane], y_recv.at[side, a, lane], peer)
 
     def z_copy(a, zz, side):
         peer = ((dp, t + wide), (dp, t - wide))[side]
-        return copy(
+        return remote(
             acc[a].at[index(a, zz, y)], from_z[a].at[side, zz], z_send.at[side, a, zz], z_recv.at[side, a, zz], peer
         )
 
-    order = list(range(n_attn, n)) + list(range(n_attn))
+    def core_stage(a, zz, yy):
+        s = index(a, zz, yy)
+        for h in range(2):
+            c_copy(a, s, h).wait_recv()
+        add_rows(to_x[a].at[s], [quarter(terms[a].at[s], a, (1 - side_x) * 2 + core), from_c[a].at[s, 1 - side_x]])
+        x_copy(a, s).start()
+        add_rows(acc[a].at[s], [quarter(terms[a].at[s], a, quad), from_c[a].at[s, side_x]])
+
+    def x_stage(a, zz, yy):
+        s = index(a, zz, yy)
+        x_copy(a, s).wait_recv()
+        add_rows(acc[a].at[s], [acc[a].at[s], from_x[a].at[s]])
+        if a < n_attn:
+            when((y == 0) & (yy > y), lambda: y_copy(a, zz, yy, 0).start())
+            when((y == wide - 1) & (yy < y), lambda: y_copy(a, zz, yy, 1).start())
+
+    def y_stage(a, zz):
+        for k in range(wide):
+            for side, yy in ((0, wide - 1 - k), (1, k)):
+                @pl.when(((yy >= y) & (y > 0)) if side == 0 else ((yy <= y) & (y < wide - 1)))
+                def _():
+                    lane = zz * wide + yy
+                    y_copy(a, zz, yy, side).wait_recv()
+                    add_rows(acc[a].at[lane], [acc[a].at[lane], from_y[a].at[side, lane]])
+                    when(yy != y, lambda: y_copy(a, zz, yy, side).start())
+
+    def z_stage(a, zz):
+        for side in range(2):
+            @pl.when((z <= zz) if side == 0 else (z >= zz))
+            def _():
+                @pl.when((z > 0) if side == 0 else (z < lines - 1))
+                def _():
+                    s = index(a, zz, y)
+                    z_copy(a, zz, side).wait_recv()
+                    add_rows(acc[a].at[s], [acc[a].at[s], from_z[a].at[side, zz]])
+
+                when(z != zz, lambda: z_copy(a, zz, side).start())
+
+    def q_copy(a, q, hop, peer):
+        return remote(quarter(final[a], a, q), quarter(final[a], a, q), q_send.at[hop, a], q_recv.at[hop, a], peer)
+
+    def home(a):
+        add_rows(quarter(final[a], a, quad), [acc[a].at[index(a, z, y)]])
+        q_copy(a, quad, 0, x_peer).start()
+        q_copy(a, quad, 1, core_peer).start()
+
+    def feed_copy(yy, slot):
+        return remote(feed_parts.at[yy], feed_got.at[slot], f_send.at[yy], f_recv.at[slot], (dp, z * wide + yy))
+
+    def feed_start():
+        for yy in range(wide):
+            when(yy != y, lambda: feed_copy(yy, y).start())
+
+    def feed_end():
+        feed_got[y] = jnp.zeros(feed_got.shape[1:], feed_got.dtype)
+        for yy in range(wide):
+            when(yy != y, lambda: feed_copy(yy, yy).wait_recv())
+        add_rows(feed_sum, [feed_base] + [feed_got.at[yy] for yy in range(wide)])
+        for yy in range(wide):
+            when(yy != y, lambda: feed_copy(yy, y).wait_send())
+
+    peers = neighbours(n_tensor)
+    if with_feed and wide > 2:
+        peers += [(yy != y, (dp, z * wide + yy)) for yy in range(wide)]
+    if with_vectors:
+        peers += [(dp >= 0, peer) for peer in doubling_peers(n_tensor)]
+    greet(peers)
+    attn, mlp = list(range(n_attn)), list(range(n_attn, n))
+    order = attn + mlp
+    lines_order = [0, lines - 1] + list(range(1, lines - 1))
+    if with_feed:
+        feed_start()
+    else:
+        rows_steps.pop(0)()
     for a in order:
         for zz, yy in slots(a):
             for h in range(2):
                 c_copy(a, index(a, zz, yy), h).start()
+    if with_vectors:
+        vec_steps.pop(0)()
+    for zz, yy in slots(0):
+        for a in order:
+            core_stage(a, zz, yy)
+    if with_feed:
+        feed_end()
+        rows_steps.pop(0)()
+
+    def aside():
+        if len(rows_steps) > 1:
+            rows_steps.pop(0)()
+        if len(vec_steps) > 1:
+            vec_steps.pop(0)()
+
+    for i in range(lines + 2):
+        if i < lines:
+            for a in order:
+                for yy in range(wide) if a < n_attn else [0]:
+                    x_stage(a, lines_order[i], yy)
+        if 0 <= i - 1 < lines:
+            for a in attn:
+                y_stage(a, lines_order[i - 1])
+        lag = 2 if n_attn else 1
+        if 0 <= i - lag < lines:
+            for a in order:
+                z_stage(a, lines_order[i - lag])
+        aside()
     for a in order:
-        for zz, yy in slots(a):
-            s = index(a, zz, yy)
-            for h in range(2):
-                c_copy(a, s, h).wait_recv()
-            add_rows(to_x[a].at[s], [quarter(terms[a].at[s], a, (1 - side_x) * 2 + core), from_c[a].at[s, 1 - side_x]])
-            x_copy(a, s).start()
-            add_rows(acc[a].at[s], [quarter(terms[a].at[s], a, quad), from_c[a].at[s, side_x]])
-    for a in order:
-        for zz, yy in slots(a):
-            s = index(a, zz, yy)
-            x_copy(a, s).wait_recv()
-            add_rows(acc[a].at[s], [acc[a].at[s], from_x[a].at[s]])
-
-            if a < n_attn:
-                @pl.when((y == 0) & (yy > y))
-                def _():
-                    y_copy(a, zz, yy, 0).start()
-
-                @pl.when((y == wide - 1) & (yy < y))
-                def _():
-                    y_copy(a, zz, yy, 1).start()
-        if a >= n_attn:
-            z_stage(a, lines, wide, z, y, z_copy, acc, from_z, index)
-    for a in range(n_attn):
-        for side in range(2):
-            for m in range(1, wide):
-                @pl.when((y >= 1) if side == 0 else (y < wide - 1))
-                def _():
-                    for zz in range(lines):
-                        for yy in range(wide):
-                            if m > 1:
-                                continue
-
-                            @pl.when((yy >= y) if side == 0 else (yy <= y))
-                            def _():
-                                s = index(a, zz, yy)
-                                y_copy(a, zz, yy, side).wait_recv()
-                                add_rows(acc[a].at[s], [acc[a].at[s], from_y[a].at[side, zz * wide + yy]])
-
-                                @pl.when(yy != y)
-                                def _():
-                                    y_copy(a, zz, yy, side).start()
-
-        z_stage(a, lines, wide, z, y, z_copy, acc, from_z, index)
-
-    def q_copy(a, q, hop, peer):
-        return copy(quarter(final[a], a, q), quarter(final[a], a, q), q_send.at[hop, a], q_recv.at[hop, a], peer)
-
-    for a in order:
-        add_rows(quarter(final[a], a, quad), [acc[a].at[index(a, z, y)]])
-        q_copy(a, quad, 0, x_peer).start()
-        q_copy(a, quad, 1, core_peer).start()
+        home(a)
+    aside()
     for a in order:
         q_copy(a, quad ^ 2, 0, x_peer).wait_recv()
         q_copy(a, quad ^ 2, 2, core_peer).start()
+    while rows_steps:
+        rows_steps.pop(0)()
+    while vec_steps:
+        vec_steps.pop(0)()
     for a in order:
         q_copy(a, quad ^ 1, 1, core_peer).wait_recv()
         q_copy(a, quad ^ 3, 2, core_peer).wait_recv()
@@ -356,80 +460,60 @@
                 c_copy(a, s, h).wait_send()
             x_copy(a, s).wait_send()
             if a < n_attn:
-                @pl.when((yy > y))
-                def _():
-                    y_copy(a, zz, yy, 0).wait_send()
-
-                @pl.when((yy < y))
-                def _():
-                    y_copy(a, zz, yy, 1).wait_send()
+                when(yy > y, lambda: y_copy(a, zz, yy, 0).wait_send())
+                when(yy < y, lambda: y_copy(a, zz, yy, 1).wait_send())
         for zz in range(lines):
-            @pl.when(zz > z)
-            def _():
-                z_copy(a, zz, 0).wait_send()
-
-            @pl.when(zz < z)
-            def _():
-                z_copy(a, zz, 1).wait_send()
-
-
-def z_stage(a, lines, wide, z, y, z_copy, acc, from_z, index):
-    for k in range(lines - 1):
-        far = lines - 1 - k
-        for side, zz in ((0, far), (1, k)):
-            @pl.when((z < zz) if side == 0 else (z > zz))
-            def _():
-                s = index(a, zz, y)
-
-                @pl.when((z > 0) if side == 0 else (z < lines - 1))
-                def _():
-                    z_copy(a, zz, side).wait_recv()
-                    add_rows(acc[a].at[s], [acc[a].at[s], from_z[a].at[side, zz]])
-
-                z_copy(a, zz, side).start()
-    s = index(a, z, y)
-    for side in range(2):
-        @pl.when((z > 0) if side == 0 else (z < lines - 1))
-        def _():
-            z_copy(a, z, side).wait_recv()
-            add_rows(acc[a].at[s], [acc[a].at[s], from_z[a].at[side, z]])
-
-
-def reduce_weights(n_tensor, attn, mlp):
+            when(zz > z, lambda: z_copy(a, zz, 0).wait_send())
+            when(zz < z, lambda: z_copy(a, zz, 1).wait_send())
+
+
+def finish(n_tensor, attn, mlp, rows, base, vectors, cid, name):
     lines, wide = grid_of(n_tensor)
     arrays = list(attn) + list(mlp)
     n = len(arrays)
     vm, dma = pltpu.VMEM, pltpu.SemaphoreType.DMA
     quarters = [(a.shape[1] // 4, a.shape[2]) for a in arrays]
-    outs = [jax.ShapeDtypeStruct(a.shape[1:], a.dtype) for a in arrays]
     low = jnp.bfloat16
+    each = lambda lead: [vm(lead(a, i) + q, low) for i, (a, q) in enumerate(zip(arrays, quarters))]
+    slots = lambda a, i: (a.shape[0],)
+    steps = (lax.axis_size("dp") - 1).bit_length() + (n_tensor - 1).bit_length()
     scratch = (
-        [vm((a.shape[0], 2) + q, low) for a, q in zip(arrays, quarters)]
-        + [vm((a.shape[0],) + q, low) for a, q in zip(arrays, quarters)]
-        + [vm((a.shape[0],) + q, low) for a, q in zip(arrays, quarters)]
-        + [vm((a.shape[0],) + q, low) for a, q in zip(arrays, quarters)]
-        + [vm(((2, n_tensor) if i < len(attn) else (1, 1)) + q, low) for i, q in enumerate(quarters)]
-        + [vm((2, lines) + q, low) for q in quarters]
+        each(lambda a, i: (a.shape[0], 2))
+        + each(slots) + each(slots) + each(slots)
+        + each(lambda a, i: (2, n_tensor) if i < len(attn) else (1, 1))
+        + each(lambda a, i: (2, lines))
     )
     sems = (
-        [dma((n, n_tensor, 2))] * 2
-        + [dma((n, n_tensor))] * 2
-        + [dma((2, len(attn), n_tensor))] * 2
-        + [dma((2, n, lines))] * 2
-        + [dma((3, n))] * 2
-    )
-    sums = pl.pallas_call(
-        functools.partial(reduce_kernel, n_tensor, len(attn), len(mlp)),
-        out_shape=outs,
-        in_specs=[VM] * n,
-        out_specs=[VM] * n,
+        [dma((n, n_tensor, 2))] * 2 + [dma((n, n_tensor))] * 2 + [dma((2, max(1, len(attn)), n_tensor))] * 2
+        + [dma((2, n, lines))] * 2 + [dma((3, n))] * 2
+        + [dma((2, 1, lines))] * 2 + [dma((2, 1, lines, wide))] * 2 + [dma((1,))]
+    )
+    inputs, in_specs = arrays + [rows], [VM] * n + [ANY]
+    chunk = rows.shape[-2:]
+    out_shape = [jax.ShapeDtypeStruct(a.shape[1:], a.dtype) for a in arrays]
+    out_shape.append(jax.ShapeDtypeStruct((n_tensor,) + chunk, low))
+    out_specs = [VM] * n + [ANY]
+    if base is not None:
+        inputs, in_specs = inputs + [base], in_specs + [VM]
+        sems += [vm((wide,) + chunk, low), vm(chunk, low), dma((wide,)), dma((wide,))]
+    if vectors is not None:
+        inputs, in_specs = inputs + [vectors], in_specs + [VM]
+        out_shape.append(jax.ShapeDtypeStruct(vectors.shape, vectors.dtype))
+        out_specs.append(VM)
+        sems += [vm((steps,) + vectors.shape, jnp.float32)] * 2 + [dma((steps,))] * 2
+    out = pl.pallas_call(
+        functools.partial(finish_kernel, n_tensor, len(attn), len(mlp), base is not None, vectors is not None),
+        out_shape=out_shape,
+        in_specs=in_specs,
+        out_specs=out_specs,
         scratch_shapes=scratch + sems,
-        compiler_params=pltpu.CompilerParams(collective_id=1, has_side_effects=True, vmem_limit_bytes=60 * 2**20),
-        name="reduce_weights",
-    )(*arrays)
+        compiler_params=pltpu.CompilerParams(collective_id=cid, has_side_effects=True, vmem_limit_bytes=60 * 2**20),
+        name=name,
+    )(*inputs)
+    sums = out[:n]
     if lax.axis_size("dp") > 4:
         sums = [lax.psum(s, "dp").astype(jnp.float32) * 0.25 for s in sums]
-    return sums
+    return list(sums) + list(out[n:])
 
 
 def group_kernel(n_tensor, scatter, own, full, send, recv, l_sem):
@@ -512,42 +596,34 @@
     )(own)
 
 
-def rows_kernel(n_tensor, n, *refs):
+def rows_program(n_tensor, own, full, z_send, z_recv, y_send, y_recv, l_sem):
     lines, wide = grid_of(n_tensor)
     dp, t, z, y = where_am_i(n_tensor)
-    own, full = refs[:n], refs[n : 2 * n]
-    z_send, z_recv, y_send, y_recv, l_sem = refs[2 * n :]
-    greet(neighbours(n_tensor, True, False, False))
-
-    def copy(src, dst, send, recv, peer):
-        return pltpu.make_async_remote_copy(
-            src_ref=src, dst_ref=dst, send_sem=send, recv_sem=recv, device_id=peer, device_id_type=MESH
-        )
+    n = len(own)
 
     def z_copy(a, zz, side, mine=False):
         dst = full[a].at[zz * wide + y]
         peer = ((dp, t + wide), (dp, t - wide))[side]
-        return copy(own[a] if mine else dst, dst, z_send.at[side, a, zz], z_recv.at[side, a, zz], peer)
+        return remote(own[a] if mine else dst, dst, z_send.at[side, a, zz], z_recv.at[side, a, zz], peer)
 
     def y_copy(a, zz, yy, side, mine=False):
         dst = full[a].at[zz * wide + yy]
         peer = ((dp, t + 1), (dp, t - 1))[side]
-        return copy(own[a] if mine else dst, dst, y_send.at[side, a, zz, yy], y_recv.at[side, a, zz, yy], peer)
+        return remote(own[a] if mine else dst, dst, y_send.at[side, a, zz, yy], y_recv.at[side, a, zz, yy], peer)
 
     z_has = ((z < lines - 1), (z > 0))
     y_has = ((y < wide - 1), (y > 0))
-
-    def when(condition, body):
-        pl.when(condition)(body)
-
     local = [pltpu.make_async_copy(own[a], full[a].at[t], l_sem.at[a]) for a in range(n)]
-    for side in range(2):
-        for a in range(n):
-            when(z_has[side], lambda: z_copy(a, z, side, True).start())
-            when(y_has[side], lambda: y_copy(a, z, y, side, True).start())
-    for c in local:
-        c.start()
-    for k in range(1, lines):
+
+    def begin():
+        for side in range(2):
+            for a in range(n):
+                when(z_has[side], lambda: z_copy(a, z, side, True).start())
+                when(y_has[side], lambda: y_copy(a, z, y, side, True).start())
+        for c in local:
+            c.start()
+
+    def along_z(k):
         for side in range(2):
             zz = z - k if side == 0 else z + k
 
@@ -558,7 +634,8 @@
                     when(z_has[side], lambda: z_copy(a, zz, side).start())
                     for s in range(2):
                         when(y_has[s], lambda: y_copy(a, zz, y, s).start())
-    for m in range(1, wide):
+
+    def along_y(m):
         for side in range(2):
             yy = y - m if side == 0 else y + m
 
@@ -569,39 +646,33 @@
                         y_copy(a, zz, yy, side).wait_recv()
                         if m < wide - 1:
                             when(y_has[side], lambda: y_copy(a, zz, yy, side).start())
-    for side in range(2):
-        for k in range(lines):
-            zz = z - k if side == 0 else z + k
-
-            @pl.when(z_has[side] & (zz >= 0) & (zz < lines))
-            def _():
-                for a in range(n):
-                    z_copy(a, zz, side).wait_send()
-        for m in range(wide):
-            yy = y - m if side == 0 else y + m
-
-            @pl.when(y_has[side] & (yy >= 0) & (yy < wide))
-            def _():
-                for zz in range(lines):
+
+    def settle():
+        for side in range(2):
+            for k in range(lines):
+                zz = z - k if side == 0 else z + k
+
+                @pl.when(z_has[side] & (zz >= 0) & (zz < lines))
+                def _():
                     for a in range(n):
-                        y_copy(a, zz, yy, side).wait_send()
-    for c in local:
-        c.wait()
-
-
-def gather_rows(n_tensor, arrays, cid):
-    lines, wide = grid_of(n_tensor)
-    n = len(arrays)
-    dma = pltpu.SemaphoreType.DMA
-    return pl.pallas_call(
-        functools.partial(rows_kernel, n_tensor, n),
-        out_shape=[jax.ShapeDtypeStruct((n_tensor,) + a.shape, a.dtype) for a in arrays],
-        in_specs=[ANY] * n,
-        out_specs=[ANY] * n,
-        scratch_shapes=[dma((2, n, lines))] * 2 + [dma((2, n, lines, wide))] * 2 + [dma((n,))],
-        compiler_params=pltpu.CompilerParams(collective_id=cid, has_side_effects=True),
-        name="gather_rows",
-    )(*arrays)
+                        z_copy(a, zz, side).wait_send()
+            for m in range(wide):
+                yy = y - m if side == 0 else y + m
+
+                @pl.when(y_has[side] & (yy >= 0) & (yy < wide))
+                def _():
+                    for zz in range(lines):
+                        for a in range(n):
+                            y_copy(a, zz, yy, side).wait_send()
+        for c in local:
+            c.wait()
+
+    return (
+        [begin]
+        + [functools.partial(along_z, k) for k in range(1, lines)]
+        + [functools.partial(along_y, m) for m in range(1, wide)]
+        + [settle]
+    )
 
 
 def dot(a, b, contract, **kwargs):
@@ -719,6 +790,10 @@
 longest = 512
 
 
+def rows_sum(v):
+    return jnp.sum(v, axis=0)
+
+
 def per_device(
     tokens, segment_ids, first_gain, first_shift, qkv_weight, qv_bias, out_weight, out_bias, second_gain, second_shift,
     up_weight, up_bias, down_weight, down_bias, cotangent,
@@ -791,10 +866,13 @@
     grad_down = jnp.einsum("ztf,td->zfd", hidden, cot_pair, preferred_element_type=f32).astype(low)
     grad_up = jnp.einsum("td,ztf->zdf", second_pair, grad_upper, preferred_element_type=f32).astype(low)
     second_part = jnp.einsum("ztf,zdf->td", grad_upper, up_all, preferred_element_type=f32)
-    parts = jnp.stack([second_part.reshape(wide, chunk, d), feed_part.reshape(wide, chunk, d)], axis=1).astype(low)
-    sums = jnp.sum(group_exchange(nt, parts, True, 4, "sum_parts").astype(f32), axis=0)
-    grad_second, feed = sums[0], sums[1]
-    output_mine = (middle + feed + down_bias.astype(f32)).astype(low)
+    terms = group_exchange(nt, second_part.reshape(wide, chunk, d).astype(low), True, 4, "sum_second")
+    grad_second = jnp.sum(terms.astype(f32), axis=0)
+    feed_part = feed_part.reshape(wide, chunk, d)
+    feed_mine = lax.dynamic_index_in_dim(feed_part, y, 0, keepdims=False)
+    g_up, g_down, output_all = finish(
+        nt, [], [grad_up, grad_down], feed_part.astype(low), middle + down_bias.astype(f32) + feed_mine, None, 1, "finish_mlp"
+    )
 
     cot_mine = lax.dynamic_slice_in_dim(cotangent, t * chunk, chunk, 0).astype(f32)
     grad_middle = cot_mine + norm_input_term(xhat2, rate2, gain2, grad_second)
@@ -818,22 +896,19 @@
     xhat_mine = xhat1[behind:]
     grad_tokens = (grad_middle + norm_input_term(xhat_mine, rate1[behind:], gain1, grad_first)).astype(low)
 
-    g_qkv, g_out, g_up, g_down = reduce_weights(nt, [grad_qkv, grad_out], [grad_up, grad_down])
-    output_all, grad_tokens_all = gather_rows(nt, [output_mine, grad_tokens], 5)
-
-    def rows_sum(v):
-        return jnp.sum(v, axis=0)
-
     up_slots = jnp.where(jnp.arange(wide)[None, :, None] == y, grad_up_bias[:, None, :], 0.0)
-    q_sum, v_sum = jnp.sum(grad_q.astype(f32), axis=1), jnp.sum(grad_v.astype(f32), axis=1)
     vectors = jnp.concatenate(
         [
             rows_sum(grad_first * xhat_mine), rows_sum(grad_first), rows_sum(grad_middle),
             rows_sum(grad_second * xhat2), rows_sum(grad_second), rows_sum(cot_mine),
-            q_sum.reshape(-1), v_sum.reshape(-1), up_slots.reshape(-1),
+            rows_sum(grad_q.astype(f32).transpose(1, 0, 2)).reshape(-1),
+            rows_sum(grad_v.astype(f32).transpose(1, 0, 2)).reshape(-1), up_slots.reshape(-1),
         ]
     )
-    vectors = lax.psum(vectors, ("dp", "tensor"))
+    g_qkv, g_out, grad_tokens_all, vectors = finish(
+        nt, [grad_qkv, grad_out], [], grad_tokens, None, vectors.reshape(-1, 128), 5, "finish_attn"
+    )
+    vectors = vectors.reshape(-1)
     g_first_gain, g_first_shift, g_out_bias, g_second_gain, g_second_shift, g_down_bias = (
         vectors[i * d : (i + 1) * d] for i in range(6)
     )

time: 632 us -> 564 us (0.89)
  the two profiles are of different devices: /device:TPU:0 before, /device:TPU:17 now
where the time goes in v3:
time: 564 us; the launch traced here: 555 us
  Pallas kernels  437 us (77%)
  matrix products  62.4 us (11%)
  other arithmetic  32.9 us (6%)
  local copies, waits for them, and re-layouts  20.6 us (4%)
    pallas_call x2, Pallas kernels, finish(): pl.pallas_call(functools.partial(finish_kernel, n_tensor, len(attn), len(...  247 us
    pallas_call x1, Pallas kernels, gather_weights(): pl.pallas_call(functools.partial(gather_kernel, n_tensor, len(attn), len(...  102 us
    pallas_call x2, Pallas kernels, group_exchange(): pl.pallas_call(functools.partial(group_kernel, n_tensor, scatter), out_sh...  35.7 us
    pallas_call x1, Pallas kernels, halo_exchange(): pl.pallas_call(functools.partial(halo_kernel, n_tensor, halo), out_shape=...  25.4 us
    pallas_call x1, Pallas kernels, attend_pull(): pl.pallas_call(functools.partial(attend_pull_kernel, heads), grid=(q.shap...  16.9 us
    unnamed x82, local copies, waits for them, and re-layouts  11.7 us

profile of v3, /device:TPU:17, one launch (start us, length us, event | category | flops | bytes accessed | tf_op | source)
XLA Modules:
  0.0 554.6 jit_solution(1147805958987278223)
XLA Ops:
  0.7 1.9 convert_reduce_fusion.4
  2.6 0.7 copy-done.1
  3.3 0.6 multiply_reduce_fusion
  4.0 2.4 subtract_multiply_fusion
  6.5 1.3 copy.65.refs_0_
  8.0 0.6 maximum_bitcast_fusion.refs_2_
  8.6 101.9 %gather_weights.1 = (bf16[8,1024,384]{2,1,0:T(8,128)(2,1)}, bf16[8,128,1024]{2,1,0:T(8,128)(2,1)}, bf16[8,64,128]{2,1,0:T(8,128)(2,1)}, bf16[4,1024,512]{2,1,0:T(8,128)(2,1)}, bf16[4,512,1024]{2,1,0:T(8,128)(2,1)}) custom-call(bf16[1024,384]{1,0:T(8,128)(2,1)} %copy.65.refs_0_, bf16[128,1024]{1,0:T(8,128)(2,1)} %refs_1_.1, ...), custom_call_target="tpu_custom_call" | custom-call | tf_op jit(solution)/shard_map/gather_weights/pallas_call | solution.py:217
  110.5 0.9 convert_bitcast_fusion.3
  111.7 4.7 fusion.24.v
  116.3 0.7 fusion.54.q
  117.1 1.8 fusion.32.k
  119.0 0.2 convert_select_fusion.1.dist
  119.3 10.1 %attend.1 = bf16[8,256,128]{2,1,0:T(8,128)(2,1)S(1)} custom-call(f32[16]{0:T(128)S(1)} %multiply_exponential_fusion.slopes, f32[256,768]{1,0:T(8,128)S(1)} %convert_select_fusion.1.dist, bf16[8,256,128]{2,1,0:T(8,128)(2,1)S(1)} %fusion.54.q, bf16[8,768,128]{2,1,0:T(8,128)(2,1)S(1)} %fusion.32.k, bf16[8,768,128]{2,1,0:T(8,128)(2,1)} %fusion.24.v), custom_call_target="tpu_custom_call" | custom-call | tf_op jit(solution)/shard_map/attend/pallas_call | solution.py:742
  129.4 0.6 fusion.74
  130.1 0.9 copy-done.4
  131.0 0.8 fusion.78
  131.8 0.3 multiply_reduce_fusion.5
  132.2 1.0 add_convert_fusion.3.own
  133.2 18.3 %share_second.1 = bf16[2,256,1024]{2,1,0:T(8,128)(2,1)} custom-call(bf16[256,1024]{1,0:T(8,128)(2,1)} %add_convert_fusion.3.own), custom_call_target="tpu_custom_call" | custom-call | tf_op jit(solution)/shard_map/share_second/pallas_call | solution.py:549
  151.5 6.9 %fusion.79 = f32[4,512,512]{1,2,0:T(8,128)} fusion(bf16[512,1024,1]{1,0,2:T(8,128)(2,1)} %bitcast.163, bf16[4,1024,512]{2,1,0:T(8,128)(2,1)} %get-tuple-element.30), kind=kOutput, calls=%fused_computation.140 | convolution fusion | flops 2147483648 | bytes 9437184 | tf_op jit(solution)/shard_map/td,zdf->ztf/dot_general | solution.py:859
  158.4 8.4 %convert_reduce_fusion = (f32[4,512]{1,0:T(4,128)S(1)}, bf16[4,512,512]{2,1,0:T(8,128)(2,1)S(1)}) fusion(f32[4,512,512]{1,2,0:T(8,128)} %fusion.79, f32[4,512]{1,0:T(4,128)S(1)} %bitcast.174, bf16[4,512,1024]{2,1,0:T(8,128)(2,1)} %get-tuple-element.29, bf16[2048,1024]{1,0:T(8,128)(2,1)} %param.29, s32[]{:T(128)S(6)} %select_n.53), kind=kOutput, calls=%fused_computation.13 | convolution fusion | flops 2170550272 | bytes 11550724 | tf_op jit(solution)/shard_map/td,zfd->ztf/dot_general | solution.py:863
  166.9 3.3 bitcast_convert_fusion
  170.2 17.4 %sum_second.1 = bf16[2,256,1024]{2,1,0:T(8,128)(2,1)} custom-call(bf16[2,256,1024]{2,1,0:T(8,128)(2,1)} %bitcast.165), custom_call_target="tpu_custom_call" | custom-call | tf_op jit(solution)/shard_map/sum_second/pallas_call | solution.py:549
  187.6 2.0 convert_reduce_fusion.2
  189.6 1.0 copy-done.3
  190.6 0.5 multiply_reduce_fusion.1
  191.1 6.3 %fusion.75 = f32[512,1024,1]{1,0,2:T(8,128)} fusion(bf16[4,512,1024]{2,1,0:T(8,128)(2,1)S(1)} %copy-done.27, f32[4,512,512]{1,2,0:T(8,128)} %fusion.79, f32[4,512]{1,0:T(4,128)S(1)} %bitcast.175), kind=kOutput, calls=%fused_computation.136 | convolution fusion | flops 2157969408 | bytes 10493952 | tf_op jit(solution)/shard_map/ztf,zfd->td/dot_general | solution.py:862
  197.4 3.4 fusion.76
  200.8 0.8 fusion.57.g
  201.6 0.2 convert_select_fusion.dist
  201.8 16.9 %attend_pull.1 = (bf16[8,256,128]{2,1,0:T(8,128)(2,1)S(1)}, bf16[8,768,128]{2,1,0:T(8,128)(2,1)S(1)}, bf16[8,768,128]{2,1,0:T(8,128)(2,1)}) custom-call(f32[16]{0:T(128)S(1)} %multiply_exponential_fusion.slopes, f32[768,256]{1,0:T(8,128)S(1)} %convert_select_fusion.dist, bf16[8,256,128]{2,1,0:T(8,128)(2,1)S(1)} %fusion.54.q, bf16[8,768,128]{2,1,0:T(8,128)(2,1)} %copy-done, ...), custom_call_target="tpu_custom_call" | custom-call | tf_op jit(solution)/shard_map/attend_pull/pallas_call | solution.py:756
  218.7 0.3 constant_dynamic-update-slice_fusion.1
  219.0 1.1 copy-done.6
  220.1 0.4 constant_dynamic-update-slice_fusion
  220.5 6.4 %fusion.14 = f32[768,1024]{1,0:T(8,128)S(1)} fusion(bf16[8,768,256]{2,1,0:T(8,128)(2,1)S(1)} %constant_dynamic-update-slice_fusion, bf16[8,1024,384]{2,1,0:T(8,128)(2,1)} %get-tuple-element.31), kind=kOutput, calls=%fused_computation.36 | convolution fusion | flops 3221225472 | bytes 10485760 | tf_op jit(solution)/shard_map/gte,gde->td/dot_general | solution.py:891
  226.9 1.6 copy-done.12
  228.5 1.1 slice.180
  229.6 25.4 %halo_exchange.1 = bf16[2,256,1024]{2,1,0:T(8,128)(2,1)} custom-call(bf16[2,256,1024]{2,1,0:T(8,128)(2,1)} %bitcast.159), custom_call_target="tpu_custom_call" | custom-call | tf_op jit(solution)/shard_map/halo_exchange/pallas_call | solution.py:588
  255.0 1.7 select_reduce_fusion
  256.8 3.3 multiply_reduce_fusion.2
  260.3 0.2 convert_reduce_fusion.1
  260.7 2.7 add_convert_fusion.2.refs_2_
  263.4 3.7 convert_bitcast_fusion
  267.1 0.8 convert_bitcast_fusion.2
  267.9 3.5 pad_maximum_fusion.refs_0_
  271.4 0.2 copy.80
  271.6 2.0 convolution_convert_fusion.1
  273.7 121.3 %finish_attn.1 = (bf16[1024,384]{1,0:T(8,128)(2,1)}, bf16[128,1024]{1,0:T(8,128)(2,1)}, bf16[8,256,1024]{2,1,0:T(8,128)(2,1)}, f32[96,128]{1,0:T(8,128)}) custom-call(bf16[8,1024,384]{2,1,0:T(8,128)(2,1)} %pad_maximum_fusion.refs_0_, bf16[8,128,1024]{2,1,0:T(8,128)(2,1)} %bitcast.153, bf16[256,1024]{1,0:T(8,128)(2,1)} %add_convert_fusion.2.refs_2_, ...), custom_call_target="tpu_custom_call" | custom-call | tf_op jit(solution)/shard_map/finish_attn/pallas_call | solution.py:504
  395.0 1.4 slice_bitcast_fusion.3
  396.5 0.6 pad_maximum_fusion.1
  397.2 1.4 copy.81
  398.6 1.2 copy.82
  399.8 0.8 convert_element_type.164
  400.7 0.7 slice.124
  401.4 0.6 constant_dynamic-slice_fusion
  402.0 2.7 convert_element_type.148.refs_2_
  404.7 7.9 %convolution_convert_fusion.refs_1_ = bf16[4,512,1024]{2,1,0:T(8,128)(2,1)} fusion(bf16[2048,1024]{1,0:T(8,128)(2,1)} %param.29, s32[]{:T(128)S(6)} %select_n.53, f32[4,512,512]{1,2,0:T(8,128)} %fusion.79, f32[4,512]{1,0:T(4,128)S(1)} %bitcast.176), kind=kOutput, calls=%fused_computation.24 | convolution fusion | flops 2160066560 | bytes 9445380 | tf_op jit(solution)/shard_map/ztf,td->zfd/dot_general | solution.py:866
  412.6 4.5 convert_bitcast_fusion.1.refs_0_
  417.1 125.7 %finish_mlp.1 = (bf16[1024,512]{1,0:T(8,128)(2,1)}, bf16[512,1024]{1,0:T(8,128)(2,1)}, bf16[8,256,1024]{2,1,0:T(8,128)(2,1)}) custom-call(bf16[4,1024,512]{2,1,0:T(8,128)(2,1)} %convert_bitcast_fusion.1.refs_0_, bf16[4,512,1024]{2,1,0:T(8,128)(2,1)} %convolution_convert_fusion.refs_1_, bf16[2,256,1024]{2,1,0:T(8,128)(2,1)} %convert_element_type.148.refs_2_, ...), custom_call_target="tpu_custom_call" | custom-call | tf_op jit(solution)/shard_map/finish_mlp/pallas_call | solution.py:504
  542.9 3.0 convert_element_type.165
  545.9 2.8 convert_element_type.166
  548.6 2.1 copy.117
  550.8 1.6 copy-done.8
  552.3 2.0 copy.118
  (111 shorter events, 1.2 us)
Async XLA Ops:
  0.7 2.7 copy-start.1
  0.7 3.3 copy-start.20
  0.7 3.3 copy-start.21
  4.0 2.4 copy-start.16
  4.0 3.8 copy-start.29
  4.0 4.0 copy-start.26
  6.4 110.7 %copy-start.10 = (bf16[768,1024]{1,0:T(8,128)(2,1)}, bf16[768,1024]{1,0:T(8,128)(2,1)S(1)}, u32[]{:S(2)}) copy-start(bf16[768,1024]{1,0:T(8,128)(2,1)S(1)} %get-tuple-element.56) | copy-start | bytes 4718596
  111.5 4.9 slice-start
  111.7 4.7 slice-start.1
  117.1 1.8 copy-start.19
  118.9 11.2 %copy-start = (bf16[8,768,128]{2,1,0:T(8,128)(2,1)}, bf16[8,768,128]{2,1,0:T(8,128)(2,1)S(1)}, u32[]{:S(2)}) copy-start(bf16[8,768,128]{2,1,0:T(8,128)(2,1)S(1)} %fusion.32.k) | copy-start | bytes 4718596
  118.9 10.5 %copy-start.2 = (bf16[2048,1024]{1,0:T(8,128)(2,1)S(1)}, bf16[2048,1024]{1,0:T(8,128)(2,1)}, u32[]{:S(2)}) copy-start(bf16[2048,1024]{1,0:T(8,128)(2,1)} %param.15) | copy-start | bytes 12582916
  129.4 0.7 copy-start.22
  129.4 1.6 copy-start.4
  130.1 2.0 copy-start.23
  130.1 2.1 copy-start.24
  158.4 8.5 %copy-start.28 = (bf16[4,1024,512]{2,1,0:T(8,128)(2,1)S(1)}, bf16[4,1024,512]{2,1,0:T(8,128)(2,1)}, u32[]{:S(2)}) copy-start(bf16[4,1024,512]{2,1,0:T(8,128)(2,1)} %get-tuple-element.30) | copy-start | bytes 12582916
  166.9 3.4 copy-start.30
  187.6 3.5 copy-start.27
  189.6 1.0 copy-start.3
  191.1 6.3 %copy-start.25 = (bf16[1024]{0:T(1024)(128)(2,1)S(1)}, bf16[1024]{0:T(1024)(128)(2,1)}, u32[]{:S(2)}) copy-start(bf16[1024]{0:T(1024)(128)(2,1)} %param.28) | copy-start | bytes 6148
  197.4 3.4 copy-start.5
  218.7 1.4 copy-start.6
  220.5 6.4 %copy-start.14 = (bf16[8,768,256]{2,1,0:T(8,128)(2,1)}, bf16[8,768,256]{2,1,0:T(8,128)(2,1)S(1)}, u32[]{:S(2)}) copy-start(bf16[8,768,256]{2,1,0:T(8,128)(2,1)S(1)} %constant_dynamic-update-slice_fusion) | copy-start | bytes 9437188
  226.9 1.6 copy-start.12
  256.8 3.5 copy-start.7
  260.1 3.2 copy-start.11
  260.1 3.2 copy-start.15
  260.7 6.5 %copy-start.18 = (f32[12288]{0:T(1024)}, f32[12288]{0:T(1024)S(1)}, u32[]{:S(2)}) copy-start(f32[12288]{0:T(1024)S(1)} %constant_dynamic-update-slice_fusion.3) | copy-start | bytes 147460
  395.0 4.8 copy-start.17
  404.7 7.9 %copy-start.13 = (bf16[2,256,1024]{2,1,0:T(8,128)(2,1)S(1)}, bf16[2,256,1024]{2,1,0:T(8,128)(2,1)}, u32[]{:S(2)}) copy-start(bf16[2,256,1024]{2,1,0:T(8,128)(2,1)} %share_second.1) | copy-start | bytes 3145732
  404.7 7.9 %copy-start.31 = (bf16[4,512,512]{2,1,0:T(8,128)(2,1)S(1)}, bf16[4,512,512]{2,1,0:T(8,128)(2,1)}, u32[]{:S(2)}) copy-start(bf16[4,512,512]{2,1,0:T(8,128)(2,1)} %copy-done.30) | copy-start | bytes 6291460
  542.9 5.8 %copy-start.9 = (bf16[8,256,1024]{2,1,0:T(8,128)(2,1)S(1)}, bf16[8,256,1024]{2,1,0:T(8,128)(2,1)}, u32[]{:S(2)}) copy-start(bf16[8,256,1024]{2,1,0:T(8,128)(2,1)} %get-tuple-element.34) | copy-start | bytes 12582916
  548.6 3.7 copy-start.8

commit v4 on v3

--- a/solution.py
+++ b/solution.py
@@ -273,7 +273,7 @@
     return [begin] + [functools.partial(advance, i) for i in range(len(peers))] + [settle]
 
 
-def finish_kernel(n_tensor, n_attn, n_mlp, with_feed, with_vectors, *refs):
+def finish_kernel(n_tensor, n_attn, n_mlp, with_feed, with_vectors, pull, *refs):
     lines, wide = grid_of(n_tensor)
     dp, t, z, y = where_am_i(n_tensor)
     n = n_attn + n_mlp
@@ -286,8 +286,10 @@
     terms, rows_own = take(n), take(1)
     feed_base = take(1)[0] if with_feed else None
     vec_own = take(1)[0] if with_vectors else None
+    pull_in = take(pull_inputs) if pull else []
     final, rows_full = take(n), take(1)
     vec_out = take(1)[0] if with_vectors else None
+    pull_out = take(pull_outputs) if pull else []
     from_c, from_x, to_x, acc, from_y, from_z = (take(n) for i in range(6))
     c_send, c_recv, x_send, x_recv, y_send, y_recv, z_send, z_recv, q_send, q_recv = take(10)
     rows_sems = take(5)
@@ -296,14 +298,19 @@
         rows_own = [feed_sum]
     rows_steps = rows_program(n_tensor, rows_own, rows_full, *rows_sems)
     vec_steps = doubling_program(n_tensor, vec_own, vec_out, *take(4)) if with_vectors else []
+    work, pull_peers, pull_end = pull_program(n_tensor, pull, pull_in, pull_out, refs) if pull else (None, [], None)
     quad = dp % 4
     side_x = quad // 2
     core = quad % 2
     core_peer, x_peer = (dp ^ 1, t), (dp ^ 2, t)
 
+    lines_order = [i // 2 if i % 2 else lines - 1 - i // 2 for i in range(lines)]
+
+    def across(a):
+        return [(y + 1 + m) % wide for m in range(wide)] if a < n_attn else [0]
+
     def slots(a):
-        order = [0, lines - 1] + list(range(1, lines - 1))
-        return [(zz, yy) for zz in order for yy in (range(wide) if a < n_attn else [0])]
+        return [(zz, yy) for zz in lines_order for yy in across(a)]
 
     def index(a, zz, yy):
         return zz * wide + yy if a < n_attn else zz
@@ -358,17 +365,22 @@
                     add_rows(acc[a].at[lane], [acc[a].at[lane], from_y[a].at[side, lane]])
                     when(yy != y, lambda: y_copy(a, zz, yy, side).start())
 
-    def z_stage(a, zz):
+    def z_round(r):
         for side in range(2):
-            @pl.when((z <= zz) if side == 0 else (z >= zz))
+            zz = lines - 1 - r + z if side == 0 else z - (lines - 1 - r)
+
+            @pl.when((zz < lines) & (zz >= 0))
             def _():
                 @pl.when((z > 0) if side == 0 else (z < lines - 1))
                 def _():
-                    s = index(a, zz, y)
-                    z_copy(a, zz, side).wait_recv()
-                    add_rows(acc[a].at[s], [acc[a].at[s], from_z[a].at[side, zz]])
-
-                when(z != zz, lambda: z_copy(a, zz, side).start())
+                    for a in order:
+                        s = index(a, zz, y)
+                        z_copy(a, zz, side).wait_recv()
+                        add_rows(acc[a].at[s], [acc[a].at[s], from_z[a].at[side, zz]])
+
+                if r < lines - 1:
+                    for a in order:
+                        z_copy(a, zz, side).start()
 
     def q_copy(a, q, hop, peer):
         return remote(quarter(final[a], a, q), quarter(final[a], a, q), q_send.at[hop, a], q_recv.at[hop, a], peer)
@@ -393,7 +405,7 @@
         for yy in range(wide):
             when(yy != y, lambda: feed_copy(yy, y).wait_send())
 
-    peers = neighbours(n_tensor)
+    peers = neighbours(n_tensor) + pull_peers
     if with_feed and wide > 2:
         peers += [(yy != y, (dp, z * wide + yy)) for yy in range(wide)]
     if with_vectors:
@@ -401,7 +413,6 @@
     greet(peers)
     attn, mlp = list(range(n_attn)), list(range(n_attn, n))
     order = attn + mlp
-    lines_order = [0, lines - 1] + list(range(1, lines - 1))
     if with_feed:
         feed_start()
     else:
@@ -425,25 +436,46 @@
         if len(vec_steps) > 1:
             vec_steps.pop(0)()
 
-    for i in range(lines + 2):
-        if i < lines:
-            for a in order:
-                for yy in range(wide) if a < n_attn else [0]:
-                    x_stage(a, lines_order[i], yy)
-        if 0 <= i - 1 < lines:
+    def x_part(zz):
+        for a in order:
+            for yy in across(a):
+                x_stage(a, zz, yy)
+
+    def turn(i, r):
+        for zz in lines_order[i : i + 2]:
             for a in attn:
-                y_stage(a, lines_order[i - 1])
-        lag = 2 if n_attn else 1
-        if 0 <= i - lag < lines:
-            for a in order:
-                z_stage(a, lines_order[i - lag])
+                y_stage(a, zz)
         aside()
+        z_round(r)
+
+    def late(r):
+        aside()
+        z_round(r)
+
+    steps = []
+    for i in range(0, lines, 2):
+        steps += [functools.partial(x_part, zz) for zz in lines_order[i : i + 2]]
+        steps.append(functools.partial(turn, i, i // 2))
+    steps += [functools.partial(late, r) for r in range((lines + 1) // 2, lines)]
+    if work:
+        @pl.loop(0, n_tensor)
+        def _(p):
+            work(p)
+            for k in range(1, n_tensor):
+                if steps:
+                    when(p == k, steps.pop(0))
+
+        pull_end[0]()
+    for step in steps:
+        step()
     for a in order:
         home(a)
     aside()
     for a in order:
         q_copy(a, quad ^ 2, 0, x_peer).wait_recv()
         q_copy(a, quad ^ 2, 2, core_peer).start()
+    if work:
+        pull_end[1]()
     while rows_steps:
         rows_steps.pop(0)()
     while vec_steps:
@@ -467,7 +499,7 @@
             when(zz < z, lambda: z_copy(a, zz, 1).wait_send())
 
 
-def finish(n_tensor, attn, mlp, rows, base, vectors, cid, name):
+def finish(n_tensor, attn, mlp, rows, base, vectors, cid, name, pull=None):
     lines, wide = grid_of(n_tensor)
     arrays = list(attn) + list(mlp)
     n = len(arrays)
@@ -501,8 +533,18 @@
         out_shape.append(jax.ShapeDtypeStruct(vectors.shape, vectors.dtype))
         out_specs.append(VM)
         sems += [vm((steps,) + vectors.shape, jnp.float32)] * 2 + [dma((steps,))] * 2
+    heads = 0
+    if pull is not None:
+        heads = pull[0].shape[0] // n_tensor
+        inputs, in_specs = inputs + list(pull), in_specs + [pl.BlockSpec(memory_space=pltpu.SMEM)] + [VM] * (pull_inputs - 1)
+        shapes, more = pull_shapes(n_tensor, pull)
+        out_shape += shapes
+        out_specs += [VM] * pull_outputs
+        sems += more
     out = pl.pallas_call(
-        functools.partial(finish_kernel, n_tensor, len(attn), len(mlp), base is not None, vectors is not None),
+        functools.partial(
+            finish_kernel, n_tensor, len(attn), len(mlp), base is not None, vectors is not None, heads
+        ),
         out_shape=out_shape,
         in_specs=in_specs,
         out_specs=out_specs,
@@ -554,45 +596,6 @@
         scratch_shapes=[dma((wide,)), dma((wide,)), dma],
         compiler_params=pltpu.CompilerParams(collective_id=cid, has_side_effects=True),
         name=name,
-    )(own)
-
-
-def halo_kernel(n_tensor, halo, own, got, send, recv):
-    dp, t, z, y = where_am_i(n_tensor)
-    ahead = [(t + 1 + m < n_tensor, (dp, t + 1 + m)) for m in range(halo)]
-    greet(ahead + [(t - 1 - m >= 0, (dp, t - 1 - m)) for m in range(halo)])
-
-    def step(m):
-        return pltpu.make_async_remote_copy(
-            src_ref=own.at[halo - 1 - m], dst_ref=got.at[m], send_sem=send.at[m], recv_sem=recv.at[m],
-            device_id=(dp, t - 1 - m), device_id_type=MESH,
-        )
-
-    for m in range(halo):
-        @pl.when(t - 1 - m >= 0)
-        def _():
-            step(m).start()
-    for m in range(halo):
-        @pl.when(t + 1 + m < n_tensor)
-        def _():
-            step(m).wait_recv()
-
-        @pl.when(t - 1 - m >= 0)
-        def _():
-            step(m).wait_send()
-
-
-def halo_exchange(n_tensor, own):
-    halo = own.shape[0]
-    dma = pltpu.SemaphoreType.DMA
-    return pl.pallas_call(
-        functools.partial(halo_kernel, n_tensor, halo),
-        out_shape=jax.ShapeDtypeStruct(own.shape, own.dtype),
-        in_specs=[ANY],
-        out_specs=ANY,
-        scratch_shapes=[dma((halo,)), dma((halo,))],
-        compiler_params=pltpu.CompilerParams(collective_id=2, has_side_effects=True),
-        name="halo_exchange",
     )(own)
 
 
@@ -704,11 +707,9 @@
     ctx[0] = out.astype(jnp.bfloat16)
 
 
-def attend_pull_kernel(heads, slopes, dist, q, k, v, g, dq, dk, dv):
-    pair = pl.program_id(0)
-    lanes = q.shape[2]
+def pull_scores(heads, slope_of, dist, query, keys, values, grad):
+    lanes = query.shape[1]
     scale = 1.0 / math.sqrt(lanes // heads)
-    query, keys, values, grad = q[0], k[0], v[0], g[0]
     head = head_of_lane(query.shape, heads)
     head_rows = lax.broadcasted_iota(jnp.int32, (lanes, query.shape[0]), 0) // (lanes // heads)
     low = jnp.bfloat16
@@ -718,7 +719,7 @@
     for h in range(heads):
         masked = jnp.where(head == h, query * low(scale), low(0))
         masked_grad = jnp.where(head == h, grad, low(0))
-        scores = dot(keys, masked, NT) - slopes[pair * heads + h] * dist[...]
+        scores = dot(keys, masked, NT) - slope_of(h) * dist[...]
         peak = jnp.max(scores, axis=0, keepdims=True)
         expo = jnp.exp(scores - peak)
         probs = expo * (1.0 / jnp.sum(expo, axis=0, keepdims=True))
@@ -728,9 +729,91 @@
         grad_v = grad_v + dot(probs.astype(low), masked_grad, NN)
         grad_k = grad_k + dot(grad_scores, masked, NN)
         grad_q = jnp.where(head_rows == h, dot(keys, grad_scores, TN), grad_q)
-    dq[0] = (jnp.transpose(grad_q) * scale).astype(low)
-    dk[0] = grad_k.astype(low)
-    dv[0] = grad_v.astype(low)
+    return (jnp.transpose(grad_q) * scale).astype(low), grad_k.astype(low), grad_v.astype(low)
+
+
+pull_inputs, pull_outputs = 10, 5
+
+
+def pull_shapes(n_tensor, pull):
+    slopes, dist, q, k, v, grad, context, out_all, qkv_all, normed_t = pull
+    span, chunk, lanes, d = k.shape[1], q.shape[1], q.shape[2], normed_t.shape[0]
+    halo = (span - chunk) // chunk
+    low, f32 = jnp.bfloat16, jnp.float32
+    shape = jax.ShapeDtypeStruct
+    vm, dma = pltpu.VMEM, pltpu.SemaphoreType.DMA
+    outs = [
+        shape(qkv_all.shape, low), shape(out_all.shape, low), shape((chunk, d), f32),
+        shape((n_tensor, 8, lanes), f32), shape((n_tensor, 8, lanes), f32),
+    ]
+    scratch = [
+        vm(q.shape, low), vm((n_tensor, span, 2 * lanes), low), vm((halo, chunk, d), low), vm((halo, chunk, d), low),
+        dma((halo,)), dma((halo,)),
+    ]
+    return outs, scratch
+
+
+def pull_program(n_tensor, heads, ins, outs, scratch):
+    dp, t, z, y = where_am_i(n_tensor)
+    slopes, dist, q, k, v, grad, context, out_all, qkv_all, normed_t = ins
+    grad_qkv, grad_out, first, q_sum, v_sum = outs
+    grad_q, grad_kv, halo_own, halo_got, h_send, h_recv = scratch
+    halo, chunk, d = halo_own.shape
+    span, lanes = k.shape[1], q.shape[2]
+    behind = span - chunk
+    low, f32 = jnp.bfloat16, jnp.float32
+
+    def work(p):
+        grad_context = dot(grad[...], out_all[p], NT).astype(low)
+        grad_out[p] = dot(context[p], grad[...], TN).astype(low)
+        gq, gk, gv = pull_scores(heads, lambda h: slopes[p * heads + h], dist, q[p], k[p], v[p], grad_context)
+        grad_q[p] = gq
+        grad_kv[p, :, :lanes] = gk
+        grad_kv[p, :, lanes:] = gv
+        q_sum[p] = jnp.broadcast_to(jnp.sum(gq.astype(f32), axis=0, keepdims=True), (8, lanes))
+        v_sum[p] = jnp.broadcast_to(jnp.sum(gv.astype(f32), axis=0, keepdims=True), (8, lanes))
+        grad_qkv[p, :, :lanes] = dot(normed_t[:, behind:], gq, NN).astype(low)
+        grad_qkv[p, :, lanes:] = dot(normed_t[...], grad_kv[p], NN).astype(low)
+
+    def step(m):
+        return remote(halo_own.at[halo - 1 - m], halo_got.at[m], h_send.at[m], h_recv.at[m], (dp, t - 1 - m))
+
+    ahead = [(t + 1 + m < n_tensor, (dp, t + 1 + m)) for m in range(halo)]
+    back = [(t - 1 - m >= 0, (dp, t - 1 - m)) for m in range(halo)]
+    tile = min(128, chunk)
+
+    def rows_first():
+        for j in range(halo):
+            @pl.loop(0, chunk // tile)
+            def _(i):
+                here = pl.multiple_of(i * tile, tile)
+                total = jnp.zeros((tile, d), f32)
+                for p in range(n_tensor):
+                    total = total + dot(grad_kv[p, pl.ds(j * chunk + here, tile)], qkv_all[p, :, lanes:], NT)
+                halo_own[j, pl.ds(here, tile)] = total.astype(low)
+
+        for m in range(halo):
+            when(back[m][0], lambda: step(m).start())
+
+        @pl.loop(0, chunk // tile)
+        def _(i):
+            here = pl.multiple_of(i * tile, tile)
+            total = jnp.zeros((tile, d), f32)
+            for p in range(n_tensor):
+                total = total + dot(grad_kv[p, pl.ds(behind + here, tile)], qkv_all[p, :, lanes:], NT)
+                total = total + dot(grad_q[p, pl.ds(here, tile)], qkv_all[p, :, :lanes], NT)
+            first[pl.ds(here, tile)] = total
+
+    def rows_last():
+        for m in range(halo):
+            @pl.when(ahead[m][0])
+            def _():
+                step(m).wait_recv()
+                add_rows(first, [first, halo_got.at[m]])
+
+            when(back[m][0], lambda: step(m).wait_send())
+
+    return work, ahead + back, (rows_first, rows_last)
 
 
 def by_shard(array):
@@ -749,20 +832,6 @@
         compiler_params=pltpu.CompilerParams(vmem_limit_bytes=50 * 2**20),
         name="attend",
     )(slopes, dist, q, k, v)
-
-
-def attend_pull(slopes, dist, q, k, v, g):
-    heads = slopes.shape[0] // q.shape[0]
-    return pl.pallas_call(
-        functools.partial(attend_pull_kernel, heads),
-        grid=(q.shape[0],),
-        out_shape=[jax.ShapeDtypeStruct(a.shape, jnp.bfloat16) for a in (q, k, v)],
-        in_specs=[pl.BlockSpec(memory_space=pltpu.SMEM), pl.BlockSpec(dist.shape, lambda p: (0, 0))]
-        + [by_shard(a) for a in (q, k, v, g)],
-        out_specs=[by_shard(a) for a in (q, k, v)],
-        compiler_params=pltpu.CompilerParams(vmem_limit_bytes=50 * 2**20),
-        name="attend_pull",
-    )(slopes, dist, q, k, v, g)
 
 
 norm_eps = 1e-05
@@ -846,8 +915,8 @@
     values = (
         jnp.einsum("td,gde->gte", normed, qkv_all[:, :, 2 * lanes :], preferred_element_type=f32) + v_bias[:, None]
     ).astype(low)
-    context = attend(slopes, dist, query, keys, values)
-    context = context.transpose(1, 0, 2).reshape(chunk, d)
+    context_by_shard = attend(slopes, dist, query, keys, values)
+    context = context_by_shard.transpose(1, 0, 2).reshape(chunk, d)
     out_full = out_all.reshape(d, d)
     mixed = jnp.dot(context, out_full, preferred_element_type=f32)
     middle = near[behind:] + mixed + out_bias.astype(f32)
@@ -870,29 +939,15 @@
     grad_second = jnp.sum(terms.astype(f32), axis=0)
     feed_part = feed_part.reshape(wide, chunk, d)
     feed_mine = lax.dynamic_index_in_dim(feed_part, y, 0, keepdims=False)
-    g_up, g_down, output_all = finish(
-        nt, [], [grad_up, grad_down], feed_part.astype(low), middle + down_bias.astype(f32) + feed_mine, None, 1, "finish_mlp"
-    )
-
     cot_mine = lax.dynamic_slice_in_dim(cotangent, t * chunk, chunk, 0).astype(f32)
     grad_middle = cot_mine + norm_input_term(xhat2, rate2, gain2, grad_second)
-    grad_middle_low = grad_middle.astype(low)
-    grad_out = jnp.dot(context.T, grad_middle_low, preferred_element_type=f32).astype(low).reshape(out_all.shape)
-    grad_context = jnp.einsum("td,gcd->gtc", grad_middle_low, out_all, preferred_element_type=f32).astype(low)
-    grad_q, grad_k, grad_v = attend_pull(slopes, dist.T, query, keys, values, grad_context)
-    grad_kv = jnp.concatenate([grad_k, grad_v], axis=2)
-    grad_qkv = jnp.concatenate(
-        [
-            jnp.einsum("td,gte->gde", mine, grad_q, preferred_element_type=f32),
-            jnp.einsum("td,gte->gde", normed, grad_kv, preferred_element_type=f32),
-        ],
-        axis=2,
-    ).astype(low)
-    first_part = jnp.einsum("gte,gde->td", grad_kv, qkv_all[:, :, lanes:], preferred_element_type=f32)
-    first_mine = first_part[behind:] + jnp.einsum("gte,gde->td", grad_q, qkv_all[:, :, :lanes], preferred_element_type=f32)
-    got = halo_exchange(nt, first_part[:behind].astype(low).reshape(halo, chunk, d)).astype(f32)
-    there = (t + 1 + jnp.arange(halo)) < nt
-    grad_first = first_mine + jnp.sum(jnp.where(there[:, None, None], got, 0.0), axis=0)
+    pull = [
+        slopes, dist.T, query, keys, values, grad_middle.astype(low), context_by_shard, out_all, qkv_all, normed.T,
+    ]
+    g_up, g_down, output_all, grad_qkv, grad_out, grad_first, q_sum, v_sum = finish(
+        nt, [], [grad_up, grad_down], feed_part.astype(low), middle + down_bias.astype(f32) + feed_mine, None, 1,
+        "finish_mlp", pull,
+    )
     xhat_mine = xhat1[behind:]
     grad_tokens = (grad_middle + norm_input_term(xhat_mine, rate1[behind:], gain1, grad_first)).astype(low)
 
@@ -901,8 +956,7 @@
         [
             rows_sum(grad_first * xhat_mine), rows_sum(grad_first), rows_sum(grad_middle),
             rows_sum(grad_second * xhat2), rows_sum(grad_second), rows_sum(cot_mine),
-            rows_sum(grad_q.astype(f32).transpose(1, 0, 2)).reshape(-1),
-            rows_sum(grad_v.astype(f32).transpose(1, 0, 2)).reshape(-1), up_slots.reshape(-1),
+            q_sum[:, 0].reshape(-1), v_sum[:, 0].reshape(-1), up_slots.reshape(-1),
         ]
     )
     g_qkv, g_out, grad_tokens_all, vectors = finish(

time: 564 us -> 475 us (0.84)
  the two profiles are of different devices: /device:TPU:17 before, /device:TPU:0 now
where the time goes in v4:
time: 475 us; the launch traced here: 466 us
  Pallas kernels  373 us (79%)
  matrix products  44.1 us (9%)
  other arithmetic  27.7 us (6%)
  local copies, waits for them, and re-layouts  19.3 us (4%)
    pallas_call x2, Pallas kernels, finish(): pl.pallas_call(functools.partial(finish_kernel, n_tensor, len(attn), len(...  222 us
    pallas_call x1, Pallas kernels, gather_weights(): pl.pallas_call(functools.partial(gather_kernel, n_tensor, len(attn), len(...  104 us
    pallas_call x2, Pallas kernels, group_exchange(): pl.pallas_call(functools.partial(group_kernel, n_tensor, scatter), out_sh...  36.1 us
    pallas_call x1, Pallas kernels, attend(): pl.pallas_call(functools.partial(attend_kernel, heads), grid=(q.shape[0],...  10.1 us

profile of v4, /device:TPU:0, one launch (start us, length us, event | category | flops | bytes accessed | tf_op | source)
XLA Modules:
  0.0 465.9 jit_solution(11095127188841843992)
XLA Ops:
  0.7 0.0 copy-start.4
  0.7 1.6 convert_reduce_fusion.3
  2.3 0.7 copy-done.4
  3.0 0.6 multiply_reduce_fusion
  3.6 0.0 copy-start.13
  3.7 2.4 subtract_multiply_fusion
  6.1 0.1 copy.54
  6.1 1.3 copy.56.refs_0_
  7.5 0.1 reshape.184
  7.6 0.1 reshape.185
  7.6 0.6 maximum_bitcast_fusion.refs_2_
  8.3 104.4 %gather_weights.1 = (bf16[8,1024,384]{2,1,0:T(8,128)(2,1)}, bf16[8,128,1024]{2,1,0:T(8,128)(2,1)}, bf16[8,64,128]{2,1,0:T(8,128)(2,1)}, bf16[4,1024,512]{2,1,0:T(8,128)(2,1)}, bf16[4,512,1024]{2,1,0:T(8,128)(2,1)}) custom-call(bf16[1024,384]{1,0:T(8,128)(2,1)} %copy.56.refs_0_, bf16[128,1024]{1,0:T(8,128)(2,1)} %refs_1_.1, ...), custom_call_target="tpu_custom_call" | custom-call | tf_op jit(solution)/shard_map/gather_weights/pallas_call | solution.py:217
  112.7 0.9 convert_bitcast_fusion.1
  113.6 0.2 copy.84
  113.8 4.7 %fusion.17.v.refs_8_ = bf16[8,768,128]{2,1,0:T(8,128)(2,1)} fusion(f32[8,128]{1,0:T(8,128)S(1)} %get-tuple-element.63, bf16[8,1024,384]{2,1,0:T(8,128)(2,1)} %get-tuple-element.33.refs_12_, bf16[768,1024]{1,0:T(8,128)(2,1)S(1)} %get-tuple-element.60), kind=kOutput, calls=%fused_computation.31 | convolution fusion | flops 1612185600 | bytes 5246976 | tf_op jit(solution)/shard_map/td,gde->gte/dot_general | solution.py:916
  118.5 0.7 fusion.37.q.refs_6_
  119.2 0.0 copy-start.16
  119.3 1.8 fusion.24.k.refs_7_
  121.1 0.1 pad_dynamic-slice_fusion.1
  121.2 0.2 convert_select_fusion.1.dist
  121.5 10.1 %attend.1.refs_10_ = bf16[8,256,128]{2,1,0:T(8,128)(2,1)S(1)} custom-call(f32[16]{0:T(128)S(1)} %multiply_exponential_fusion.slopes.refs_4_, f32[256,768]{1,0:T(8,128)S(1)} %convert_select_fusion.1.dist, bf16[8,256,128]{2,1,0:T(8,128)(2,1)S(1)} %fusion.37.q.refs_6_, bf16[8,768,128]{2,1,0:T(8,128)(2,1)S(1)} %fusion.24.k.refs_7_, ...), custom_call_target="tpu_custom_call" | custom-call | tf_op jit(solution)/shard_map/attend/pallas_call | solution.py:825
  131.7 0.6 fusion.53
  132.3 0.0 copy-done.19
  132.3 1.1 copy-done.6
  133.4 0.8 fusion.57
  134.3 0.2 multiply_reduce_fusion.5
  134.6 1.0 add_convert_fusion.3.own
  135.6 18.5 %share_second.1 = bf16[2,256,1024]{2,1,0:T(8,128)(2,1)} custom-call(bf16[256,1024]{1,0:T(8,128)(2,1)} %add_convert_fusion.3.own), custom_call_target="tpu_custom_call" | custom-call | tf_op jit(solution)/shard_map/share_second/pallas_call | solution.py:591
  154.1 6.9 %fusion.58 = f32[4,512,512]{1,2,0:T(8,128)} fusion(bf16[512,1024,1]{1,0,2:T(8,128)(2,1)} %bitcast.132, bf16[4,1024,512]{2,1,0:T(8,128)(2,1)} %get-tuple-element.32), kind=kOutput, calls=%fused_computation.115 | convolution fusion | flops 2147483648 | bytes 9437184 | tf_op jit(solution)/shard_map/td,zdf->ztf/dot_general | solution.py:928
  161.1 8.4 %convert_reduce_fusion = (f32[4,512]{1,0:T(4,128)S(1)}, bf16[4,512,512]{2,1,0:T(8,128)(2,1)S(1)}) fusion(f32[4,512,512]{1,2,0:T(8,128)} %fusion.58, f32[4,512]{1,0:T(4,128)S(1)} %bitcast.143, bf16[4,512,1024]{2,1,0:T(8,128)(2,1)} %get-tuple-element.31, bf16[2048,1024]{1,0:T(8,128)(2,1)} %param.29, s32[]{:T(128)S(6)} %select_n.49), kind=kOutput, calls=%fused_computation.12 | convolution fusion | flops 2170550272 | bytes 11550724 | tf_op jit(solution)/shard_map/td,zfd->ztf/dot_general | solution.py:932
  169.6 3.3 bitcast_convert_fusion
  172.9 17.6 %sum_second.1 = bf16[2,256,1024]{2,1,0:T(8,128)(2,1)} custom-call(bf16[2,256,1024]{2,1,0:T(8,128)(2,1)} %bitcast.134), custom_call_target="tpu_custom_call" | custom-call | tf_op jit(solution)/shard_map/sum_second/pallas_call | solution.py:591
  190.5 2.0 convert_reduce_fusion.1
  192.4 0.5 multiply_reduce_fusion.1
  192.9 0.0 copy-done.24
  193.0 6.3 %fusion.54 = f32[512,1024,1]{1,0,2:T(8,128)} fusion(bf16[4,512,1024]{2,1,0:T(8,128)(2,1)S(1)} %copy-done.24, f32[4,512,512]{1,2,0:T(8,128)} %fusion.58, f32[4,512]{1,0:T(4,128)S(1)} %bitcast.144), kind=kOutput, calls=%fused_computation.111 | convolution fusion | flops 2157969408 | bytes 10493952 | tf_op jit(solution)/shard_map/ztf,zfd->td/dot_general | solution.py:931
  199.3 3.0 fusion.55
  202.3 0.9 convert_element_type.136.refs_9_
  203.2 1.1 convert_element_type.129.refs_2_
  204.3 6.7 %convolution_convert_fusion.refs_1_ = bf16[4,512,1024]{2,1,0:T(8,128)(2,1)} fusion(bf16[2048,1024]{1,0:T(8,128)(2,1)} %param.29, s32[]{:T(128)S(6)} %select_n.49, f32[4,512,512]{1,2,0:T(8,128)S(1)} %copy-done.27, f32[4,512]{1,0:T(4,128)S(1)} %bitcast.145), kind=kOutput, calls=%fused_computation.19 | convolution fusion | flops 2160066560 | bytes 9445380 | tf_op jit(solution)/shard_map/ztf,td->zfd/dot_general | solution.py:935
  211.0 4.5 convert_bitcast_fusion.refs_0_
  215.5 2.6 copy.66.refs_13_
  218.1 1.1 convert_select_fusion.refs_5_
  219.2 117.2 %finish_mlp.1 = (bf16[1024,512]{1,0:T(8,128)(2,1)}, bf16[512,1024]{1,0:T(8,128)(2,1)}, bf16[8,256,1024]{2,1,0:T(8,128)(2,1)}, bf16[8,1024,384]{2,1,0:T(8,128)(2,...) custom-call(bf16[4,1024,512]{2,1,0:T(8,128)(2,1)} %convert_bitcast_fusion, ...), custom_call_target="tpu_custom_call" | custom-call | tf_op jit(solution)/shard_map/finish_mlp/pallas_call | solution.py:544
  336.5 1.9 multiply_reduce_fusion.2
  338.5 0.8 slice.104
  339.2 0.8 slice.105
  340.0 0.1 select_bitcast_fusion
  340.1 2.6 add_convert_fusion.2.refs_2_
  342.8 105.2 %finish_attn.1 = (bf16[1024,384]{1,0:T(8,128)(2,1)}, bf16[128,1024]{1,0:T(8,128)(2,1)}, bf16[8,256,1024]{2,1,0:T(8,128)(2,1)}, f32[96,128]{1,0:T(8,128)}) custom-call(bf16[8,1024,384]{2,1,0:T(8,128)(2,1)} %get-tuple-element.37.refs_0_, bf16[8,128,1024]{2,1,0:T(8,128)(2,1)} %get-tuple-element.38.refs_1_, bf16[256,1024]{1,0:T(8,128)(2,1)} %add_convert_fusion.2.refs_2_, ...), custom_call_target="tpu_custom_call" | custom-call | tf_op jit(solution)/shard_map/finish_attn/pallas_call | solution.py:544
  448.0 1.4 slice_bitcast_fusion.2
  449.4 0.1 reshape.196
  449.4 0.1 reshape.197
  449.5 0.6 pad_maximum_fusion
  450.2 1.5 copy.67
  451.7 1.2 copy.68
  452.9 0.8 convert_element_type.139
  453.7 0.7 slice.118
  454.5 0.6 constant_dynamic-slice_fusion
  455.1 3.1 convert_element_type.140
  458.2 1.6 convert_element_type.141
  459.8 2.1 copy.97
  461.9 1.6 copy-done.10
  463.5 2.0 copy.98
  (95 shorter events, 0.3 us)
Async XLA Ops:
  0.7 2.3 copy-start.4
  0.7 2.9 copy-start.17
  0.7 3.0 copy-start.18
  3.6 2.4 copy-start.13
  3.7 3.8 copy-start.26
  3.7 4.0 copy-start.23
  6.1 113.2 %copy-start.7 = (bf16[768,1024]{1,0:T(8,128)(2,1)}, bf16[768,1024]{1,0:T(8,128)(2,1)S(1)}, u32[]{:S(2)}) copy-start(bf16[768,1024]{1,0:T(8,128)(2,1)S(1)} %get-tuple-element.60) | copy-start | bytes 4718596
  113.6 4.9 %slice-start = ((s8[6291456]{0:T(1024)(128)(4,1)}), s8[4194304]{0:T(1024)(128)(4,1)S(1)}, s32[]{:S(2)}) async-start(s8[6291456]{0:T(1024)(128)(4,1)} %bitcast.124), calls=%async_computation | async-start | bytes 8388608
  113.8 4.7 %slice-start.1 = ((s8[6291456]{0:T(1024)(128)(4,1)}), s8[2097152]{0:T(1024)(128)(4,1)S(1)}, s32[]{:S(2)}) async-start(s8[6291456]{0:T(1024)(128)(4,1)} %bitcast.124), calls=%async_computation.1 | async-start | bytes 4194304
  119.2 2.2 copy-start.2
  119.2 1.8 copy-start.16
  121.0 11.2 %copy-start = (bf16[8,768,128]{2,1,0:T(8,128)(2,1)}, bf16[8,768,128]{2,1,0:T(8,128)(2,1)S(1)}, u32[]{:S(2)}) copy-start(bf16[8,768,128]{2,1,0:T(8,128)(2,1)S(1)} %fusion.24.k.refs_7_) | copy-start | bytes 4718596
  121.1 10.6 %copy-start.5 = (bf16[2048,1024]{1,0:T(8,128)(2,1)S(1)}, bf16[2048,1024]{1,0:T(8,128)(2,1)}, u32[]{:S(2)}) copy-start(bf16[2048,1024]{1,0:T(8,128)(2,1)} %param.15) | copy-start | bytes 12582916
  121.4 10.8 %copy-start.3 = (f32[16]{0:T(128)}, f32[16]{0:T(128)S(1)}, u32[]{:S(2)}) copy-start(f32[16]{0:T(128)S(1)} %multiply_exponential_fusion.slopes.refs_4_) | copy-start | bytes 196
  131.6 2.6 copy-start.1
  131.6 0.7 copy-start.19
  131.6 1.8 copy-start.6
  132.3 2.3 copy-start.20
  132.3 2.3 copy-start.21
  161.1 8.5 %copy-start.25 = (bf16[4,1024,512]{2,1,0:T(8,128)(2,1)S(1)}, bf16[4,1024,512]{2,1,0:T(8,128)(2,1)}, u32[]{:S(2)}) copy-start(bf16[4,1024,512]{2,1,0:T(8,128)(2,1)} %get-tuple-element.32) | copy-start | bytes 12582916
  169.5 3.4 copy-start.28
  190.5 2.5 copy-start.24
  193.0 6.3 %copy-start.22 = (bf16[1024]{0:T(1024)(128)(2,1)S(1)}, bf16[1024]{0:T(1024)(128)(2,1)}, u32[]{:S(2)}) copy-start(bf16[1024]{0:T(1024)(128)(2,1)} %param.28) | copy-start | bytes 6148
  199.3 3.9 copy-start.8
  199.3 5.1 %copy-start.27 = (f32[4,512,512]{1,2,0:T(8,128)S(1)}, f32[4,512,512]{1,2,0:T(8,128)}, u32[]{:S(2)}) copy-start(f32[4,512,512]{1,2,0:T(8,128)} %fusion.58) | copy-start | bytes 12582916
  204.3 6.7 %copy-start.12 = (bf16[2,256,1024]{2,1,0:T(8,128)(2,1)S(1)}, bf16[2,256,1024]{2,1,0:T(8,128)(2,1)}, u32[]{:S(2)}) copy-start(bf16[2,256,1024]{2,1,0:T(8,128)(2,1)} %share_second.1) | copy-start | bytes 3145732
  204.3 6.7 %copy-start.29 = (bf16[4,512,512]{2,1,0:T(8,128)(2,1)S(1)}, bf16[4,512,512]{2,1,0:T(8,128)(2,1)}, u32[]{:S(2)}) copy-start(bf16[4,512,512]{2,1,0:T(8,128)(2,1)} %copy-done.28) | copy-start | bytes 6291460
  340.1 2.7 copy-start.15
  448.0 4.9 %copy-start.14 = (bf16[128,1024]{1,0:T(8,128)(2,1)S(1)}, bf16[128,1024]{1,0:T(8,128)(2,1)}, u32[]{:S(2)}) copy-start(bf16[128,1024]{1,0:T(8,128)(2,1)} %get-tuple-element.45) | copy-start | bytes 786436
  450.2 8.0 %copy-start.11 = (bf16[512,1024]{1,0:T(8,128)(2,1)S(1)}, bf16[512,1024]{1,0:T(8,128)(2,1)}, u32[]{:S(2)}) copy-start(bf16[512,1024]{1,0:T(8,128)(2,1)} %get-tuple-element.47) | copy-start | bytes 3145732
  454.5 5.3 %copy-start.9 = (bf16[8,256,1024]{2,1,0:T(8,128)(2,1)S(1)}, bf16[8,256,1024]{2,1,0:T(8,128)(2,1)}, u32[]{:S(2)}) copy-start(bf16[8,256,1024]{2,1,0:T(8,128)(2,1)} %get-tuple-element.36) | copy-start | bytes 12582916
  459.8 3.7 copy-start.10

commit v5 on v4

v5 whole, which is shorter than its diff:
```python
import functools
import math

import jax
import jax.numpy as jnp
from jax import lax
from jax.experimental import pallas as pl
from jax.experimental.pallas import tpu as pltpu
from jax.sharding import PartitionSpec as P

MESH = pl.DeviceIdType.MESH
ANY = pl.BlockSpec(memory_space=pl.ANY)
VM = pl.BlockSpec(memory_space=pltpu.VMEM)


def grid_of(n_tensor):
    lines = min(4, n_tensor)
    return lines, n_tensor // lines


def where_am_i(n_tensor):
    lines, wide = grid_of(n_tensor)
    dp, t = lax.axis_index("dp"), lax.axis_index("tensor")
    return dp, t, t // wide, t % wide


def remote(src, dst, send, recv, peer):
    return pltpu.make_async_remote_copy(
        src_ref=src, dst_ref=dst, send_sem=send, recv_sem=recv, device_id=peer, device_id_type=MESH
    )


def when(condition, body):
    pl.when(condition)(body)


def greet(peers):
    barrier = pltpu.get_barrier_semaphore()
    for ok, peer in peers:
        @pl.when(ok)
        def _():
            pl.semaphore_signal(barrier, inc=1, device_id=peer, device_id_type=MESH)
    pl.semaphore_wait(barrier, sum(jnp.int32(ok) for ok, peer in peers))


def neighbours(n_tensor, use_y=True, use_x=True, use_core=True):
    lines, wide = grid_of(n_tensor)
    dp, t, z, y = where_am_i(n_tensor)
    out = [(z > 0, (dp, t - wide)), (z < lines - 1, (dp, t + wide))]
    if use_y:
        out += [(y > 0, (dp, t - 1)), (y < wide - 1, (dp, t + 1))]
    if use_x:
        out.append((dp >= 0, (dp ^ 2, t)))
    if use_core:
        out.append((dp >= 0, (dp ^ 1, t)))
    return out


def front_kernel(n_tensor, heads, n_attn, n_mlp, *refs):
    lines, wide = grid_of(n_tensor)
    dp, t, z, y = where_am_i(n_tensor)
    n = n_attn + n_mlp
    refs = list(refs)

    def take(count):
        got, refs[:] = refs[:count], refs[count:]
        return got

    own, inputs = take(n), take(front_inputs)
    full, outputs = take(n), take(front_outputs)
    z_send, z_recv, y_send, y_recv, x_send, x_recv, c_send, c_recv, l_sem = take(9)
    before, work, after, share, share_end = front_program(n_tensor, heads, inputs, full[:n_attn], outputs, refs)
    quad = dp % 4

    items, group_of = [], ([], [])
    for a in range(n):
        size = own[a].shape[0]
        split = a < n_attn and size % 128 == 0
        for item in [(a, 0, size // 8, True), (a, size // 2, size // 4, False)] if split else [(a, 0, size // 4, True)]:
            group_of[a >= n_attn].append(len(items))
            items.append(item)

    def slot(i, zz, yy):
        return zz * wide + yy if items[i][0] < n_attn else zz

    def piece(ref, i, q):
        a, first, size, by_x = items[i]
        return ref.at[pl.ds(pl.multiple_of(first + (q if by_x else q % 2) * size, size), size)]

    def block(i, zz, yy, q):
        return piece(full[items[i][0]].at[slot(i, zz, yy)], i, q)

    peers = neighbours(n_tensor)
    if wide > 2:
        peers += [(yy != y, (dp, z * wide + yy)) for yy in range(wide)]
    greet(peers)
    local = [pltpu.make_async_copy(own[a], full[a].at[z * wide + y if a < n_attn else z], l_sem.at[a]) for a in range(n)]
    for c in local:
        c.start()
    up, down = (dp, t + wide), (dp, t - wide)
    z_has = ((z < lines - 1), (z > 0))
    y_has = ((y < wide - 1), (y > 0))

    def z_copy(a, zz, side, mine=False):
        src = piece(own[items[a][0]], a, quad) if mine else block(a, zz, y, quad)
        return remote(src, block(a, zz, y, quad), z_send.at[side, a, zz], z_recv.at[side, a, zz], (up, down)[side])

    def y_copy(a, zz, yy, side, mine=False):
        src = piece(own[items[a][0]], a, quad) if mine else block(a, zz, yy, quad)
        peer = ((dp, t + 1), (dp, t - 1))[side]
        return remote(src, block(a, zz, yy, quad), y_send.at[side, a, zz, yy], y_recv.at[side, a, zz, yy], peer)

    def x_copy(a, zz, yy, q):
        return remote(block(a, zz, yy, q), block(a, zz, yy, q), x_send.at[a, zz, yy], x_recv.at[a, zz, yy], (dp ^ 2, t))

    def c_copy(a, zz, yy, q, hop):
        return remote(
            block(a, zz, yy, q), block(a, zz, yy, q), c_send.at[hop, a, zz, yy], c_recv.at[hop, a, zz, yy], (dp ^ 1, t)
        )

    def spread(a, zz, yy):
        if items[a][3]:
            x_copy(a, zz, yy, quad).start()
        c_copy(a, zz, yy, quad, 0).start()

    def arrays(group):
        return group_of[group]

    def y_start(zz, yy, side, mine=False):
        @pl.when(y_has[side])
        def _():
            for a in arrays(0):
                y_copy(a, zz, yy, side, mine).start()

    def z_begin(group):
        for side in range(2):
            @pl.when(z_has[side])
            def _():
                for a in arrays(group):
                    z_copy(a, z, side, True).start()

    def z_step(group, k):
        for side in range(2):
            zz = z - k if side == 0 else z + k

            @pl.when((zz >= 0) if side == 0 else (zz < lines))
            def _():
                for a in arrays(group):
                    z_copy(a, zz, side).wait_recv()

                @pl.when(z_has[side])
                def _():
                    for a in arrays(group):
                        z_copy(a, zz, side).start()

                if group == 0:
                    for s in range(2):
                        y_start(zz, y, s)
                for a in arrays(group):
                    spread(a, zz, y)

    def others(group, zs, body):
        for zz in zs:
            for yy in range(wide) if group == 0 else [y]:
                @pl.when((zz != z) | (yy != y))
                def _():
                    body(zz, yy)

    def pass_on(group, zs):
        def body(zz, yy):
            for a in arrays(group):
                if items[a][3]:
                    x_copy(a, zz, yy, quad ^ 2).wait_recv()
                    c_copy(a, zz, yy, quad ^ 2, 1).start()

        others(group, zs, body)

    def arrived(group):
        def body(zz, yy):
            for a in arrays(group):
                for hop in range(1 + items[a][3]):
                    c_copy(a, zz, yy, quad ^ (1 + 2 * hop), hop).wait_recv()

        others(group, range(lines), body)

    def settle(group):
        def body(zz, yy):
            for a in arrays(group):
                for hop in range(1 + items[a][3]):
                    c_copy(a, zz, yy, quad ^ (2 * hop), hop).wait_send()
                if items[a][3]:
                    x_copy(a, zz, yy, quad).wait_send()

        others(group, range(lines), body)
        for side in range(2):
            for k in range(lines):
                zz = z - k if side == 0 else z + k

                @pl.when(z_has[side] & (zz >= 0) & (zz < lines))
                def _():
                    for a in arrays(group):
                        z_copy(a, zz, side).wait_send()

    z_begin(0)
    for side in range(2):
        y_start(z, y, side, True)
    before()
    for k in range(1, lines):
        z_step(0, k)
    z_begin(1)
    for m in range(1, wide):
        for side in range(2):
            yy = y - m if side == 0 else y + m

            @pl.when((yy >= 0) if side == 0 else (yy < wide))
            def _():
                for zz in range(lines):
                    for a in arrays(0):
                        y_copy(a, zz, yy, side).wait_recv()
                    if m < wide - 1:
                        y_start(zz, yy, side)
                    for a in arrays(0):
                        spread(a, zz, yy)
    z_step(1, 1)
    for zz in range(lines):
        pass_on(0, [zz])
        if zz == lines // 2:
            z_step(1, 2)
    arrived(0)
    for c in local:
        c.wait()
    steps = [functools.partial(z_step, 1, k) for k in range(3, lines)]
    steps += [functools.partial(pass_on, 1, [zz]) for zz in range(lines)]

    @pl.loop(0, n_tensor)
    def _(p):
        work(p)
        for k in range(n_tensor):
            if steps:
                when(p == k, steps.pop(0))

    after()
    share()
    for step in steps:
        step()
    share_end()
    arrived(1)
    settle(0)
    settle(1)
    for side in range(2):
        @pl.when(y_has[side])
        def _():
            for zz in range(lines):
                for m in range(wide):
                    yy = y - m if side == 0 else y + m

                    @pl.when((yy >= 0) if side == 0 else (yy < wide))
                    def _():
                        for a in arrays(0):
                            y_copy(a, zz, yy, side).wait_send()


def front(n_tensor, attn, mlp, slopes, dist, near, rows):
    lines, wide = grid_of(n_tensor)
    n = len(attn) + len(mlp)
    arrays = list(attn) + list(mlp)
    span, d = near.shape
    chunk = dist.shape[0]
    lanes = attn[0].shape[1] // 3
    shape, low, f32 = jax.ShapeDtypeStruct, jnp.bfloat16, jnp.float32
    outs = [shape(((n_tensor if i < len(attn) else lines),) + a.shape, a.dtype) for i, a in enumerate(arrays)]
    outs += [
        shape((n_tensor, chunk, lanes), low), shape((n_tensor, span, lanes), low), shape((n_tensor, span, lanes), low),
        shape((n_tensor, chunk, lanes), low), shape((chunk, d), f32), shape((wide, chunk, d), low), shape((d, span), low),
    ]
    dma = pltpu.SemaphoreType.DMA
    return pl.pallas_call(
        functools.partial(front_kernel, n_tensor, slopes.shape[0] // n_tensor, len(attn), len(mlp)),
        out_shape=outs,
        in_specs=[VM] * n + [pl.BlockSpec(memory_space=pltpu.SMEM)] + [VM] * (front_inputs - 1),
        out_specs=[VM] * len(attn) + [ANY] * len(mlp) + [VM] * front_outputs,
        scratch_shapes=[dma((2, 2 * n, lines))] * 2
        + [dma((2, 2 * n, lines, wide))] * 2
        + [dma((2 * n, lines, wide))] * 2
        + [dma((2, 2 * n, lines, wide))] * 2
        + [dma((n,))]
        + [pltpu.VMEM((span, d), low), dma((wide,)), dma((wide,))],
        compiler_params=pltpu.CompilerParams(collective_id=0, has_side_effects=True, vmem_limit_bytes=60 * 2**20),
        name="front",
    )(*arrays, slopes, dist, near, rows)


def add_rows(dst, terms):
    rows = dst.shape[0]
    step = 32 if rows % 32 == 0 else rows

    @pl.loop(0, rows // step)
    def _(i):
        part = pl.ds(pl.multiple_of(i * step, step), step)
        total = terms[0][part].astype(jnp.float32)
        for term in terms[1:]:
            total = total + term[part].astype(jnp.float32)
        dst[part] = total.astype(dst.dtype)


def pair_sums(n_tensor, terms, sums, from_c, to_x, from_x, c_send, c_recv, x_send, x_recv):
    dp, t, z, y = where_am_i(n_tensor)
    quad = dp % 4
    side_x, core = quad // 2, quad % 2
    arrays = range(len(terms))

    def quarter(a, s, q):
        rows = terms[a].shape[1] // 4
        return terms[a].at[s, pl.ds(pl.multiple_of(q * rows, rows), rows)]

    def c_copy(a, s, h):
        return remote(
            quarter(a, s, h * 2 + 1 - core), from_c[a].at[s, h], c_send.at[a, s, h], c_recv.at[a, s, h], (dp ^ 1, t)
        )

    def x_copy(a, s):
        return remote(to_x[a].at[s], from_x[a].at[s], x_send.at[a, s], x_recv.at[a, s], (dp ^ 2, t))

    def start(s):
        for a in arrays:
            for h in range(2):
                c_copy(a, s, h).start()

    def core_stage(s):
        for a in arrays:
            for h in range(2):
                c_copy(a, s, h).wait_recv()
            add_rows(to_x[a].at[s], [quarter(a, s, (1 - side_x) * 2 + core), from_c[a].at[s, 1 - side_x]])
            x_copy(a, s).start()
            add_rows(sums[a].at[s], [quarter(a, s, quad), from_c[a].at[s, side_x]])

    def x_stage(s):
        for a in arrays:
            x_copy(a, s).wait_recv()
            add_rows(sums[a].at[s], [sums[a].at[s], from_x[a].at[s]])

    def settle(s):
        for a in arrays:
            for h in range(2):
                c_copy(a, s, h).wait_send()
            x_copy(a, s).wait_send()

    return start, core_stage, x_stage, settle


def pair_scratch(shapes, slots):
    low, dma = jnp.bfloat16, pltpu.SemaphoreType.DMA
    n = len(shapes)
    quarters = [(r // 4, c) for r, c in shapes]
    return (
        [pltpu.VMEM((slots, 2) + q, low) for q in quarters]
        + [pltpu.VMEM((slots,) + q, low) for q in quarters] * 2
        + [dma((n, slots, 2))] * 2 + [dma((n, slots))] * 2
    )


def doubling_peers(n_tensor):
    dp, t, z, y = where_am_i(n_tensor)
    bits = lambda size: [1 << i for i in range((size - 1).bit_length())]
    return [(dp ^ b, t) for b in bits(lax.axis_size("dp"))] + [(dp, t ^ b) for b in bits(n_tensor)]


def doubling_program(n_tensor, own, out, total, got, send, recv):
    peers = doubling_peers(n_tensor)

    def step(i):
        return remote(total.at[i], got.at[i], send.at[i], recv.at[i], peers[i])

    def begin():
        total[0] = own[...]
        step(0).start()

    def advance(i):
        step(i).wait_recv()
        if i + 1 < len(peers):
            total[i + 1] = total[i] + got[i]
            step(i + 1).start()
        else:
            out[...] = total[i] + got[i]

    def settle():
        for i in range(len(peers)):
            step(i).wait_send()

    return [begin] + [functools.partial(advance, i) for i in range(len(peers))] + [settle]


def finish_kernel(n_tensor, n_attn, n_mlp, with_vectors, pull, *refs):
    lines, wide = grid_of(n_tensor)
    dp, t, z, y = where_am_i(n_tensor)
    n = n_attn + n_mlp
    refs = list(refs)

    def take(count):
        got, refs[:] = refs[:count], refs[count:]
        return got

    terms, rows_own = take(n), take(1)
    vec_own = take(1)[0] if with_vectors else None
    pull_in = take(pull_inputs) if pull else []
    final, rows_full = take(n), take(1)
    vec_out = take(1)[0] if with_vectors else None
    pull_out = take(pull_outputs) if pull else []
    acc, from_y, from_z, whole = (take(n) for i in range(4))
    y_send, y_recv, z_send, z_recv, q_send, q_recv = take(6)
    rows_steps = rows_program(n_tensor, rows_own, rows_full, *take(5))
    vec_steps = doubling_program(n_tensor, vec_own, vec_out, *take(4)) if with_vectors else []
    if pull:
        work, pull_peers, pull_first, pull_last = pull_program(n_tensor, pull, pull_in, pull_out, refs)
    quad = dp % 4
    core_peer, x_peer = (dp ^ 1, t), (dp ^ 2, t)
    lines_order = [i // 2 if i % 2 else lines - 1 - i // 2 for i in range(lines)]
    attn, order = list(range(n_attn)), list(range(n))

    def index(a, zz, yy):
        return zz * wide + yy if a < n_attn else zz

    def quarter(ref, q):
        rows = ref.shape[0] // 4
        return ref.at[pl.ds(pl.multiple_of(q * rows, rows), rows)]

    def y_copy(a, zz, yy, side):
        peer = ((dp, t + 1), (dp, t - 1))[side]
        lane = zz * wide + yy
        return remote(acc[a].at[lane], from_y[a].at[side, lane], y_send.at[side, a, lane], y_recv.at[side, a, lane], peer)

    def z_copy(a, zz, side):
        peer = ((dp, t + wide), (dp, t - wide))[side]
        return remote(
            acc[a].at[index(a, zz, y)], from_z[a].at[side, zz], z_send.at[side, a, zz], z_recv.at[side, a, zz], peer
        )

    def y_begin(zz):
        for m in range(wide):
            yy = (y + 1 + m) % wide
            for a in attn:
                lane = zz * wide + yy
                add_rows(acc[a].at[lane], [terms[a].at[lane]])
                when((y == 0) & (yy > y), lambda: y_copy(a, zz, yy, 0).start())
                when((y == wide - 1) & (yy < y), lambda: y_copy(a, zz, yy, 1).start())

    def y_stage(zz):
        for a in attn:
            for k in range(wide):
                for side, yy in ((0, wide - 1 - k), (1, k)):
                    @pl.when(((yy >= y) & (y > 0)) if side == 0 else ((yy <= y) & (y < wide - 1)))
                    def _():
                        lane = zz * wide + yy
                        y_copy(a, zz, yy, side).wait_recv()
                        add_rows(acc[a].at[lane], [acc[a].at[lane], from_y[a].at[side, lane]])
                        when(yy != y, lambda: y_copy(a, zz, yy, side).start())

    def z_round(r):
        for side in range(2):
            zz = lines - 1 - r + z if side == 0 else z - (lines - 1 - r)

            @pl.when((zz < lines) & (zz >= 0))
            def _():
                @pl.when((z > 0) if side == 0 else (z < lines - 1))
                def _():
                    for a in order:
                        s = index(a, zz, y)
                        z_copy(a, zz, side).wait_recv()
                        add_rows(acc[a].at[s], [acc[a].at[s], from_z[a].at[side, zz]])

                if r < lines - 1:
                    for a in order:
                        z_copy(a, zz, side).start()

    def q_copy(a, q, hop, peer):
        return remote(quarter(whole[a], q), quarter(whole[a], q), q_send.at[hop, a], q_recv.at[hop, a], peer)

    def home(a):
        add_rows(quarter(whole[a], quad), [acc[a].at[index(a, z, y)]])
        q_copy(a, quad, 0, x_peer).start()
        q_copy(a, quad, 1, core_peer).start()

    def widen(a, q):
        add_rows(quarter(final[a], q), [quarter(whole[a], q)])

    def aside():
        if len(rows_steps) > 1:
            rows_steps.pop(0)()
        if len(vec_steps) > 1:
            vec_steps.pop(0)()

    def late(r):
        aside()
        z_round(r)

    peers = neighbours(n_tensor)
    if pull:
        peers += pull_peers
    if with_vectors:
        peers += [(dp >= 0, peer) for peer in doubling_peers(n_tensor)]
    greet(peers)
    for zz in lines_order:
        y_begin(zz)
        for a in order[n_attn:]:
            add_rows(acc[a].at[zz], [terms[a].at[zz]])
    if not attn:
        z_round(0)
    rows_steps.pop(0)()
    if with_vectors:
        vec_steps.pop(0)()
    if attn:
        for zz in lines_order:
            y_stage(zz)
            if with_vectors:
                vec_steps.pop(0)()
        z_round(0)
    steps = [functools.partial(late, r) for r in range(1, lines)]
    if pull:
        @pl.loop(0, n_tensor)
        def _(p):
            work(p)
            for k in (n_tensor // 2, n_tensor - 1):
                when(p == k, steps.pop(0))

        pull_first()
    for step in steps:
        step()
    for a in order:
        home(a)
    aside()
    for a in order:
        widen(a, quad)
        q_copy(a, quad ^ 2, 0, x_peer).wait_recv()
        q_copy(a, quad ^ 2, 2, core_peer).start()
        widen(a, quad ^ 2)
    if pull:
        pull_last()
    while rows_steps:
        rows_steps.pop(0)()
    while vec_steps:
        vec_steps.pop(0)()
    for a in order:
        q_copy(a, quad ^ 1, 1, core_peer).wait_recv()
        widen(a, quad ^ 1)
        q_copy(a, quad ^ 3, 2, core_peer).wait_recv()
        widen(a, quad ^ 3)
        q_copy(a, quad, 0, x_peer).wait_send()
        q_copy(a, quad, 1, core_peer).wait_send()
        q_copy(a, quad ^ 2, 2, core_peer).wait_send()
        if a < n_attn:
            for zz in range(lines):
                for yy in range(wide):
                    when(yy > y, lambda: y_copy(a, zz, yy, 0).wait_send())
                    when(yy < y, lambda: y_copy(a, zz, yy, 1).wait_send())
        for zz in range(lines):
            when(zz > z, lambda: z_copy(a, zz, 0).wait_send())
            when(zz < z, lambda: z_copy(a, zz, 1).wait_send())


def finish(n_tensor, attn, mlp, rows, vectors, cid, name, pull=None):
    lines, wide = grid_of(n_tensor)
    arrays = list(attn) + list(mlp)
    n = len(arrays)
    vm, dma = pltpu.VMEM, pltpu.SemaphoreType.DMA
    low, f32 = jnp.bfloat16, jnp.float32
    quarters = [a.shape[1:] for a in arrays]
    each = lambda lead: [vm(lead(a, i) + q, low) for i, (a, q) in enumerate(zip(arrays, quarters))]
    steps = (lax.axis_size("dp") - 1).bit_length() + (n_tensor - 1).bit_length()
    scratch = (
        each(lambda a, i: (a.shape[0],))
        + each(lambda a, i: (2, n_tensor) if i < len(attn) else (1, 1))
        + each(lambda a, i: (2, lines))
        + [vm((4 * q[0], q[1]), low) for q in quarters]
    )
    sems = (
        [dma((2, max(1, len(attn)), n_tensor))] * 2 + [dma((2, n, lines))] * 2 + [dma((3, n))] * 2
        + [dma((2, 1, lines))] * 2 + [dma((2, 1, lines, wide))] * 2 + [dma((1,))]
    )
    inputs, in_specs = arrays + [rows], [VM] * n + [VM]
    out_shape = [jax.ShapeDtypeStruct((4 * q[0], q[1]), f32) for q in quarters]
    out_shape.append(jax.ShapeDtypeStruct((n_tensor,) + rows.shape, low))
    out_specs = [VM] * n + [ANY]
    if vectors is not None:
        inputs, in_specs = inputs + [vectors], in_specs + [VM]
        out_shape.append(jax.ShapeDtypeStruct(vectors.shape, vectors.dtype))
        out_specs.append(VM)
        sems += [vm((steps,) + vectors.shape, jnp.float32)] * 2 + [dma((steps,))] * 2
    heads = 0
    if pull is not None:
        heads = pull[0].shape[0] // n_tensor
        inputs, in_specs = inputs + list(pull), in_specs + [pl.BlockSpec(memory_space=pltpu.SMEM)] + [VM] * (pull_inputs - 1)
        shapes, more = pull_shapes(n_tensor, pull)
        out_shape += shapes
        out_specs += [VM] * pull_outputs
        sems += more
    out = pl.pallas_call(
        functools.partial(
            finish_kernel, n_tensor, len(attn), len(mlp), vectors is not None, heads
        ),
        out_shape=out_shape,
        in_specs=in_specs,
        out_specs=out_specs,
        scratch_shapes=scratch + sems,
        compiler_params=pltpu.CompilerParams(collective_id=cid, has_side_effects=True, vmem_limit_bytes=63 * 2**20),
        name=name,
    )(*inputs)
    sums = out[:n]
    if lax.axis_size("dp") > 4:
        sums = [lax.psum(s, "dp") * 0.25 for s in sums]
    return list(sums) + list(out[n:])


def mlp_kernel(n_tensor, *refs):
    lines, wide = grid_of(n_tensor)
    dp, t, z, y = where_am_i(n_tensor)
    second, cot, up, down, bias, base = refs[:6]
    sum_up, sum_down, up_sum, grad_second, output = refs[6:11]
    terms_up, terms_down = refs[11:13]
    pair, (feed, grad, second_t, share_own, share_got, s_send, s_recv) = refs[13:23], refs[23:]
    sums, terms = (sum_up, sum_down), (terms_up, terms_down)
    pair_start, core_stage, x_stage, pair_settle = pair_sums(
        n_tensor, terms, sums, pair[0:2], pair[2:4], pair[4:6], *pair[6:]
    )
    low, f32 = jnp.bfloat16, jnp.float32
    chunk = output.shape[0]
    tile = min(128, chunk)

    def share(kind, yy, slot):
        return remote(
            share_own.at[kind, yy], share_got.at[kind, slot], s_send.at[kind, yy], s_recv.at[kind, slot],
            (dp, z * wide + yy),
        )

    peers = [(dp >= 0, (dp ^ 1, t)), (dp >= 0, (dp ^ 2, t))]
    peers += [(yy != y, (dp, z * wide + yy)) for yy in range(wide)]
    greet(peers)
    feed[...] = jnp.zeros(feed.shape, f32)
    grad[...] = jnp.zeros(grad.shape, f32)

    @pl.loop(0, second.shape[0] // tile)
    def _(i):
        here = pl.ds(pl.multiple_of(i * tile, tile), tile)
        second_t[:, here] = second[here].T

    @pl.loop(0, lines)
    def _(s):
        upper = dot(second[...], up[s], NN) + bias[s, 0:1]
        hidden, slope = gelu_and_slope(upper)
        hidden = hidden.astype(low)
        grad_upper = (dot(cot[...], down[s], NT) * slope).astype(low)
        up_sum[s] = jnp.broadcast_to(jnp.sum(grad_upper.astype(f32), axis=0, keepdims=True), up_sum.shape[1:])
        terms_down[s] = dot(hidden, cot[...], TN).astype(low)
        terms_up[s] = dot(second_t[...], grad_upper, NN).astype(low)
        pair_start(s)
        feed[...] += dot(hidden, down[s], NN)
        grad[...] += dot(grad_upper, up[s], NT)
        when(s >= 1, lambda: core_stage(jnp.maximum(s - 1, 0)))

    for kind, whole in ((0, grad), (1, feed)):
        for yy in range(wide):
            @pl.when(yy != y)
            def _():
                add_rows(share_own.at[kind, yy], [whole.at[pl.ds(yy * chunk, chunk)]])
                share(kind, yy, y).start()
    core_stage(lines - 1)
    for s in range(lines - 1):
        x_stage(s)
    for kind, whole, out in ((0, grad, grad_second), (1, feed, output)):
        share_got[kind, y] = jnp.zeros((chunk, second.shape[1]), low)
        for yy in range(wide):
            when(yy != y, lambda: share(kind, yy, yy).wait_recv())
        mine = whole.at[pl.ds(pl.multiple_of(y * chunk, chunk), chunk)]
        add_rows(out, [mine] + [share_got.at[kind, yy] for yy in range(wide)] + ([base] if kind else []))
    x_stage(lines - 1)
    for yy in range(wide):
        for kind in range(2):
            when(yy != y, lambda: share(kind, yy, y).wait_send())
    for s in range(lines):
        pair_settle(s)


def mlp(n_tensor, second, cot, up, down, bias, base):
    lines, wide = grid_of(n_tensor)
    shape, vm, dma = jax.ShapeDtypeStruct, pltpu.VMEM, pltpu.SemaphoreType.DMA
    low, f32 = jnp.bfloat16, jnp.float32
    d, hidden = up.shape[1:]
    chunk = base.shape[0]
    quarters = [(d // 4, hidden), (hidden // 4, d)]
    return pl.pallas_call(
        functools.partial(mlp_kernel, n_tensor),
        out_shape=[shape((lines,) + q, low) for q in quarters]
        + [shape((lines, 8, hidden), f32), shape((chunk, d), f32), shape((chunk, d), low)],
        in_specs=[VM] * 6,
        out_specs=[VM] * 5,
        scratch_shapes=[vm(up.shape, low), vm(down.shape, low)] + pair_scratch([up.shape[1:], down.shape[1:]], lines)
        + [vm(second.shape, f32)] * 2 + [vm((d, second.shape[0]), low)] + [vm((2, wide, chunk, d), low)] * 2
        + [dma((2, wide))] * 2,
        compiler_params=pltpu.CompilerParams(collective_id=3, has_side_effects=True, vmem_limit_bytes=60 * 2**20),
        name="mlp",
    )(second, cot, up, down, bias, base)


def rows_program(n_tensor, own, full, z_send, z_recv, y_send, y_recv, l_sem):
    lines, wide = grid_of(n_tensor)
    dp, t, z, y = where_am_i(n_tensor)
    n = len(own)

    def z_copy(a, zz, side, mine=False):
        dst = full[a].at[zz * wide + y]
        peer = ((dp, t + wide), (dp, t - wide))[side]
        return remote(own[a] if mine else dst, dst, z_send.at[side, a, zz], z_recv.at[side, a, zz], peer)

    def y_copy(a, zz, yy, side, mine=False):
        dst = full[a].at[zz * wide + yy]
        peer = ((dp, t + 1), (dp, t - 1))[side]
        return remote(own[a] if mine else dst, dst, y_send.at[side, a, zz, yy], y_recv.at[side, a, zz, yy], peer)

    z_has = ((z < lines - 1), (z > 0))
    y_has = ((y < wide - 1), (y > 0))
    local = [pltpu.make_async_copy(own[a], full[a].at[t], l_sem.at[a]) for a in range(n)]

    def begin():
        for side in range(2):
            for a in range(n):
                when(z_has[side], lambda: z_copy(a, z, side, True).start())
                when(y_has[side], lambda: y_copy(a, z, y, side, True).start())
        for c in local:
            c.start()

    def along_z(k):
        for side in range(2):
            zz = z - k if side == 0 else z + k

            @pl.when((zz >= 0) & (zz < lines))
            def _():
                for a in range(n):
                    z_copy(a, zz, side).wait_recv()
                    when(z_has[side], lambda: z_copy(a, zz, side).start())
                    for s in range(2):
                        when(y_has[s], lambda: y_copy(a, zz, y, s).start())

    def along_y(m):
        for side in range(2):
            yy = y - m if side == 0 else y + m

            @pl.when((yy >= 0) & (yy < wide))
            def _():
                for zz in range(lines):
                    for a in range(n):
                        y_copy(a, zz, yy, side).wait_recv()
                        if m < wide - 1:
                            when(y_has[side], lambda: y_copy(a, zz, yy, side).start())

    def settle():
        for side in range(2):
            for k in range(lines):
                zz = z - k if side == 0 else z + k

                @pl.when(z_has[side] & (zz >= 0) & (zz < lines))
                def _():
                    for a in range(n):
                        z_copy(a, zz, side).wait_send()
            for m in range(wide):
                yy = y - m if side == 0 else y + m

                @pl.when(y_has[side] & (yy >= 0) & (yy < wide))
                def _():
                    for zz in range(lines):
                        for a in range(n):
                            y_copy(a, zz, yy, side).wait_send()
        for c in local:
            c.wait()

    return (
        [begin]
        + [functools.partial(along_z, k) for k in range(1, lines)]
        + [functools.partial(along_y, m) for m in range(1, wide)]
        + [settle]
    )


def dot(a, b, contract, **kwargs):
    return lax.dot_general(a, b, (contract, ((), ())), preferred_element_type=jnp.float32, **kwargs)


NN, NT, TN = ((1,), (0,)), ((1,), (1,)), ((0,), (0,))


def head_of_lane(shape, heads):
    return lax.broadcasted_iota(jnp.int32, shape, 1) // (shape[1] // heads)


def attend(heads, slope_of, dist, query, keys, values):
    scale = 1.0 / math.sqrt(query.shape[1] // heads)
    head = head_of_lane(query.shape, heads)
    out = jnp.zeros(query.shape, jnp.float32)
    for h in range(heads):
        masked = jnp.where(head == h, query * jnp.bfloat16(scale), jnp.bfloat16(0))
        scores = dot(masked, keys, NT) - slope_of(h) * dist[...]
        peak = jnp.max(scores, axis=1, keepdims=True)
        expo = jnp.exp(scores - peak)
        total = jnp.sum(expo, axis=1, keepdims=True)
        part = dot(expo.astype(jnp.bfloat16), values, NN) / total
        out = jnp.where(head == h, part, out)
    return out.astype(jnp.bfloat16)


front_inputs, front_outputs = 4, 7


def front_program(n_tensor, heads, ins, weights, outs, scratch):
    lines, wide = grid_of(n_tensor)
    dp, t, z, y = where_am_i(n_tensor)
    slopes, dist, near, rows = ins
    qkv_all, out_all, small_all = weights
    q, k, v, context, middle, second, normed_t = outs
    normed, s_send, s_recv = scratch
    chunk, lanes = q.shape[1:]
    span, d = near.shape
    behind = span - chunk
    low, f32 = jnp.bfloat16, jnp.float32
    tile = min(128, chunk)

    def before():
        @pl.loop(0, span // tile)
        def _(i):
            here = pl.ds(pl.multiple_of(i * tile, tile), tile)
            xhat, rate = normalized(near[here].astype(f32))
            value = (xhat * rows[0:1] + rows[1:2]).astype(low)
            normed[here] = value
            normed_t[:, here] = value.T

    def work(p):
        bias = small_all[p, 0:16, :].astype(f32)
        query = (dot(normed[behind:], qkv_all[p, :, :lanes], NN) + bias[0:1, :lanes]).astype(low)
        both = dot(normed[...], qkv_all[p, :, lanes:], NN)
        keys = both[:, :lanes].astype(low)
        values = (both[:, lanes:] + bias[1:2, :lanes]).astype(low)
        q[p], k[p], v[p] = query, keys, values
        context[p] = attend(heads, lambda h: slopes[p * heads + h], dist, query, keys, values)

    def after():
        @pl.loop(0, chunk // tile)
        def _(i):
            start = pl.multiple_of(i * tile, tile)
            here = pl.ds(start, tile)
            total = near[pl.ds(behind + start, tile)].astype(f32) + rows[4:5]
            for p in range(n_tensor):
                total = total + dot(context[p, here], out_all[p], NN)
            middle[here] = total
            xhat, rate = normalized(total)
            second[y, here] = (xhat * rows[2:3] + rows[3:4]).astype(low)

    def step(yy, slot):
        return remote(second.at[slot], second.at[slot], s_send.at[yy], s_recv.at[slot], (dp, z * wide + yy))

    def share():
        for yy in range(wide):
            when(yy != y, lambda: step(yy, y).start())

    def share_end():
        for yy in range(wide):
            @pl.when(yy != y)
            def _():
                step(yy, yy).wait_recv()
                step(yy, y).wait_send()

    return before, work, after, share, share_end


def pull_scores(heads, slope_of, dist, query, keys, values, grad):
    lanes = query.shape[1]
    scale = 1.0 / math.sqrt(lanes // heads)
    head = head_of_lane(query.shape, heads)
    head_rows = lax.broadcasted_iota(jnp.int32, (lanes, query.shape[0]), 0) // (lanes // heads)
    low = jnp.bfloat16
    grad_q = jnp.zeros((lanes, query.shape[0]), jnp.float32)
    grad_k = jnp.zeros(keys.shape, jnp.float32)
    grad_v = jnp.zeros(keys.shape, jnp.float32)
    for h in range(heads):
        masked = jnp.where(head == h, query * low(scale), low(0))
        masked_grad = jnp.where(head == h, grad, low(0))
        scores = dot(keys, masked, NT) - slope_of(h) * dist[...]
        peak = jnp.max(scores, axis=0, keepdims=True)
        expo = jnp.exp(scores - peak)
        probs = expo * (1.0 / jnp.sum(expo, axis=0, keepdims=True))
        grad_probs = dot(values, masked_grad, NT)
        inner = jnp.sum(probs * grad_probs, axis=0, keepdims=True)
        grad_scores = (probs * (grad_probs - inner)).astype(low)
        grad_v = grad_v + dot(probs.astype(low), masked_grad, NN)
        grad_k = grad_k + dot(grad_scores, masked, NN)
        grad_q = jnp.where(head_rows == h, dot(keys, grad_scores, TN), grad_q)
    return (jnp.transpose(grad_q) * scale).astype(low), grad_k.astype(low), grad_v.astype(low)


pull_inputs, pull_outputs = 10, 5


def pull_shapes(n_tensor, pull):
    slopes, dist, q, k, v, grad, context, out_all, qkv_all, normed_t = pull
    span, chunk, lanes, d = k.shape[1], q.shape[1], q.shape[2], normed_t.shape[0]
    halo = (span - chunk) // chunk
    low, f32 = jnp.bfloat16, jnp.float32
    shape = jax.ShapeDtypeStruct
    vm, dma = pltpu.VMEM, pltpu.SemaphoreType.DMA
    outs = [
        shape((n_tensor, d // 4, 3 * lanes), low), shape((n_tensor, lanes // 4, d), low), shape((chunk, d), f32),
        shape((n_tensor, 8, lanes), f32), shape((n_tensor, 8, lanes), f32),
    ]
    scratch = [vm(qkv_all.shape, low), vm(out_all.shape, low)]
    scratch += pair_scratch([qkv_all.shape[1:], out_all.shape[1:]], n_tensor) + [
        vm(q.shape, low), vm((n_tensor, span, 2 * lanes), low), vm((halo, chunk, d), low), vm((halo, chunk, d), low),
        dma((halo,)), dma((halo,)),
    ]
    return outs, scratch


def pull_program(n_tensor, heads, ins, outs, scratch):
    dp, t, z, y = where_am_i(n_tensor)
    slopes, dist, q, k, v, grad, context, out_all, qkv_all, normed_t = ins
    sum_qkv, sum_out, first, q_sum, v_sum = outs
    (grad_qkv, grad_out), pair = scratch[:2], scratch[2:12]
    grad_q, grad_kv, halo_own, halo_got, h_send, h_recv = scratch[12:]
    pair_start, core_stage, x_stage, pair_settle = pair_sums(
        n_tensor, (grad_qkv, grad_out), (sum_qkv, sum_out), pair[0:2], pair[2:4], pair[4:6], *pair[6:]
    )
    halo, chunk, d = halo_own.shape
    span, lanes = k.shape[1], q.shape[2]
    behind = span - chunk
    low, f32 = jnp.bfloat16, jnp.float32

    def work(p):
        grad_context = dot(grad[...], out_all[p], NT).astype(low)
        grad_out[p] = dot(context[p], grad[...], TN).astype(low)
        gq, gk, gv = pull_scores(heads, lambda h: slopes[p * heads + h], dist, q[p], k[p], v[p], grad_context)
        grad_q[p] = gq
        grad_kv[p, :, :lanes] = gk
        grad_kv[p, :, lanes:] = gv
        q_sum[p] = jnp.broadcast_to(jnp.sum(gq.astype(f32), axis=0, keepdims=True), (8, lanes))
        v_sum[p] = jnp.broadcast_to(jnp.sum(gv.astype(f32), axis=0, keepdims=True), (8, lanes))
        grad_qkv[p, :, :lanes] = dot(normed_t[:, behind:], gq, NN).astype(low)
        grad_qkv[p, :, lanes:] = dot(normed_t[...], grad_kv[p], NN).astype(low)
        pair_start(p)
        when(p >= 1, lambda: core_stage(jnp.maximum(p - 1, 0)))

    def step(m):
        return remote(halo_own.at[halo - 1 - m], halo_got.at[m], h_send.at[m], h_recv.at[m], (dp, t - 1 - m))

    ahead = [(t + 1 + m < n_tensor, (dp, t + 1 + m)) for m in range(halo)]
    back = [(t - 1 - m >= 0, (dp, t - 1 - m)) for m in range(halo)]
    tile = min(128, chunk)

    def rows_first():
        core_stage(n_tensor - 1)
        for j in range(halo):
            @pl.loop(0, chunk // tile)
            def _(i):
                here = pl.multiple_of(i * tile, tile)
                total = jnp.zeros((tile, d), f32)
                for p in range(n_tensor):
                    total = total + dot(grad_kv[p, pl.ds(j * chunk + here, tile)], qkv_all[p, :, lanes:], NT)
                halo_own[j, pl.ds(here, tile)] = total.astype(low)

        for m in range(halo):
            when(back[m][0], lambda: step(m).start())

        @pl.loop(0, chunk // tile)
        def _(i):
            here = pl.multiple_of(i * tile, tile)
            total = jnp.zeros((tile, d), f32)
            for p in range(n_tensor):
                total = total + dot(grad_kv[p, pl.ds(behind + here, tile)], qkv_all[p, :, lanes:], NT)
                total = total + dot(grad_q[p, pl.ds(here, tile)], qkv_all[p, :, :lanes], NT)
            first[pl.ds(here, tile)] = total

    def rows_last():
        for m in range(halo):
            @pl.when(ahead[m][0])
            def _():
                step(m).wait_recv()
                add_rows(first, [first, halo_got.at[m]])

            when(back[m][0], lambda: step(m).wait_send())

        @pl.loop(0, n_tensor)
        def _(p):
            x_stage(p)
            pair_settle(p)

    return work, ahead + back, rows_first, rows_last


norm_eps = 1e-05


def normalized(values):
    offset = values - jnp.mean(values, axis=-1, keepdims=True)
    rate = lax.rsqrt(jnp.mean(offset * offset, axis=-1, keepdims=True) + norm_eps)
    return offset * rate, rate


def norm_input_term(xhat, rate, gain, grad):
    e = grad * gain
    return rate * (e - jnp.mean(e, axis=-1, keepdims=True) - xhat * jnp.mean(e * xhat, axis=-1, keepdims=True))


def gelu_and_slope(u):
    c, a = 0.7978845608028654, 0.044715
    th = jnp.tanh(c * (u + a * u * u * u))
    slope = 0.5 * (1.0 + th) + 0.5 * u * (1.0 - th * th) * (c * (1.0 + 3.0 * a * u * u))
    return 0.5 * u * (1.0 + th), slope


far_off = 1e33
longest = 512


def rows_sum(v):
    return jnp.sum(v, axis=0)


def per_device(
    tokens, segment_ids, first_gain, first_shift, qkv_weight, qv_bias, out_weight, out_bias, second_gain, second_shift,
    up_weight, up_bias, down_weight, down_bias, cotangent,
):
    low, f32 = jnp.bfloat16, jnp.float32
    nt = lax.axis_size("tensor")
    lines, wide = grid_of(nt)
    t = lax.axis_index("tensor")
    z, y = t // wide, t % wide
    length, d = tokens.shape
    chunk = length // nt
    halo = -(-(longest - 1) // chunk)
    behind = halo * chunk
    span = behind + chunk
    heads_here, width = qkv_weight.shape[1], qkv_weight.shape[2] // 3
    lanes = heads_here * width
    hidden_here = up_weight.shape[1]

    qkv_own = qkv_weight.reshape(d, heads_here, 3, width).transpose(0, 2, 1, 3).reshape(d, 3 * lanes)
    bias_own = jnp.pad(qv_bias.reshape(heads_here, 2, width).transpose(1, 0, 2).reshape(2, lanes), ((0, 0), (0, 128 - lanes)))
    small = jnp.concatenate([bias_own.reshape(256), up_bias])
    small = jnp.pad(small, (0, 64 * 128 - small.shape[0])).reshape(64, 128)

    padded = jnp.concatenate([jnp.zeros((behind, d), low), tokens])
    near = lax.dynamic_slice_in_dim(padded, t * chunk, span, 0)
    seg_row = jnp.concatenate([jnp.full((behind,), -1, jnp.int32), segment_ids[0]])
    seg_near = lax.dynamic_slice_in_dim(seg_row, t * chunk, span, 0)
    seg_mine = seg_near[behind:]
    distance = (behind + jnp.arange(chunk)[:, None]) - jnp.arange(span)[None, :]
    allowed = (seg_mine[:, None] == seg_near[None, :]) & (distance >= 0)
    dist = jnp.where(allowed, distance.astype(f32), far_off)
    total_heads = heads_here * nt
    slopes = jnp.exp2(-8.0 * (jnp.arange(total_heads, dtype=jnp.int32) + 1).astype(f32) / total_heads)

    gain1, shift1 = first_gain.astype(f32), first_shift.astype(f32)
    gain2, shift2 = second_gain.astype(f32), second_shift.astype(f32)
    rows = jnp.stack([gain1, shift1, gain2, shift2, out_bias.astype(f32)] + [shift1] * 3)
    (qkv_all, out_all, small_all, up_all, down_all, query, keys, values, context, middle, second_pair, normed_t) = front(
        nt, [qkv_own, out_weight, small], [up_weight, down_weight], slopes, dist, near, rows
    )
    small_all = small_all.reshape(nt, 64 * 128).astype(f32)
    up_bias_all = lax.dynamic_index_in_dim(
        small_all[:, 256 : 256 + hidden_here].reshape(lines, wide, hidden_here), y, 1, keepdims=False
    )
    xhat1, rate1 = normalized(near[behind:].astype(f32))
    xhat2, rate2 = normalized(middle)
    second_pair = second_pair.reshape(wide * chunk, d)

    cot_pair = lax.dynamic_slice_in_dim(cotangent, z * (wide * chunk), wide * chunk, 0)
    sum_up, sum_down, grad_up_bias, grad_second, output_mine = mlp(
        nt, second_pair, cot_pair, up_all, down_all, jnp.broadcast_to(up_bias_all[:, None], (lines, 8, hidden_here)),
        middle + down_bias.astype(f32),
    )
    grad_up_bias = grad_up_bias[:, 0]
    cot_mine = lax.dynamic_slice_in_dim(cotangent, t * chunk, chunk, 0).astype(f32)
    grad_middle = cot_mine + norm_input_term(xhat2, rate2, gain2, grad_second)
    pull = [
        slopes, dist.T, query, keys, values, grad_middle.astype(low), context, out_all, qkv_all, normed_t,
    ]
    g_up, g_down, output_all, sum_qkv, sum_out, grad_first, q_sum, v_sum = finish(
        nt, [], [sum_up, sum_down], output_mine, None, 1, "finish_mlp", pull
    )
    grad_tokens = (grad_middle + norm_input_term(xhat1, rate1, gain1, grad_first)).astype(low)

    up_slots = jnp.where(jnp.arange(wide)[None, :, None] == y, grad_up_bias[:, None, :], 0.0)
    vectors = jnp.concatenate(
        [
            rows_sum(grad_first * xhat1), rows_sum(grad_first), rows_sum(grad_middle),
            rows_sum(grad_second * xhat2), rows_sum(grad_second), rows_sum(cot_mine),
            q_sum[:, 0].reshape(-1), v_sum[:, 0].reshape(-1), up_slots.reshape(-1),
        ]
    )
    g_qkv, g_out, grad_tokens_all, vectors = finish(
        nt, [sum_qkv, sum_out], [], grad_tokens, vectors.reshape(-1, 128), 5, "finish_attn"
    )
    vectors = vectors.reshape(-1)
    g_first_gain, g_first_shift, g_out_bias, g_second_gain, g_second_shift, g_down_bias = (
        vectors[i * d : (i + 1) * d] for i in range(6)
    )
    rest = vectors[6 * d :]
    g_q = lax.dynamic_index_in_dim(rest[:d].reshape(nt, heads_here, width), t, 0, keepdims=False)
    g_v = lax.dynamic_index_in_dim(rest[d : 2 * d].reshape(nt, heads_here, width), t, 0, keepdims=False)
    g_up_bias = lax.dynamic_index_in_dim(rest[2 * d :].reshape(nt, hidden_here), t, 0, keepdims=False)
    g_qkv = g_qkv.reshape(d, 3, heads_here, width).transpose(0, 2, 1, 3).reshape(d, heads_here, 3 * width)
    return (
        output_all.reshape(length, d), grad_tokens_all.reshape(length, d), g_first_gain, g_first_shift, g_qkv,
        jnp.concatenate([g_q, g_v], axis=1), g_out, g_out_bias, g_second_gain, g_second_shift,
        g_up, g_up_bias, g_down, g_down_bias,
    )


def solution(mesh):
    rows, cols, both = P("dp", None), P(None, "tensor"), P("tensor", None)
    return jax.shard_map(
        per_device,
        mesh=mesh,
        in_specs=(
            rows, rows, P(), P(), P(None, "tensor", None), both, both, P(), P(), P(), cols, P("tensor"), both, P(), rows,
        ),
        out_specs=(
            rows, rows, P(), P(), P(None, "tensor", None), both, both, P(), P(), P(), cols, P("tensor"), both, P(),
        ),
        check_vma=False,
    )
```

time: 475 us -> 419 us (0.88); the launches traced: 466 us -> 419 us
  matrix products: 44.1 us -> 0 us
  other arithmetic: 27.7 us -> 15.7 us
  local copies, waits for them, and re-layouts: 19.3 us -> 29.8 us
    dot_general x10 -> x0, matrix products: 44.1 us -> none  [the longest x1 8.44 us: per_device(): jnp.einsum('td,zfd->ztf', cot_pair, down_all, preferred_element_type=f32)]
    pallas_call x2, Pallas kernels: 222 us -> 191 us  [finish(): pl.pallas_call(functools.partial(finish_kernel, n_tensor, len(attn), len(...]
    pallas_call x4 -> x2, Pallas kernels: 151 us -> 181 us  [the longest x1 118 us: front(): pl.pallas_call(functools.partial(front_kernel, n_tensor, slopes.shape[0]...]
    convert_element_type x8 -> x1, other arithmetic: 10.9 us -> 1.21 us  [per_device(): (grad_middle + norm_input_term(xhat1, rate1, gain1, grad_first)).astype(low)]
    unnamed x77 -> x53, local copies, waits for them, and re-layouts: 7.97 us -> 13 us
    dynamic_slice x1 -> x3, local copies, waits for them, and re-layouts: 0.01 us -> 4.94 us  [the longest x1 2.66 us: per_device(): near = lax.dynamic_slice_in_dim(padded, t * chunk, span, 0)]
where the time goes in v5:
time: 419 us
  Pallas kernels  372 us (89%)
  local copies, waits for them, and re-layouts  29.8 us (7%)
  other arithmetic  15.7 us (4%)
    pallas_call x2, Pallas kernels, finish(): pl.pallas_call(functools.partial(finish_kernel, n_tensor, len(attn), len(...  191 us
    pallas_call x1, Pallas kernels, front(): pl.pallas_call(functools.partial(front_kernel, n_tensor, slopes.shape[0]...  118 us
    pallas_call x1, Pallas kernels, mlp(): pl.pallas_call(functools.partial(mlp_kernel, n_tensor), out_shape=[shape(...  62.4 us
    unnamed x53, local copies, waits for them, and re-layouts  13 us

profile of v5, /device:TPU:0, one launch (start us, length us, event | category | flops | bytes accessed | tf_op | source)
XLA Modules:
  0.0 418.7 jit_solution(8029680975389358419)
XLA Ops:
  0.6 0.0 copy-start.10
  0.7 0.0 copy-start.11
  0.7 0.0 copy-start.12
  0.7 0.0 copy-start.13
  0.7 0.0 copy-start.14
  0.7 0.0 copy-start.7
  0.7 0.9 pad_dynamic-slice_fusion.2
  1.6 1.1 convert_select_fusion.1.refs_6_
  2.7 2.7 pad_dynamic-slice_fusion.1.refs_7_
  5.4 0.0 copy-done.10
  5.4 0.0 copy-done.11
  5.4 0.0 copy-done.12
  5.4 0.0 copy-done.13
  5.4 0.0 copy-done.14
  5.5 0.7 stack.38.refs_8_
  6.1 0.5 multiply_exponential_fusion.refs_5_.refs_3_
  6.7 0.0 copy-done.7
  6.7 0.1 copy.36
  6.7 0.0 copy-start.15
  6.8 1.2 copy.38.refs_0_
  7.9 0.0 copy-done.17
  7.9 0.1 reshape.157
  8.0 0.1 reshape.158
  8.1 0.6 fusion.19.refs_2_
  8.7 118.2 %front.1 = (bf16[8,1024,384]{2,1,0:T(8,128)(2,1)}, bf16[8,128,1024]{2,1,0:T(8,128)(2,1)}, bf16[8,64,128]{2,1,0:T(8,128)(2,1)}, bf16[4,1024,512]{2,1,0:T(8,128)(2...) custom-call(bf16[1024,384]{1,0:T(8,128)(2,1)} %copy.38.refs_0_, ...), custom_call_target="tpu_custom_call" | custom-call | tf_op jit(solution)/shard_map/front/pallas_call | solution.py:277
  126.9 1.4 reduce_sum.126
  128.3 2.4 multiply_reduce_fusion.2
  130.7 1.0 copy.50
  131.7 0.6 broadcast_in_dim.27.refs_4_
  132.4 2.3 constant_dynamic-slice_fusion.4.refs_1_
  134.6 62.4 %mlp.1 = (bf16[4,256,512]{2,1,0:T(8,128)(2,1)}, bf16[4,128,1024]{2,1,0:T(8,128)(2,1)}, f32[4,8,512]{2,1,0:T(8,128)}, f32[256,1024]{1,0:T(8,128)}, bf16[256,1024]{1,0:T(8,128)(2,1)}) custom-call(bf16[512,1024]{1,0:T(8,128)(2,1)} %bitcast.60, bf16[512,1024]{1,0:T(8,128)(2,1)} %constant_dynamic-slice_fusion.4.refs_1_, ...), custom_call_target="tpu_custom_call" | custom-call | tf_op jit(solution)/shard_map/mlp/pallas_call | solution.py:689
  197.1 1.7 multiply_reduce_fusion
  198.8 1.9 fusion.22
  200.7 0.0 copy-start.1
  200.7 1.0 copy-done.1
  201.6 0.9 convert_element_type.49.refs_8_
  202.5 1.1 convert_select_fusion.refs_4_
  203.6 108.7 %finish_mlp.1 = (f32[1024,512]{1,0:T(8,128)}, f32[512,1024]{1,0:T(8,128)}, bf16[8,256,1024]{2,1,0:T(8,128)(2,1)}, bf16[8,256,384]{2,1,0:T(8,128)(2,1)}, bf16[8,3...) custom-call(bf16[4,256,512]{2,1,0:T(8,128)(2,1)} %get-tuple-element.48.refs_0_, ...), custom_call_target="tpu_custom_call" | custom-call | tf_op jit(solution)/shard_map/finish_mlp/pallas_call | solution.py:596
  312.3 0.0 copy-start.2
  312.3 1.4 convert_reduce_fusion
  313.7 0.3 fusion.11
  314.0 0.6 fusion.10
  314.6 0.8 slice.75
  315.4 0.8 slice.76
  316.2 0.8 slice.77
  317.0 0.1 select_bitcast_fusion
  317.1 0.0 copy-start.9
  317.2 1.2 fusion.9.refs_2_
  318.4 82.8 %finish_attn.1 = (f32[1024,384]{1,0:T(8,128)}, f32[128,1024]{1,0:T(8,128)}, bf16[8,256,1024]{2,1,0:T(8,128)(2,1)}, f32[96,128]{1,0:T(8,128)}) custom-call(bf16[8,256,384]{2,1,0:T(8,128)(2,1)} %get-tuple-element.60.refs_0_, bf16[8,32,1024]{2,1,0:T(8,128)(2,1)} %get-tuple-element.61.refs_1_, bf16[256,1024]{1,0:T(8,128)(2,1)} %fusion.9.refs_2_, f32[96,128]{1,0:T(8,128)} %bitcast.71), custom_call_target="tpu_custom_call" | custom-call | tf_op jit(solution)/shard_map/finish_attn/pallas_call | solution.py:596
  401.2 1.3 slice_bitcast_fusion
  402.5 0.1 reshape.168
  402.6 0.1 reshape.169
  402.7 0.6 pad_maximum_fusion
  403.3 1.9 copy.40
  405.2 1.2 copy.41
  406.4 0.7 slice.90
  407.2 0.6 constant_dynamic-slice_fusion
  407.7 4.8 %copy.67 = bf16[2048,1024]{1,0:T(8,128)(2,1)} copy(bf16[2048,1024]{1,0:T(8,128)(2,1)} %bitcast.56) | data formatting | bytes 8388608
  412.6 0.0 copy-done.4
  412.6 2.1 copy.68
  414.7 0.8 copy.69
  415.5 0.5 copy-done.6
  416.0 1.3 copy.70
  417.4 1.3 copy.71
  (51 shorter events, 0.2 us)
Async XLA Ops:
  0.6 4.7 %copy-start.10 = (bf16[1024]{0:T(1024)(128)(2,1)S(1)}, bf16[1024]{0:T(1024)(128)(2,1)}, u32[]{:S(2)}) copy-start(bf16[1024]{0:T(1024)(128)(2,1)} %param.17) | copy-start | bytes 6148
  0.7 4.7 %copy-start.11 = (bf16[1024]{0:T(1024)(128)(2,1)S(1)}, bf16[1024]{0:T(1024)(128)(2,1)}, u32[]{:S(2)}) copy-start(bf16[1024]{0:T(1024)(128)(2,1)} %param.23) | copy-start | bytes 6148
  0.7 4.7 %copy-start.12 = (bf16[1024]{0:T(1024)(128)(2,1)S(1)}, bf16[1024]{0:T(1024)(128)(2,1)}, u32[]{:S(2)}) copy-start(bf16[1024]{0:T(1024)(128)(2,1)} %param.22) | copy-start | bytes 6148
  0.7 4.7 %copy-start.13 = (bf16[1024]{0:T(1024)(128)(2,1)S(1)}, bf16[1024]{0:T(1024)(128)(2,1)}, u32[]{:S(2)}) copy-start(bf16[1024]{0:T(1024)(128)(2,1)} %param.18) | copy-start | bytes 6148
  0.7 4.8 %copy-start.14 = (bf16[1024]{0:T(1024)(128)(2,1)S(1)}, bf16[1024]{0:T(1024)(128)(2,1)}, u32[]{:S(2)}) copy-start(bf16[1024]{0:T(1024)(128)(2,1)} %param.24) | copy-start | bytes 6148
  0.7 6.0 %copy-start.7 = (bf16[1024,2,192]{0,2,1:T(8,128)(2,1)S(1)}, bf16[1024,2,192]{0,2,1:T(8,128)(2,1)}, u32[]{:S(2)}) copy-start(bf16[1024,2,192]{0,2,1:T(8,128)(2,1)} %param.19) | copy-start | bytes 2359300
  2.7 5.2 %copy-start.17 = (bf16[2,128]{1,0:T(2,128)(2,1)S(1)}, bf16[2,128]{1,0:T(2,128)(2,1)}, u32[]{:S(2)}) copy-start(bf16[2,128]{1,0:T(2,128)(2,1)} %param.20) | copy-start | bytes 1540
  2.7 5.4 %copy-start.16 = (bf16[512]{0:T(512)(128)(2,1)S(1)}, bf16[512]{0:T(512)(128)(2,1)}, u32[]{:S(2)}) copy-start(bf16[512]{0:T(512)(128)(2,1)} %param.26) | copy-start | bytes 3076
  6.7 121.5 %copy-start.15 = (bf16[1024]{0:T(1024)(128)(2,1)S(1)}, bf16[1024]{0:T(1024)(128)(2,1)}, u32[]{:S(2)}) copy-start(bf16[1024]{0:T(1024)(128)(2,1)} %param.28) | copy-start | bytes 6148
  134.6 62.4 %copy-start = (f32[256,1024]{1,0:T(8,128)S(1)}, f32[256,1024]{1,0:T(8,128)}, u32[]{:S(2)}) copy-start(f32[256,1024]{1,0:T(8,128)} %get-tuple-element.47) | copy-start | bytes 3145732
  200.7 1.0 copy-start.1
  312.3 1.7 copy-start.3
  312.3 4.9 %copy-start.2 = (f32[256,1024]{1,0:T(8,128)S(1)}, f32[256,1024]{1,0:T(8,128)}, u32[]{:S(2)}) copy-start(f32[256,1024]{1,0:T(8,128)} %copy-done.1) | copy-start | bytes 3145732
  317.1 1.3 copy-start.9
  407.7 4.8 %copy-start.4 = (bf16[8,256,1024]{2,1,0:T(8,128)(2,1)S(1)}, bf16[8,256,1024]{2,1,0:T(8,128)(2,1)}, u32[]{:S(2)}) copy-start(bf16[8,256,1024]{2,1,0:T(8,128)(2,1)} %get-tuple-element.66) | copy-start | bytes 12582916
  412.6 2.1 copy-start.8
  412.6 3.5 copy-start.6
  414.7 2.7 copy-start.5

commit v6 on v5

--- a/solution.py
+++ b/solution.py
@@ -28,6 +28,10 @@
     return pltpu.make_async_remote_copy(
         src_ref=src, dst_ref=dst, send_sem=send, recv_sem=recv, device_id=peer, device_id_type=MESH
     )
+
+
+def as_row(vector):
+    return vector[...].astype(jnp.float32).reshape(1, vector.shape[0])
 
 
 def when(condition, body):
@@ -229,20 +233,16 @@
     arrived(0)
     for c in local:
         c.wait()
-    steps = [functools.partial(z_step, 1, k) for k in range(3, lines)]
-    steps += [functools.partial(pass_on, 1, [zz]) for zz in range(lines)]
-
     @pl.loop(0, n_tensor)
     def _(p):
         work(p)
-        for k in range(n_tensor):
-            if steps:
-                when(p == k, steps.pop(0))
+        for k in range(3, lines):
+            when(p == k - 2, functools.partial(z_step, 1, k))
 
     after()
     share()
-    for step in steps:
-        step()
+    for zz in range(lines):
+        pass_on(1, [zz])
     share_end()
     arrived(1)
     settle(0)
@@ -260,12 +260,12 @@
                             y_copy(a, zz, yy, side).wait_send()
 
 
-def front(n_tensor, attn, mlp, slopes, dist, near, rows):
+def front(n_tensor, attn, mlp, slopes, segments, tokens, rows):
     lines, wide = grid_of(n_tensor)
     n = len(attn) + len(mlp)
     arrays = list(attn) + list(mlp)
-    span, d = near.shape
-    chunk = dist.shape[0]
+    d = tokens.shape[1]
+    chunk, span = tokens.shape[0] // n_tensor, segments.shape[1]
     lanes = attn[0].shape[1] // 3
     shape, low, f32 = jax.ShapeDtypeStruct, jnp.bfloat16, jnp.float32
     outs = [shape(((n_tensor if i < len(attn) else lines),) + a.shape, a.dtype) for i, a in enumerate(arrays)]
@@ -277,17 +277,17 @@
     return pl.pallas_call(
         functools.partial(front_kernel, n_tensor, slopes.shape[0] // n_tensor, len(attn), len(mlp)),
         out_shape=outs,
-        in_specs=[VM] * n + [pl.BlockSpec(memory_space=pltpu.SMEM)] + [VM] * (front_inputs - 1),
+        in_specs=[VM] * n + [pl.BlockSpec(memory_space=pltpu.SMEM), VM, ANY] + [VM] * len(rows),
         out_specs=[VM] * len(attn) + [ANY] * len(mlp) + [VM] * front_outputs,
         scratch_shapes=[dma((2, 2 * n, lines))] * 2
         + [dma((2, 2 * n, lines, wide))] * 2
         + [dma((2 * n, lines, wide))] * 2
         + [dma((2, 2 * n, lines, wide))] * 2
         + [dma((n,))]
-        + [pltpu.VMEM((span, d), low), dma((wide,)), dma((wide,))],
+        + [pltpu.VMEM((chunk, span), f32)] + [pltpu.VMEM((span, d), low)] * 2 + [dma((span // chunk,)), dma((wide,)), dma((wide,))],
         compiler_params=pltpu.CompilerParams(collective_id=0, has_side_effects=True, vmem_limit_bytes=60 * 2**20),
         name="front",
-    )(*arrays, slopes, dist, near, rows)
+    )(*arrays, slopes, segments, tokens, *rows)
 
 
 def add_rows(dst, terms):
@@ -411,11 +411,11 @@
     rows_steps = rows_program(n_tensor, rows_own, rows_full, *take(5))
     vec_steps = doubling_program(n_tensor, vec_own, vec_out, *take(4)) if with_vectors else []
     if pull:
-        work, pull_peers, pull_first, pull_last = pull_program(n_tensor, pull, pull_in, pull_out, refs)
+        pull_prepare, work, pull_peers, pull_first, pull_last = pull_program(n_tensor, pull, pull_in, pull_out, refs)
     quad = dp % 4
     core_peer, x_peer = (dp ^ 1, t), (dp ^ 2, t)
     lines_order = [i // 2 if i % 2 else lines - 1 - i // 2 for i in range(lines)]
-    attn, order = list(range(n_attn)), list(range(n))
+    attn, mlp, order = list(range(n_attn)), list(range(n_attn, n)), list(range(n))
 
     def index(a, zz, yy):
         return zz * wide + yy if a < n_attn else zz
@@ -455,7 +455,7 @@
                         add_rows(acc[a].at[lane], [acc[a].at[lane], from_y[a].at[side, lane]])
                         when(yy != y, lambda: y_copy(a, zz, yy, side).start())
 
-    def z_round(r):
+    def z_round(r, chosen):
         for side in range(2):
             zz = lines - 1 - r + z if side == 0 else z - (lines - 1 - r)
 
@@ -463,13 +463,13 @@
             def _():
                 @pl.when((z > 0) if side == 0 else (z < lines - 1))
                 def _():
-                    for a in order:
+                    for a in chosen:
                         s = index(a, zz, y)
                         z_copy(a, zz, side).wait_recv()
                         add_rows(acc[a].at[s], [acc[a].at[s], from_z[a].at[side, zz]])
 
                 if r < lines - 1:
-                    for a in order:
+                    for a in chosen:
                         z_copy(a, zz, side).start()
 
     def q_copy(a, q, hop, peer):
@@ -491,7 +491,12 @@
 
     def late(r):
         aside()
-        z_round(r)
+        if r == 1:
+            z_round(1, mlp)
+            z_round(0, attn)
+        else:
+            z_round(r, mlp)
+            z_round(r - 1, attn)
 
     peers = neighbours(n_tensor)
     if pull:
@@ -503,8 +508,7 @@
         y_begin(zz)
         for a in order[n_attn:]:
             add_rows(acc[a].at[zz], [terms[a].at[zz]])
-    if not attn:
-        z_round(0)
+    z_round(0, mlp)
     rows_steps.pop(0)()
     if with_vectors:
         vec_steps.pop(0)()
@@ -513,9 +517,10 @@
             y_stage(zz)
             if with_vectors:
                 vec_steps.pop(0)()
-        z_round(0)
     steps = [functools.partial(late, r) for r in range(1, lines)]
     if pull:
+        pull_prepare()
+
         @pl.loop(0, n_tensor)
         def _(p):
             work(p)
@@ -525,10 +530,13 @@
         pull_first()
     for step in steps:
         step()
-    for a in order:
+    for a in mlp:
+        home(a)
+    z_round(lines - 1, attn)
+    for a in attn:
         home(a)
     aside()
-    for a in order:
+    for a in mlp + attn:
         widen(a, quad)
         q_copy(a, quad ^ 2, 0, x_peer).wait_recv()
         q_copy(a, quad ^ 2, 2, core_peer).start()
@@ -588,7 +596,7 @@
     heads = 0
     if pull is not None:
         heads = pull[0].shape[0] // n_tensor
-        inputs, in_specs = inputs + list(pull), in_specs + [pl.BlockSpec(memory_space=pltpu.SMEM)] + [VM] * (pull_inputs - 1)
+        inputs, in_specs = inputs + list(pull), in_specs + [pl.BlockSpec(memory_space=pltpu.SMEM)] + [VM] * (pull_inputs - 3) + [ANY, VM]
         shapes, more = pull_shapes(n_tensor, pull)
         out_shape += shapes
         out_specs += [VM] * pull_outputs
@@ -613,10 +621,11 @@
 def mlp_kernel(n_tensor, *refs):
     lines, wide = grid_of(n_tensor)
     dp, t, z, y = where_am_i(n_tensor)
-    second, cot, up, down, bias, base = refs[:6]
-    sum_up, sum_down, up_sum, grad_second, output = refs[6:11]
-    terms_up, terms_down = refs[11:13]
-    pair, (feed, grad, second_t, share_own, share_got, s_send, s_recv) = refs[13:23], refs[23:]
+    second, cot_all, up, down, bias, middle, gain2, down_bias = refs[:8]
+    sum_up, sum_down, up_sum, grad_middle, grad_low, output, columns = refs[8:15]
+    terms_up, terms_down = refs[15:17]
+    pair, (feed, grad, second_t, share_own, share_got, grad_second, cot) = refs[17:27], refs[27:34]
+    s_send, s_recv, l_sem = refs[34:]
     sums, terms = (sum_up, sum_down), (terms_up, terms_down)
     pair_start, core_stage, x_stage, pair_settle = pair_sums(
         n_tensor, terms, sums, pair[0:2], pair[2:4], pair[4:6], *pair[6:]
@@ -633,6 +642,9 @@
 
     peers = [(dp >= 0, (dp ^ 1, t)), (dp >= 0, (dp ^ 2, t))]
     peers += [(yy != y, (dp, z * wide + yy)) for yy in range(wide)]
+    count = second.shape[0]
+    load = pltpu.make_async_copy(cot_all.at[pl.ds(pl.multiple_of(z * count, count), count)], cot, l_sem)
+    load.start()
     greet(peers)
     feed[...] = jnp.zeros(feed.shape, f32)
     grad[...] = jnp.zeros(grad.shape, f32)
@@ -641,6 +653,8 @@
     def _(i):
         here = pl.ds(pl.multiple_of(i * tile, tile), tile)
         second_t[:, here] = second[here].T
+
+    load.wait()
 
     @pl.loop(0, lines)
     def _(s):
@@ -663,14 +677,35 @@
                 add_rows(share_own.at[kind, yy], [whole.at[pl.ds(yy * chunk, chunk)]])
                 share(kind, yy, y).start()
     core_stage(lines - 1)
-    for s in range(lines - 1):
-        x_stage(s)
-    for kind, whole, out in ((0, grad, grad_second), (1, feed, output)):
+
+    def collect(kind, whole, out, more):
         share_got[kind, y] = jnp.zeros((chunk, second.shape[1]), low)
         for yy in range(wide):
             when(yy != y, lambda: share(kind, yy, yy).wait_recv())
         mine = whole.at[pl.ds(pl.multiple_of(y * chunk, chunk), chunk)]
-        add_rows(out, [mine] + [share_got.at[kind, yy] for yy in range(wide)] + ([base] if kind else []))
+        add_rows(out, [mine] + [share_got.at[kind, yy] for yy in range(wide)] + more)
+
+    for s in range(lines // 2):
+        x_stage(s)
+    collect(0, grad, grad_second, [])
+    columns[...] = jnp.zeros(columns.shape, f32)
+
+    @pl.loop(0, chunk // tile)
+    def _(i):
+        here = pl.ds(pl.multiple_of(i * tile, tile), tile)
+        mine = cot[pl.ds(pl.multiple_of(y * chunk + i * tile, tile), tile)].astype(f32)
+        xhat, rate = normalized(middle[here])
+        got = grad_second[here]
+        total = mine + norm_input_term(xhat, rate, as_row(gain2), got)
+        grad_middle[here] = total
+        grad_low[here] = total.astype(low)
+        for j, term in enumerate((got * xhat, got, total, mine)):
+            columns[j : j + 1] += jnp.sum(term, axis=0, keepdims=True)
+        feed[pl.ds(pl.multiple_of(y * chunk + i * tile, tile), tile)] += middle[here] + as_row(down_bias)
+
+    for s in range(lines // 2, lines - 1):
+        x_stage(s)
+    collect(1, feed, output, [])
     x_stage(lines - 1)
     for yy in range(wide):
         for kind in range(2):
@@ -679,25 +714,25 @@
         pair_settle(s)
 
 
-def mlp(n_tensor, second, cot, up, down, bias, base):
+def mlp(n_tensor, second, cot, up, down, bias, middle, gain2, down_bias):
     lines, wide = grid_of(n_tensor)
     shape, vm, dma = jax.ShapeDtypeStruct, pltpu.VMEM, pltpu.SemaphoreType.DMA
     low, f32 = jnp.bfloat16, jnp.float32
     d, hidden = up.shape[1:]
-    chunk = base.shape[0]
+    chunk = middle.shape[0]
     quarters = [(d // 4, hidden), (hidden // 4, d)]
     return pl.pallas_call(
         functools.partial(mlp_kernel, n_tensor),
         out_shape=[shape((lines,) + q, low) for q in quarters]
-        + [shape((lines, 8, hidden), f32), shape((chunk, d), f32), shape((chunk, d), low)],
-        in_specs=[VM] * 6,
-        out_specs=[VM] * 5,
+        + [shape((lines, 8, hidden), f32), shape((chunk, d), f32), shape((chunk, d), low), shape((chunk, d), low), shape((8, d), f32)],
+        in_specs=[VM, ANY] + [VM] * 6,
+        out_specs=[VM] * 7,
         scratch_shapes=[vm(up.shape, low), vm(down.shape, low)] + pair_scratch([up.shape[1:], down.shape[1:]], lines)
         + [vm(second.shape, f32)] * 2 + [vm((d, second.shape[0]), low)] + [vm((2, wide, chunk, d), low)] * 2
-        + [dma((2, wide))] * 2,
+        + [vm((chunk, d), f32), vm(second.shape, low)] + [dma((2, wide))] * 2 + [dma],
         compiler_params=pltpu.CompilerParams(collective_id=3, has_side_effects=True, vmem_limit_bytes=60 * 2**20),
         name="mlp",
-    )(second, cot, up, down, bias, base)
+    )(second, cot, up, down, bias, middle, gain2, down_bias)
 
 
 def rows_program(n_tensor, own, full, z_send, z_recv, y_send, y_recv, l_sem):
@@ -805,28 +840,57 @@
     return out.astype(jnp.bfloat16)
 
 
-front_inputs, front_outputs = 4, 7
+front_inputs, front_outputs = 8, 7
+
+
+def column_of(row):
+    return jnp.broadcast_to(row.astype(jnp.float32), (128, row.shape[1])).T[:, 0:1].astype(jnp.int32)
+
+
+def masked_distance(left, top, left_start, top_start):
+    shape = (left.shape[0], top.shape[1])
+    down = left_start + lax.broadcasted_iota(jnp.int32, shape, 0)
+    across = top_start + lax.broadcasted_iota(jnp.int32, shape, 1)
+    far = down - across if left_start else across - down
+    return jnp.where((left == top) & (far >= 0), far.astype(jnp.float32), far_off)
 
 
 def front_program(n_tensor, heads, ins, weights, outs, scratch):
     lines, wide = grid_of(n_tensor)
     dp, t, z, y = where_am_i(n_tensor)
-    slopes, dist, near, rows = ins
+    slopes, segments, tokens, *rows = ins
     qkv_all, out_all, small_all = weights
     q, k, v, context, middle, second, normed_t = outs
-    normed, s_send, s_recv = scratch
+    dist, near, normed, l_sem, s_send, s_recv = scratch
     chunk, lanes = q.shape[1:]
     span, d = near.shape
     behind = span - chunk
     low, f32 = jnp.bfloat16, jnp.float32
     tile = min(128, chunk)
 
+    def row(i):
+        return as_row(rows[i])
+
     def before():
+        loads = [
+            pltpu.make_async_copy(
+                tokens.at[pl.ds(pl.multiple_of(jnp.maximum(t - behind // chunk + j, 0) * chunk, chunk), chunk)],
+                near.at[pl.ds(j * chunk, chunk)], l_sem.at[j],
+            )
+            for j in range(span // chunk)
+        ]
+        for load in loads:
+            load.start()
+        own = column_of(segments[0:1, behind:])
+        dist[...] = masked_distance(own, segments[0:1, :], behind, 0)
+        for load in loads:
+            load.wait()
+
         @pl.loop(0, span // tile)
         def _(i):
             here = pl.ds(pl.multiple_of(i * tile, tile), tile)
             xhat, rate = normalized(near[here].astype(f32))
-            value = (xhat * rows[0:1] + rows[1:2]).astype(low)
+            value = (xhat * row(0) + row(1)).astype(low)
             normed[here] = value
             normed_t[:, here] = value.T
 
@@ -844,12 +908,12 @@
         def _(i):
             start = pl.multiple_of(i * tile, tile)
             here = pl.ds(start, tile)
-            total = near[pl.ds(behind + start, tile)].astype(f32) + rows[4:5]
+            total = near[pl.ds(behind + start, tile)].astype(f32) + row(4)
             for p in range(n_tensor):
                 total = total + dot(context[p, here], out_all[p], NN)
             middle[here] = total
             xhat, rate = normalized(total)
-            second[y, here] = (xhat * rows[2:3] + rows[3:4]).astype(low)
+            second[y, here] = (xhat * row(2) + row(3)).astype(low)
 
     def step(yy, slot):
         return remote(second.at[slot], second.at[slot], s_send.at[yy], s_recv.at[slot], (dp, z * wide + yy))
@@ -893,34 +957,34 @@
     return (jnp.transpose(grad_q) * scale).astype(low), grad_k.astype(low), grad_v.astype(low)
 
 
-pull_inputs, pull_outputs = 10, 5
+pull_inputs, pull_outputs = 13, 6
 
 
 def pull_shapes(n_tensor, pull):
-    slopes, dist, q, k, v, grad, context, out_all, qkv_all, normed_t = pull
+    slopes, segments, q, k, v, grad, context, out_all, qkv_all, normed_t, grad_middle, tokens, gain1 = pull
     span, chunk, lanes, d = k.shape[1], q.shape[1], q.shape[2], normed_t.shape[0]
     halo = (span - chunk) // chunk
     low, f32 = jnp.bfloat16, jnp.float32
     shape = jax.ShapeDtypeStruct
     vm, dma = pltpu.VMEM, pltpu.SemaphoreType.DMA
     outs = [
-        shape((n_tensor, d // 4, 3 * lanes), low), shape((n_tensor, lanes // 4, d), low), shape((chunk, d), f32),
+        shape((n_tensor, d // 4, 3 * lanes), low), shape((n_tensor, lanes // 4, d), low), shape((chunk, d), low), shape((8, d), f32),
         shape((n_tensor, 8, lanes), f32), shape((n_tensor, 8, lanes), f32),
     ]
     scratch = [vm(qkv_all.shape, low), vm(out_all.shape, low)]
     scratch += pair_scratch([qkv_all.shape[1:], out_all.shape[1:]], n_tensor) + [
         vm(q.shape, low), vm((n_tensor, span, 2 * lanes), low), vm((halo, chunk, d), low), vm((halo, chunk, d), low),
-        dma((halo,)), dma((halo,)),
+        dma((halo,)), dma((halo,)), vm((chunk, d), f32), vm((chunk, d), low), dma, vm((span, chunk), f32),
     ]
     return outs, scratch
 
 
 def pull_program(n_tensor, heads, ins, outs, scratch):
     dp, t, z, y = where_am_i(n_tensor)
-    slopes, dist, q, k, v, grad, context, out_all, qkv_all, normed_t = ins
-    sum_qkv, sum_out, first, q_sum, v_sum = outs
+    slopes, segments, q, k, v, grad, context, out_all, qkv_all, normed_t, grad_middle, tokens, gain1 = ins
+    sum_qkv, sum_out, grad_tokens, columns, q_sum, v_sum = outs
     (grad_qkv, grad_out), pair = scratch[:2], scratch[2:12]
-    grad_q, grad_kv, halo_own, halo_got, h_send, h_recv = scratch[12:]
+    grad_q, grad_kv, halo_own, halo_got, h_send, h_recv, first, mine, l_sem, dist = scratch[12:]
     pair_start, core_stage, x_stage, pair_settle = pair_sums(
         n_tensor, (grad_qkv, grad_out), (sum_qkv, sum_out), pair[0:2], pair[2:4], pair[4:6], *pair[6:]
     )
@@ -928,6 +992,9 @@
     span, lanes = k.shape[1], q.shape[2]
     behind = span - chunk
     low, f32 = jnp.bfloat16, jnp.float32
+
+    def prepare():
+        dist[...] = masked_distance(column_of(segments[0:1, :]), segments[0:1, behind:], 0, behind)
 
     def work(p):
         grad_context = dot(grad[...], out_all[p], NT).astype(low)
@@ -950,7 +1017,10 @@
     back = [(t - 1 - m >= 0, (dp, t - 1 - m)) for m in range(halo)]
     tile = min(128, chunk)
 
+    load = pltpu.make_async_copy(tokens.at[pl.ds(pl.multiple_of(t * chunk, chunk), chunk)], mine, l_sem)
+
     def rows_first():
+        load.start()
         core_stage(n_tensor - 1)
         for j in range(halo):
             @pl.loop(0, chunk // tile)
@@ -982,12 +1052,24 @@
 
             when(back[m][0], lambda: step(m).wait_send())
 
+        load.wait()
+        columns[...] = jnp.zeros(columns.shape, f32)
+
+        @pl.loop(0, chunk // tile)
+        def _(i):
+            here = pl.ds(pl.multiple_of(i * tile, tile), tile)
+            xhat, rate = normalized(mine[here].astype(f32))
+            got = first[here]
+            grad_tokens[here] = (grad_middle[here] + norm_input_term(xhat, rate, as_row(gain1), got)).astype(low)
+            for j, term in enumerate((got * xhat, got)):
+                columns[j : j + 1] += jnp.sum(term, axis=0, keepdims=True)
+
         @pl.loop(0, n_tensor)
         def _(p):
             x_stage(p)
             pair_settle(p)
 
-    return work, ahead + back, rows_first, rows_last
+    return prepare, work, ahead + back, rows_first, rows_last
 
 
 norm_eps = 1e-05
@@ -1013,10 +1095,6 @@
 
 far_off = 1e33
 longest = 512
-
-
-def rows_sum(v):
-    return jnp.sum(v, axis=0)
 
 
 def per_device(
@@ -1042,57 +1120,43 @@
     small = jnp.concatenate([bias_own.reshape(256), up_bias])
     small = jnp.pad(small, (0, 64 * 128 - small.shape[0])).reshape(64, 128)
 
-    padded = jnp.concatenate([jnp.zeros((behind, d), low), tokens])
-    near = lax.dynamic_slice_in_dim(padded, t * chunk, span, 0)
     seg_row = jnp.concatenate([jnp.full((behind,), -1, jnp.int32), segment_ids[0]])
     seg_near = lax.dynamic_slice_in_dim(seg_row, t * chunk, span, 0)
-    seg_mine = seg_near[behind:]
-    distance = (behind + jnp.arange(chunk)[:, None]) - jnp.arange(span)[None, :]
-    allowed = (seg_mine[:, None] == seg_near[None, :]) & (distance >= 0)
-    dist = jnp.where(allowed, distance.astype(f32), far_off)
+    segments = jnp.broadcast_to(seg_near[None], (8, span))
     total_heads = heads_here * nt
     slopes = jnp.exp2(-8.0 * (jnp.arange(total_heads, dtype=jnp.int32) + 1).astype(f32) / total_heads)
 
-    gain1, shift1 = first_gain.astype(f32), first_shift.astype(f32)
-    gain2, shift2 = second_gain.astype(f32), second_shift.astype(f32)
-    rows = jnp.stack([gain1, shift1, gain2, shift2, out_bias.astype(f32)] + [shift1] * 3)
     (qkv_all, out_all, small_all, up_all, down_all, query, keys, values, context, middle, second_pair, normed_t) = front(
-        nt, [qkv_own, out_weight, small], [up_weight, down_weight], slopes, dist, near, rows
+        nt, [qkv_own, out_weight, small], [up_weight, down_weight], slopes, segments, tokens,
+        [first_gain, first_shift, second_gain, second_shift, out_bias],
     )
     small_all = small_all.reshape(nt, 64 * 128).astype(f32)
     up_bias_all = lax.dynamic_index_in_dim(
         small_all[:, 256 : 256 + hidden_here].reshape(lines, wide, hidden_here), y, 1, keepdims=False
     )
-    xhat1, rate1 = normalized(near[behind:].astype(f32))
-    xhat2, rate2 = normalized(middle)
     second_pair = second_pair.reshape(wide * chunk, d)
 
-    cot_pair = lax.dynamic_slice_in_dim(cotangent, z * (wide * chunk), wide * chunk, 0)
-    sum_up, sum_down, grad_up_bias, grad_second, output_mine = mlp(
-        nt, second_pair, cot_pair, up_all, down_all, jnp.broadcast_to(up_bias_all[:, None], (lines, 8, hidden_here)),
-        middle + down_bias.astype(f32),
+    sum_up, sum_down, grad_up_bias, grad_middle, grad_middle_low, output_mine, columns2 = mlp(
+        nt, second_pair, cotangent, up_all, down_all, jnp.broadcast_to(up_bias_all[:, None], (lines, 8, hidden_here)),
+        middle, second_gain, down_bias,
     )
     grad_up_bias = grad_up_bias[:, 0]
-    cot_mine = lax.dynamic_slice_in_dim(cotangent, t * chunk, chunk, 0).astype(f32)
-    grad_middle = cot_mine + norm_input_term(xhat2, rate2, gain2, grad_second)
     pull = [
-        slopes, dist.T, query, keys, values, grad_middle.astype(low), context, out_all, qkv_all, normed_t,
+        slopes, segments, query, keys, values, grad_middle_low, context, out_all, qkv_all, normed_t, grad_middle, tokens,
+        first_gain,
     ]
-    g_up, g_down, output_all, sum_qkv, sum_out, grad_first, q_sum, v_sum = finish(
-        nt, [], [sum_up, sum_down], output_mine, None, 1, "finish_mlp", pull
-    )
-    grad_tokens = (grad_middle + norm_input_term(xhat1, rate1, gain1, grad_first)).astype(low)
-
+    g_down, output_all, sum_qkv, sum_out, grad_tokens, columns1, q_sum, v_sum = finish(
+        nt, [], [sum_down], output_mine, None, 1, "finish_mlp", pull
+    )
     up_slots = jnp.where(jnp.arange(wide)[None, :, None] == y, grad_up_bias[:, None, :], 0.0)
     vectors = jnp.concatenate(
         [
-            rows_sum(grad_first * xhat1), rows_sum(grad_first), rows_sum(grad_middle),
-            rows_sum(grad_second * xhat2), rows_sum(grad_second), rows_sum(cot_mine),
+            columns1[0], columns1[1], columns2[2], columns2[0], columns2[1], columns2[3],
             q_sum[:, 0].reshape(-1), v_sum[:, 0].reshape(-1), up_slots.reshape(-1),
         ]
     )
-    g_qkv, g_out, grad_tokens_all, vectors = finish(
-        nt, [sum_qkv, sum_out], [], grad_tokens, vectors.reshape(-1, 128), 5, "finish_attn"
+    g_qkv, g_out, g_up, grad_tokens_all, vectors = finish(
+        nt, [sum_qkv, sum_out], [sum_up], grad_tokens, vectors.reshape(-1, 128), 5, "finish_attn"
     )
     vectors = vectors.reshape(-1)
     g_first_gain, g_first_shift, g_out_bias, g_second_gain, g_second_shift, g_down_bias = (

time: 419 us -> 380 us (0.907)
  Pallas kernels: 372 us -> 346 us
  other arithmetic: 15.7 us -> 2.54 us
    pallas_call x2, Pallas kernels: 191 us -> 171 us  [finish(): pl.pallas_call(functools.partial(finish_kernel, n_tensor, len(attn), len(...]
    reduce_sum x7 -> x0, other arithmetic: 9.56 us -> none  [the longest x3 4.14 us: rows_sum(): return jnp.sum(v, axis=0)]
    pallas_call x1, Pallas kernels: 118 us -> 112 us  [front(): pl.pallas_call(functools.partial(front_kernel, n_tensor, slopes.shape[0]...]
    dynamic_slice x2 -> x0, local copies, waits for them, and re-layouts: 4.93 us -> none  [the longest x1 2.66 us: per_device(): near = lax.dynamic_slice_in_dim(padded, t * chunk, span, 0)]
    unnamed x53 -> x29, local copies, waits for them, and re-layouts: 13 us -> 13.6 us
where the time goes in v6:
time: 380 us; the launch traced here: 377 us
  Pallas kernels  346 us (91%)
  local copies, waits for them, and re-layouts  28 us (7%)
    pallas_call x2, Pallas kernels, finish(): pl.pallas_call(functools.partial(finish_kernel, n_tensor, len(attn), len(...  171 us
    pallas_call x1, Pallas kernels, front(): pl.pallas_call(functools.partial(front_kernel, n_tensor, slopes.shape[0]...  112 us
    pallas_call x1, Pallas kernels, mlp(): pl.pallas_call(functools.partial(mlp_kernel, n_tensor), out_shape=[shape(...  63.2 us
    unnamed x29, local copies, waits for them, and re-layouts  13.6 us

profile of v6, /device:TPU:0, one launch (start us, length us, event | category | flops | bytes accessed | tf_op | source)
XLA Modules:
  0.0 377.4 jit_solution(4205245566312852977)
XLA Ops:
  0.7 0.5 multiply_exponential_fusion.refs_5_.refs_2_
  1.2 0.7 reshape.108
  1.9 0.1 reshape.109
  2.0 0.8 pad_dynamic-slice_fusion
  2.8 1.3 fusion.3.refs_2_
  4.1 0.6 broadcast_in_dim.38.refs_6_.refs_3_
  4.7 1.2 copy.36
  5.9 1.2 copy.38.refs_0_
  7.0 112.0 %front.1 = (bf16[8,1024,384]{2,1,0:T(8,128)(2,1)}, bf16[8,128,1024]{2,1,0:T(8,128)(2,1)}, bf16[8,64,128]{2,1,0:T(8,128)(2,1)}, bf16[4,1024,512]{2,1,0:T(8,128)(2...) custom-call(bf16[1024,384]{1,0:T(8,128)(2,1)} %copy.38.refs_0_, ...), custom_call_target="tpu_custom_call" | custom-call | tf_op jit(solution)/shard_map/front/pallas_call | solution.py:277
  119.0 1.0 copy.50
  120.1 0.6 broadcast_in_dim.40.refs_4_
  120.7 63.2 %mlp.1 = (bf16[4,256,512]{2,1,0:T(8,128)(2,1)}, bf16[4,128,1024]{2,1,0:T(8,128)(2,1)}, f32[4,8,512]{2,1,0:T(8,128)}, f32[256,1024]{1,0:T(8,128)}, bf16[256,1024]...) custom-call(bf16[512,1024]{1,0:T(8,128)(2,1)} %bitcast.61, bf16[2048,1024]{1,0:T(8,128)(2,1)} %refs_1_.3, ...), custom_call_target="tpu_custom_call" | custom-call | tf_op jit(solution)/shard_map/mlp/pallas_call | solution.py:724
  183.9 0.0 copy-start.5
  183.9 83.6 %finish_mlp.1 = (f32[512,1024]{1,0:T(8,128)}, bf16[8,256,1024]{2,1,0:T(8,128)(2,1)}, bf16[8,256,384]{2,1,0:T(8,128)(2,1)}, bf16[8,32,1024]{2,1,0:T(8,128)(2,1)},...) custom-call(bf16[4,128,1024]{2,1,0:T(8,128)(2,1)} %get-tuple-element.51.refs_0_, ...), custom_call_target="tpu_custom_call" | custom-call | tf_op jit(solution)/shard_map/finish_mlp/pallas_call | solution.py:604
  267.5 0.8 slice.91
  268.3 0.8 slice.92
  269.0 0.8 slice.93
  269.9 0.1 select_bitcast_fusion
  270.0 0.8 fusion.5
  270.8 0.0 copy-done.5
  270.9 0.0 copy-start.4
  270.9 0.6 copy-done.4
  271.6 87.3 %finish_attn.1 = (f32[1024,384]{1,0:T(8,128)}, f32[128,1024]{1,0:T(8,128)}, f32[1024,512]{1,0:T(8,128)}, bf16[8,256,1024]{2,1,0:T(8,128)(2,1)}, f32[96,128]{1,0:T(8,128)}) custom-call(bf16[8,256,384]{2,1,0:T(8,128)(2,1)} %get-tuple-element.63.refs_0_, bf16[8,32,1024]{2,1,0:T(8,128)(2,1)} %get-tuple-element.64.refs_1_, ...), custom_call_target="tpu_custom_call" | custom-call | tf_op jit(solution)/shard_map/finish_attn/pallas_call | solution.py:604
  358.9 0.7 slice.106
  359.6 1.3 slice_bitcast_fusion
  360.9 0.6 constant_dynamic-slice_fusion
  361.5 0.1 reshape.120
  361.6 0.1 reshape.119
  361.7 0.6 pad_maximum_fusion
  362.3 1.9 copy.40
  364.2 1.2 copy.41
  365.5 0.0 copy-start
  365.5 4.8 %copy.67 = bf16[2048,1024]{1,0:T(8,128)(2,1)} copy(bf16[2048,1024]{1,0:T(8,128)(2,1)} %bitcast.57) | data formatting | bytes 8388608
  370.3 0.0 copy-done
  370.3 0.0 copy-start.3
  370.3 0.0 copy-start.2
  370.3 2.1 copy.68
  372.4 0.0 copy-done.3
  372.4 0.8 copy.69
  373.2 0.5 copy-done.2
  373.7 0.0 copy-start.1
  373.7 1.3 copy.70
  375.1 1.0 copy-done.1
  376.1 1.3 copy.71
  (20 shorter events, 0.1 us)
Async XLA Ops:
  183.9 86.9 %copy-start.5 = (f32[8,1024]{1,0:T(8,128)S(1)}, f32[8,1024]{1,0:T(8,128)}, u32[]{:S(2)}) copy-start(f32[8,1024]{1,0:T(8,128)} %get-tuple-element.68) | copy-start | bytes 98308
  270.9 0.6 copy-start.4
  365.5 4.8 %copy-start = (bf16[8,256,1024]{2,1,0:T(8,128)(2,1)S(1)}, bf16[8,256,1024]{2,1,0:T(8,128)(2,1)}, u32[]{:S(2)}) copy-start(bf16[8,256,1024]{2,1,0:T(8,128)(2,1)} %get-tuple-element.72) | copy-start | bytes 12582916
  370.3 2.1 copy-start.3
  370.3 3.5 copy-start.2
  373.7 2.3 copy-start.1

commit v7 on v6

--- a/solution.py
+++ b/solution.py
@@ -303,7 +303,7 @@
         dst[part] = total.astype(dst.dtype)
 
 
-def pair_sums(n_tensor, terms, sums, from_c, to_x, from_x, c_send, c_recv, x_send, x_recv):
+def pair_sums(n_tensor, terms, sums, from_c, to_x, from_x, c_send, c_recv, x_send, x_recv, held=()):
     dp, t, z, y = where_am_i(n_tensor)
     quad = dp % 4
     side_x, core = quad // 2, quad % 2
@@ -331,11 +331,12 @@
             for h in range(2):
                 c_copy(a, s, h).wait_recv()
             add_rows(to_x[a].at[s], [quarter(a, s, (1 - side_x) * 2 + core), from_c[a].at[s, 1 - side_x]])
-            x_copy(a, s).start()
+            if a not in held:
+                x_copy(a, s).start()
             add_rows(sums[a].at[s], [quarter(a, s, quad), from_c[a].at[s, side_x]])
 
     def x_stage(s):
-        for a in arrays:
+        for a in [a for a in arrays if a not in held]:
             x_copy(a, s).wait_recv()
             add_rows(sums[a].at[s], [sums[a].at[s], from_x[a].at[s]])
 
@@ -343,7 +344,8 @@
         for a in arrays:
             for h in range(2):
                 c_copy(a, s, h).wait_send()
-            x_copy(a, s).wait_send()
+            if a not in held:
+                x_copy(a, s).wait_send()
 
     return start, core_stage, x_stage, settle
 
@@ -622,13 +624,13 @@
     lines, wide = grid_of(n_tensor)
     dp, t, z, y = where_am_i(n_tensor)
     second, cot_all, up, down, bias, middle, gain2, down_bias = refs[:8]
-    sum_up, sum_down, up_sum, grad_middle, grad_low, output, columns = refs[8:15]
-    terms_up, terms_down = refs[15:17]
-    pair, (feed, grad, second_t, share_own, share_got, grad_second, cot) = refs[17:27], refs[27:34]
-    s_send, s_recv, l_sem = refs[34:]
+    sum_up, sum_down, up_sum, grad_middle, grad_low, output, columns, give_up = refs[8:16]
+    terms_up, terms_down = refs[16:18]
+    pair, (feed, grad, second_t, share_own, share_got, grad_second, cot) = refs[18:28], refs[28:35]
+    s_send, s_recv, l_sem = refs[35:]
     sums, terms = (sum_up, sum_down), (terms_up, terms_down)
     pair_start, core_stage, x_stage, pair_settle = pair_sums(
-        n_tensor, terms, sums, pair[0:2], pair[2:4], pair[4:6], *pair[6:]
+        n_tensor, terms, sums, pair[0:2], (give_up, pair[3]), pair[4:6], *pair[6:], held=(0,)
     )
     low, f32 = jnp.bfloat16, jnp.float32
     chunk = output.shape[0]
@@ -724,9 +726,10 @@
     return pl.pallas_call(
         functools.partial(mlp_kernel, n_tensor),
         out_shape=[shape((lines,) + q, low) for q in quarters]
-        + [shape((lines, 8, hidden), f32), shape((chunk, d), f32), shape((chunk, d), low), shape((chunk, d), low), shape((8, d), f32)],
+        + [shape((lines, 8, hidden), f32), shape((chunk, d), f32), shape((chunk, d), low), shape((chunk, d), low), shape((8, d), f32),
+           shape((lines,) + quarters[0], low)],
         in_specs=[VM, ANY] + [VM] * 6,
-        out_specs=[VM] * 7,
+        out_specs=[VM] * 8,
         scratch_shapes=[vm(up.shape, low), vm(down.shape, low)] + pair_scratch([up.shape[1:], down.shape[1:]], lines)
         + [vm(second.shape, f32)] * 2 + [vm((d, second.shape[0]), low)] + [vm((2, wide, chunk, d), low)] * 2
         + [vm((chunk, d), f32), vm(second.shape, low)] + [dma((2, wide))] * 2 + [dma],
@@ -957,11 +960,11 @@
     return (jnp.transpose(grad_q) * scale).astype(low), grad_k.astype(low), grad_v.astype(low)
 
 
-pull_inputs, pull_outputs = 13, 6
+pull_inputs, pull_outputs = 15, 7
 
 
 def pull_shapes(n_tensor, pull):
-    slopes, segments, q, k, v, grad, context, out_all, qkv_all, normed_t, grad_middle, tokens, gain1 = pull
+    slopes, segments, q, k, v, grad, context, out_all, qkv_all, normed_t, grad_middle, keep_up, give_up, tokens, gain1 = pull
     span, chunk, lanes, d = k.shape[1], q.shape[1], q.shape[2], normed_t.shape[0]
     halo = (span - chunk) // chunk
     low, f32 = jnp.bfloat16, jnp.float32
@@ -969,22 +972,23 @@
     vm, dma = pltpu.VMEM, pltpu.SemaphoreType.DMA
     outs = [
         shape((n_tensor, d // 4, 3 * lanes), low), shape((n_tensor, lanes // 4, d), low), shape((chunk, d), low), shape((8, d), f32),
-        shape((n_tensor, 8, lanes), f32), shape((n_tensor, 8, lanes), f32),
+        shape((n_tensor, 8, lanes), f32), shape((n_tensor, 8, lanes), f32), shape(keep_up.shape, low),
     ]
     scratch = [vm(qkv_all.shape, low), vm(out_all.shape, low)]
     scratch += pair_scratch([qkv_all.shape[1:], out_all.shape[1:]], n_tensor) + [
         vm(q.shape, low), vm((n_tensor, span, 2 * lanes), low), vm((halo, chunk, d), low), vm((halo, chunk, d), low),
         dma((halo,)), dma((halo,)), vm((chunk, d), f32), vm((chunk, d), low), dma, vm((span, chunk), f32),
+        vm(keep_up.shape, low), dma((keep_up.shape[0],)), dma((keep_up.shape[0],)),
     ]
     return outs, scratch
 
 
 def pull_program(n_tensor, heads, ins, outs, scratch):
     dp, t, z, y = where_am_i(n_tensor)
-    slopes, segments, q, k, v, grad, context, out_all, qkv_all, normed_t, grad_middle, tokens, gain1 = ins
-    sum_qkv, sum_out, grad_tokens, columns, q_sum, v_sum = outs
+    slopes, segments, q, k, v, grad, context, out_all, qkv_all, normed_t, grad_middle, keep_up, give_up, tokens, gain1 = ins
+    sum_qkv, sum_out, grad_tokens, columns, q_sum, v_sum, sum_up = outs
     (grad_qkv, grad_out), pair = scratch[:2], scratch[2:12]
-    grad_q, grad_kv, halo_own, halo_got, h_send, h_recv, first, mine, l_sem, dist = scratch[12:]
+    grad_q, grad_kv, halo_own, halo_got, h_send, h_recv, first, mine, l_sem, dist, got_up, u_send, u_recv = scratch[12:]
     pair_start, core_stage, x_stage, pair_settle = pair_sums(
         n_tensor, (grad_qkv, grad_out), (sum_qkv, sum_out), pair[0:2], pair[2:4], pair[4:6], *pair[6:]
     )
@@ -993,7 +997,12 @@
     behind = span - chunk
     low, f32 = jnp.bfloat16, jnp.float32
 
+    def up_copy(s):
+        return remote(give_up.at[s], got_up.at[s], u_send.at[s], u_recv.at[s], (dp ^ 2, t))
+
     def prepare():
+        for s in range(give_up.shape[0]):
+            up_copy(s).start()
         dist[...] = masked_distance(column_of(segments[0:1, :]), segments[0:1, behind:], 0, behind)
 
     def work(p):
@@ -1063,6 +1072,11 @@
             grad_tokens[here] = (grad_middle[here] + norm_input_term(xhat, rate, as_row(gain1), got)).astype(low)
             for j, term in enumerate((got * xhat, got)):
                 columns[j : j + 1] += jnp.sum(term, axis=0, keepdims=True)
+
+        for s in range(give_up.shape[0]):
+            up_copy(s).wait_recv()
+            add_rows(sum_up.at[s], [keep_up.at[s], got_up.at[s]])
+            up_copy(s).wait_send()
 
         @pl.loop(0, n_tensor)
         def _(p):
@@ -1136,16 +1150,16 @@
     )
     second_pair = second_pair.reshape(wide * chunk, d)
 
-    sum_up, sum_down, grad_up_bias, grad_middle, grad_middle_low, output_mine, columns2 = mlp(
+    keep_up, sum_down, grad_up_bias, grad_middle, grad_middle_low, output_mine, columns2, give_up = mlp(
         nt, second_pair, cotangent, up_all, down_all, jnp.broadcast_to(up_bias_all[:, None], (lines, 8, hidden_here)),
         middle, second_gain, down_bias,
     )
     grad_up_bias = grad_up_bias[:, 0]
     pull = [
-        slopes, segments, query, keys, values, grad_middle_low, context, out_all, qkv_all, normed_t, grad_middle, tokens,
-        first_gain,
+        slopes, segments, query, keys, values, grad_middle_low, context, out_all, qkv_all, normed_t, grad_middle, keep_up,
+        give_up, tokens, first_gain,
     ]
-    g_down, output_all, sum_qkv, sum_out, grad_tokens, columns1, q_sum, v_sum = finish(
+    g_down, output_all, sum_qkv, sum_out, grad_tokens, columns1, q_sum, v_sum, sum_up = finish(
         nt, [], [sum_down], output_mine, None, 1, "finish_mlp", pull
     )
     up_slots = jnp.where(jnp.arange(wide)[None, :, None] == y, grad_up_bias[:, None, :], 0.0)

time: 380 us -> 372 us (0.979)
  Pallas kernels: 346 us -> 340 us
    pallas_call x1, Pallas kernels: 63.2 us -> 49.6 us  [mlp(): pl.pallas_call(functools.partial(mlp_kernel, n_tensor), out_shape=[shape(...]
    pallas_call x2, Pallas kernels: 171 us -> 179 us  [finish(): pl.pallas_call(functools.partial(finish_kernel, n_tensor, len(attn), len(...]
where the time goes in v7:
time: 372 us
  Pallas kernels  340 us (91%)
  local copies, waits for them, and re-layouts  28 us (8%)
    pallas_call x2, Pallas kernels, finish(): pl.pallas_call(functools.partial(finish_kernel, n_tensor, len(attn), len(...  179 us
    pallas_call x1, Pallas kernels, front(): pl.pallas_call(functools.partial(front_kernel, n_tensor, slopes.shape[0]...  112 us
    pallas_call x1, Pallas kernels, mlp(): pl.pallas_call(functools.partial(mlp_kernel, n_tensor), out_shape=[shape(...  49.6 us
    unnamed x29, local copies, waits for them, and re-layouts  13.6 us

profile of v7, /device:TPU:0, one launch (start us, length us, event | category | flops | bytes accessed | tf_op | source)
XLA Modules:
  0.0 371.5 jit_solution(6471304390217513464)
XLA Ops:
  0.7 0.5 multiply_exponential_fusion.refs_5_.refs_2_
  1.2 0.7 reshape.108
  1.9 0.1 reshape.109
  2.0 0.8 pad_dynamic-slice_fusion
  2.8 1.3 fusion.3.refs_2_
  4.1 0.6 broadcast_in_dim.38.refs_6_.refs_3_
  4.7 1.2 copy.36
  5.9 1.2 copy.38.refs_0_
  7.0 111.9 %front.1 = (bf16[8,1024,384]{2,1,0:T(8,128)(2,1)}, bf16[8,128,1024]{2,1,0:T(8,128)(2,1)}, bf16[8,64,128]{2,1,0:T(8,128)(2,1)}, bf16[4,1024,512]{2,1,0:T(8,128)(2...) custom-call(bf16[1024,384]{1,0:T(8,128)(2,1)} %copy.38.refs_0_, ...), custom_call_target="tpu_custom_call" | custom-call | tf_op jit(solution)/shard_map/front/pallas_call | solution.py:277
  118.9 1.0 copy.50
  120.0 0.6 broadcast_in_dim.40.refs_4_
  120.6 49.6 %mlp.1 = (bf16[4,256,512]{2,1,0:T(8,128)(2,1)}, bf16[4,128,1024]{2,1,0:T(8,128)(2,1)}, f32[4,8,512]{2,1,0:T(8,128)}, f32[256,1024]{1,0:T(8,128)}, bf16[256,1024]...) custom-call(bf16[512,1024]{1,0:T(8,128)(2,1)} %bitcast.61, ...), custom_call_target="tpu_custom_call" | custom-call | tf_op jit(solution)/shard_map/mlp/pallas_call | solution.py:726
  170.2 0.0 copy-start.5
  170.2 89.9 %finish_mlp.1 = (f32[512,1024]{1,0:T(8,128)}, bf16[8,256,1024]{2,1,0:T(8,128)(2,1)}, bf16[8,256,384]{2,1,0:T(8,128)(2,1)}, bf16[8,32,1024]{2,1,0:T(8,128)(2,1)},...) custom-call(bf16[4,128,1024]{2,1,0:T(8,128)(2,1)} %get-tuple-element, ...), custom_call_target="tpu_custom_call" | custom-call | tf_op jit(solution)/shard_map/finish_mlp/pallas_call | solution.py:606
  260.2 0.8 slice.91
  260.9 0.8 slice.92
  261.7 0.8 slice.93
  262.6 0.1 select_bitcast_fusion
  262.6 0.8 fusion.5
  263.5 0.0 copy-done.5
  263.6 0.0 copy-start.4
  263.6 0.6 copy-done.4
  264.2 88.8 %finish_attn.1 = (f32[1024,384]{1,0:T(8,128)}, f32[128,1024]{1,0:T(8,128)}, f32[1024,512]{1,0:T(8,128)}, bf16[8,256,1024]{2,1,0:T(8,128)(2,1)}, f32[96,128]{1,0:T(8,128)}) custom-call(bf16[8,256,384]{2,1,0:T(8,128)(2,1)} %get-tuple-element.67.refs_0_, bf16[8,32,1024]{2,1,0:T(8,128)(2,1)} %get-tuple-element.68.refs_1_, ...), custom_call_target="tpu_custom_call" | custom-call | tf_op jit(solution)/shard_map/finish_attn/pallas_call | solution.py:606
  353.0 0.7 slice.106
  353.7 1.3 slice_bitcast_fusion
  355.0 0.6 constant_dynamic-slice_fusion
  355.6 0.1 reshape.120
  355.7 0.1 reshape.119
  355.8 0.6 pad_maximum_fusion
  356.4 1.9 copy.40
  358.3 1.2 copy.41
  359.6 0.0 copy-start
  359.6 4.8 %copy.67 = bf16[2048,1024]{1,0:T(8,128)(2,1)} copy(bf16[2048,1024]{1,0:T(8,128)(2,1)} %bitcast.57) | data formatting | bytes 8388608
  364.4 0.0 copy-done
  364.4 0.0 copy-start.3
  364.4 0.0 copy-start.2
  364.4 2.1 copy.68
  366.5 0.0 copy-done.3
  366.5 0.8 copy.69
  367.3 0.5 copy-done.2
  367.9 0.0 copy-start.1
  367.9 1.3 copy.70
  369.2 1.0 copy-done.1
  370.2 1.3 copy.71
  (20 shorter events, 0.1 us)
Async XLA Ops:
  170.2 93.3 %copy-start.5 = (f32[8,1024]{1,0:T(8,128)S(1)}, f32[8,1024]{1,0:T(8,128)}, u32[]{:S(2)}) copy-start(f32[8,1024]{1,0:T(8,128)} %get-tuple-element.72) | copy-start | bytes 98308
  263.6 0.6 copy-start.4
  359.6 4.8 %copy-start = (bf16[8,256,1024]{2,1,0:T(8,128)(2,1)S(1)}, bf16[8,256,1024]{2,1,0:T(8,128)(2,1)}, u32[]{:S(2)}) copy-start(bf16[8,256,1024]{2,1,0:T(8,128)(2,1)} %get-tuple-element.76) | copy-start | bytes 12582916
  364.4 2.1 copy-start.3
  364.4 3.5 copy-start.2
  367.9 2.3 copy-start.1
